TPU v7x, 32 devices: a whole 2x2x4 slice. The times are simulated.
32 devices in a mesh: groups: 2 (over y), blocks: 16 (over z, x, core).
Axes of the slice: x: 2, y: 2, z: 4, core: 2. Of those that a mesh axis runs over, the one named last changes fastest.
Arguments:
- snapshot: bfloat16 [2, 128, 32, 512], P('groups', 'blocks'), parts along dimension 0, may hold values from -6 to 6
- cotangent: bfloat16 [2, 128, 32, 512], P('groups', 'blocks'), parts along dimension 0, may hold values from -6 to 6
- first_weight: bfloat16 [32, 864], replicated, may hold values from -0.21875 to 0.21875
- second_weight: bfloat16 [32, 864], replicated, may hold values from -0.21875 to 0.21875
- face_codes: int32 [32, 2], P(('groups', 'blocks')), parts along dimension 0, may hold values from 0 to 3, as said below
Outputs:
- input_grad: float32 [2, 128, 32, 512], P('groups', 'blocks'), parts along dimension 0
- first_update: float32 [64, 864], P('groups'), parts along dimension 0
- second_update: float32 [64, 864], P('groups'), parts along dimension 0
There are 2 independent parts, one for each index of `groups`. A program takes and returns all parts, laid end to end along the dimension named above; an argument that names none is the same for every part. Nothing has to cross between parts.
Inputs may be any that keep to these rules, and one draw needn't show every extreme that they name: face_codes[b, 1] equals face_codes[(b + 1) mod 16, 0]: both blocks of an interface carry the same code.
All inputs are finite; a program needn't handle non-finite values.
Results may differ from a plain program's by a relative error of at most 0.003.
Values may be sent and summed in bfloat16 or wider, within the bound.
No kernel may reach another device: no remote copies, remote signals or barrier semaphores. Data moves between devices by JAX's collectives and lax.ppermute only.
A program may use at most 64 MiB of HBM per device.

v0:
```python
import jax
import jax.numpy as jnp
from jax import lax
from jax.sharding import PartitionSpec as P

R_CELLS = 32


def shifted_2(value, axis, steps):
    count = lax.axis_size(axis)
    pairs = [(source, (source + steps) % count) for source in range(count)]
    return lax.ppermute(value, axis, pairs)


def flip_plane(plane, code, radial, vertical):
    batch_count = plane.shape[0]
    channels = plane.shape[1]
    grid = plane.reshape(batch_count, channels, radial, vertical)
    grid = jnp.where(code % 2 == 1, grid[:, :, ::-1, :], grid)
    grid = jnp.where(code // 2 == 1, grid[:, :, :, ::-1], grid)
    return grid.reshape(batch_count, channels, radial * vertical)


def shifted(field, step_r, step_z, vertical):
    cells = field.shape[-1]
    margin = vertical + 1
    widths = [(0, 0)] * (field.ndim - 1) + [(margin, margin)]
    wide = jnp.pad(field, widths)
    offset = margin + (step_r - 1) * vertical + (step_z - 1)
    piece = lax.slice_in_dim(wide, offset, offset + cells, axis=field.ndim - 1)
    place = lax.broadcasted_iota(jnp.int32, (cells,), 0) % vertical + step_z - 1
    valid = (place >= 0) & (place < vertical)
    return jnp.where(valid, piece, jnp.zeros((), field.dtype))


def neighbor_planes(field):
    count = field.shape[1]
    from_lower = shifted_2(field[:, count - 1], "blocks", 1)
    from_upper = shifted_2(field[:, 0], "blocks", -1)
    return (from_lower, from_upper)


def padded_field(field, codes, radial, vertical):
    from_lower, from_upper = neighbor_planes(field)
    lower = flip_plane(from_lower, codes[0], radial, vertical)
    upper = flip_plane(from_upper, codes[1], radial, vertical)
    return jnp.concatenate([lower[:, None], field, upper[:, None]], axis=1)


def zero_padded(field):
    return jnp.pad(field, ((0, 0), (1, 1), (0, 0), (0, 0)))


def convolve(padded, weight, count, vertical):
    channels = padded.shape[2]
    total = None
    for step_r in range(3):
        for step_z in range(3):
            moved = shifted(padded, step_r, step_z, vertical)
            for step_a in range(3):
                tap_index = 9 * step_a + 3 * step_r + step_z
                kernel = weight[:, tap_index * channels : (tap_index + 1) * channels]
                term = jnp.einsum(
                    "oc,bacp->baop",
                    kernel,
                    moved[:, step_a : step_a + count],
                    preferred_element_type=jnp.float32,
                )
                total = term if total is None else total + term
    return total


def weight_gradient(padded, cotan, vertical):
    count = cotan.shape[1]
    found = {}
    for step_r in range(3):
        for step_z in range(3):
            moved = shifted(padded, step_r, step_z, vertical)
            for step_a in range(3):
                tap_index = 9 * step_a + 3 * step_r + step_z
                found[tap_index] = jnp.einsum(
                    "baop,bacp->oc",
                    cotan,
                    moved[:, step_a : step_a + count],
                    preferred_element_type=jnp.float32,
                )
    return jnp.concatenate([found[index] for index in range(27)], axis=1)


def plane_adjoint(plane, weight, step_a, vertical):
    channels = weight.shape[1] // 27
    total = None
    for step_r in range(3):
        for step_z in range(3):
            tap_index = 9 * step_a + 3 * step_r + step_z
            kernel = weight[:, tap_index * channels : (tap_index + 1) * channels]
            piece = shifted(plane, 2 - step_r, 2 - step_z, vertical)
            term = jnp.einsum("oc,bop->bcp", kernel, piece, preferred_element_type=jnp.float32)
            total = term if total is None else total + term
    return total


def adjoint(cotan, weight, codes, radial, vertical):
    count = cotan.shape[1]
    out_channels = weight.shape[0]
    channels = weight.shape[1] // 27
    reversed_weight = weight.reshape(out_channels, 27, channels)[:, ::-1, :]
    reversed_weight = reversed_weight.transpose(2, 1, 0).reshape(channels, 27 * out_channels)
    interior = convolve(zero_padded(cotan), reversed_weight, count, vertical)
    own_lower = flip_plane(
        plane_adjoint(cotan[:, 0], weight, 0, vertical), codes[0], radial, vertical
    )
    own_upper = flip_plane(
        plane_adjoint(cotan[:, count - 1], weight, 2, vertical), codes[1], radial, vertical
    )
    lower_add = shifted_2(own_upper, "blocks", 1)
    upper_add = shifted_2(own_lower, "blocks", -1)
    interior = interior.at[:, 0].add(lower_add)
    return interior.at[:, count - 1].add(upper_add)


def normalize(grad):
    return grad / jnp.sqrt(jnp.mean(grad * grad) + 1e-06)


def body(snapshot, cotangent, first_weight, second_weight, face_codes):
    count = snapshot.shape[1]
    radial = R_CELLS
    vertical = snapshot.shape[3] // radial
    codes = face_codes[0]
    field_padded = padded_field(snapshot, codes, radial, vertical)
    pre = convolve(field_padded, first_weight, count, vertical)
    hidden = jax.nn.silu(pre).astype(jnp.bfloat16)
    hidden_padded = padded_field(hidden, codes, radial, vertical)
    second_grad = weight_gradient(hidden_padded, cotangent, vertical)
    hidden_grad = adjoint(cotangent, second_weight, codes, radial, vertical)
    sigmoid_part = jax.nn.sigmoid(pre)
    pre_grad = (hidden_grad * sigmoid_part * (1.0 + pre * (1.0 - sigmoid_part))).astype(
        jnp.bfloat16
    )
    first_grad = weight_gradient(field_padded, pre_grad, vertical)
    first_total, second_total = lax.psum((first_grad, second_grad), "blocks")
    input_grad = cotangent.astype(jnp.float32) + adjoint(
        pre_grad, first_weight, codes, radial, vertical
    )
    return (input_grad, normalize(first_total), normalize(second_total))


def solution(mesh):
    return jax.shard_map(
        body,
        mesh=mesh,
        in_specs=(
            P("groups", "blocks", None, None),
            P("groups", "blocks", None, None),
            P(),
            P(),
            P(("groups", "blocks"), None),
        ),
        out_specs=(P("groups", "blocks", None, None), P("groups", None), P("groups", None)),
        check_vma=False,
    )
```

profile of v0, /device:TPU:1, one launch (start us, length us, event | category | flops | bytes accessed | tf_op | source)
XLA Modules:
  0.0 206.2 jit_solution(6006155757848173578)
XLA Ops:
  7.2 0.8 fusion.446
  8.4 2.6 %collective-permute-start.2 = (bf16[1,32,512]{1,2,0:T(8,128)(2,1)S(1)}, bf16[1,32,512]{1,2,0:T(8,128)(2,1)S(1)}, u32[]{:S(2)}, u32[]{:S(2)}) collective-permute-start(bf16[1,32,512]{1,2,0:T(8,128)(2,1)S(1)} %bitcast.1332), channel_id=1, source_target_pairs={{0,1},{1,2},{2,3},{3,4},{4,5},{5,6},{6,7},{7,8},{8,9},{9,10},{10,1... | collective-permute-start | bytes 98312 | tf_op jit(solution)/shard_map/ppermute | solution.py:12
  17.6 3.5 %collective-permute-start.1 = (f32[1,32,512]{2,1,0:T(8,128)S(1)}, f32[1,32,512]{2,1,0:T(8,128)S(1)}, u32[]{:S(2)}, u32[]{:S(2)}) collective-permute-start(f32[1,32,512]{2,1,0:T(8,128)S(1)} %copy.14), channel_id=1, source_target_pairs={{0,15},{1,0},{2,1},{3,2},{4,3},{5,4},{6,5},{7,6},{8,7},{9,8},{10,9... | collective-permute-start | bytes 196616 | tf_op jit(solution)/shard_map/ppermute | solution.py:12
  30.8 1.9 fusion.54
  53.0 4.1 %collective-permute-start.7 = (bf16[1,32,512]{2,1,0:T(8,128)(2,1)S(1)}, bf16[1,32,512]{2,1,0:T(8,128)(2,1)S(1)}, u32[]{:S(2)}, u32[]{:S(2)}) collective-permute-start(bf16[1,32,512]{2,1,0:T(8,128)(2,1)S(1)} %get-tuple-element.112), channel_id=1, source_target_pairs={{0,15},{1,0},{2,1},{3,2},{4,3},{5,4},{6,5},{7,6},{8,7},{9,8},{10,9... | collective-permute-start | bytes 98312 | tf_op jit(solution)/shard_map/ppermute | solution.py:12
  62.7 4.4 %collective-permute-start.5 = (f32[1,32,512]{2,1,0:T(8,128)}, f32[1,32,512]{2,1,0:T(8,128)}, u32[]{:S(2)}, u32[]{:S(2)}) collective-permute-start(f32[1,32,512]{2,1,0:T(8,128)} %copy.23), channel_id=1, source_target_pairs={{0,15},{1,0},{2,1},{3,2},{4,3},{5,4},{6,5},{7,6},{8,7},{9,8},{10,9... | collective-permute-start | bytes 196616 | tf_op jit(solution)/shard_map/ppermute | solution.py:12
  69.8 0.8 convolution_bitcast_fusion.46
  71.4 1.8 fusion.62
  75.6 0.8 convolution_bitcast_fusion.40
  76.5 0.8 convolution_bitcast_fusion.49
  79.7 0.8 convolution_bitcast_fusion.53
  88.6 0.8 convolution_bitcast_fusion.48
  94.1 1.1 convolution_bitcast_fusion.3
  95.2 1.0 convolution_bitcast_fusion.4
  96.2 1.1 convolution_bitcast_fusion.5
  101.1 1.1 convolution_bitcast_fusion.9
  102.2 1.1 fusion
  103.3 1.8 concatenate.39
  105.1 2.1 %fusion.38 = f32[1,8,32,512]{3,2,1,0:T(8,128)S(1)} fusion(f32[1,8,32,512]{3,2,1,0:T(8,128)S(1)} %convolution_bitcast_fusion, f32[1,8,32,512]{3,2,1,0:T(8,128)S(1)} %convolution_bitcast_fusion.1, f32[1,8,32,512]{3,2,1,0:T(8,128)S(1)} %convolution_bitcast_fusion.2, f32[1,8,32,512]{3,2,1,0:T(8,128)} %convolution_bitcast_fusion.3, ...), kind=kOutput, calls=%fused_computation.116 | convolution fusion | flops 9830400 | bytes 6561792 | tf_op jit(solution)/shard_map/oc,bacp->baop/dot_general | solution.py:63
  107.2 0.9 fusion.133
  108.1 0.9 fusion.132
  109.0 0.9 convert_add_fusion
  109.9 84.3 %all-reduce.13.cloned.1.call-done = (f32[32,864]{1,0:T(8,128)}, f32[32,864]{1,0:T(8,128)}) async-done(((f32[32,864]{1,0:T(8,128)}, f32[32,864]{1,0:T(8,128)}), (f32[32,864]{1,0:T(8,128)}, f32[32,864]{1,0:T(8,128)})) %all-reduce.13.cloned.1.call-update) | async-done | bytes 221200 | tf_op jit(solution)/shard_map/psum | solution.py:142
  194.2 1.6 multiply_reduce_fusion
  (252 shorter events, 63.6 us)
Async XLA Ops:
  7.2 7.1 %copy-start.1 = (bf16[1,8,32,512]{3,2,1,0:T(8,128)(2,1)S(1)}, bf16[1,8,32,512]{3,2,1,0:T(8,128)(2,1)}, u32[]{:S(2)}) copy-start(bf16[1,8,32,512]{3,2,1,0:T(8,128)(2,1)} %param.14) | copy-start | bytes 786436
  7.2 187.0 %all-reduce.13.cloned.1.call-start = ((), (), s32[]{:S(2)}) async-start(), calls=%async_computation | async-start | bytes 458752 | tf_op jit(solution)/shard_map/psum | solution.py:142
  8.2 21.3 %collective-permute-start.3 = (bf16[1,32,512]{1,2,0:T(8,128)(2,1)S(1)}, bf16[1,32,512]{1,2,0:T(8,128)(2,1)S(1)}, u32[]{:S(2)}, u32[]{:S(2)}) collective-permute-start(bf16[1,32,512]{1,2,0:T(8,128)(2,1)S(1)} %bitcast.1333), channel_id=1, source_target_pairs={{0,15},{1,0},{2,1},{3,2},{4,3},{5,4},{6,5},{7,6},{8,7},{9,8},{10,9... | collective-permute-start | bytes 98312 | tf_op jit(solution)/shard_map/ppermute | solution.py:12
  8.4 2.6 %copy-start.7 = (s32[1,2]{1,0:T(1,128)S(1)}, s32[1,2]{1,0:T(1,128)}, u32[]{:S(2)}) copy-start(s32[1,2]{1,0:T(1,128)} %param.17) | copy-start | bytes 28
  8.4 21.3 %collective-permute-start.2 = (bf16[1,32,512]{1,2,0:T(8,128)(2,1)S(1)}, bf16[1,32,512]{1,2,0:T(8,128)(2,1)S(1)}, u32[]{:S(2)}, u32[]{:S(2)}) collective-permute-start(bf16[1,32,512]{1,2,0:T(8,128)(2,1)S(1)} %bitcast.1332), channel_id=1, source_target_pairs={{0,1},{1,2},{2,3},{3,4},{4,5},{5,6},{6,7},{7,8},{8,9},{9,10},{10,1... | collective-permute-start | bytes 98312 | tf_op jit(solution)/shard_map/ppermute | solution.py:12
  14.3 0.8 copy-start.3
  17.6 29.0 %collective-permute-start.1 = (f32[1,32,512]{2,1,0:T(8,128)S(1)}, f32[1,32,512]{2,1,0:T(8,128)S(1)}, u32[]{:S(2)}, u32[]{:S(2)}) collective-permute-start(f32[1,32,512]{2,1,0:T(8,128)S(1)} %copy.14), channel_id=1, source_target_pairs={{0,15},{1,0},{2,1},{3,2},{4,3},{5,4},{6,5},{7,6},{8,7},{9,8},{10,9... | collective-permute-start | bytes 196616 | tf_op jit(solution)/shard_map/ppermute | solution.py:12
  26.3 20.3 %collective-permute-start = (f32[1,32,512]{2,1,0:T(8,128)S(1)}, f32[1,32,512]{2,1,0:T(8,128)S(1)}, u32[]{:S(2)}, u32[]{:S(2)}) collective-permute-start(f32[1,32,512]{2,1,0:T(8,128)S(1)} %copy.12), channel_id=1, source_target_pairs={{0,1},{1,2},{2,3},{3,4},{4,5},{5,6},{6,7},{7,8},{8,9},{9,10},{10,1... | collective-permute-start | bytes 196616 | tf_op jit(solution)/shard_map/ppermute | solution.py:12
  27.4 0.8 copy-start
  29.8 1.0 copy-start.6
  53.0 15.8 %collective-permute-start.6 = (bf16[1,32,512]{2,1,0:T(8,128)(2,1)S(1)}, bf16[1,32,512]{2,1,0:T(8,128)(2,1)S(1)}, u32[]{:S(2)}, u32[]{:S(2)}) collective-permute-start(bf16[1,32,512]{2,1,0:T(8,128)(2,1)S(1)} %get-tuple-element.111), channel_id=1, source_target_pairs={{0,1},{1,2},{2,3},{3,4},{4,5},{5,6},{6,7},{7,8},{8,9},{9,10},{10,1... | collective-permute-start | bytes 98312 | tf_op jit(solution)/shard_map/ppermute | solution.py:12
  53.0 16.1 %collective-permute-start.7 = (bf16[1,32,512]{2,1,0:T(8,128)(2,1)S(1)}, bf16[1,32,512]{2,1,0:T(8,128)(2,1)S(1)}, u32[]{:S(2)}, u32[]{:S(2)}) collective-permute-start(bf16[1,32,512]{2,1,0:T(8,128)(2,1)S(1)} %get-tuple-element.112), channel_id=1, source_target_pairs={{0,15},{1,0},{2,1},{3,2},{4,3},{5,4},{6,5},{7,6},{8,7},{9,8},{10,9... | collective-permute-start | bytes 98312 | tf_op jit(solution)/shard_map/ppermute | solution.py:12
  62.7 45.4 %collective-permute-start.5 = (f32[1,32,512]{2,1,0:T(8,128)}, f32[1,32,512]{2,1,0:T(8,128)}, u32[]{:S(2)}, u32[]{:S(2)}) collective-permute-start(f32[1,32,512]{2,1,0:T(8,128)} %copy.23), channel_id=1, source_target_pairs={{0,15},{1,0},{2,1},{3,2},{4,3},{5,4},{6,5},{7,6},{8,7},{9,8},{10,9... | collective-permute-start | bytes 196616 | tf_op jit(solution)/shard_map/ppermute | solution.py:12
  68.0 39.3 %collective-permute-start.4 = (f32[1,32,512]{2,1,0:T(8,128)}, f32[1,32,512]{2,1,0:T(8,128)}, u32[]{:S(2)}, u32[]{:S(2)}) collective-permute-start(f32[1,32,512]{2,1,0:T(8,128)} %copy.21), channel_id=1, source_target_pairs={{0,1},{1,2},{2,3},{3,4},{4,5},{5,6},{6,7},{7,8},{8,9},{9,10},{10,1... | collective-permute-start | bytes 196616 | tf_op jit(solution)/shard_map/ppermute | solution.py:12
  107.2 1.8 copy-start.2
  194.2 2.3 %copy-start.5 = (f32[32,864]{1,0:T(8,128)S(1)}, f32[32,864]{1,0:T(8,128)}, u32[]{:S(2)}) copy-start(f32[32,864]{1,0:T(8,128)} %get-tuple-element.51) | copy-start | bytes 331780
  197.8 0.9 copy-start.4
Sparse Core Ops, SparseCore 0:
  105.2 88.9 all-reduce.12
where the time goes:
time: 208 us; the launch traced here: 206 us
  waiting for transfers between devices  84.4 us (41%)
  matrix products  62.4 us (30%)
  between operations  21.7 us (10%)
  starting transfers between devices  14.9 us (7%)
  local copies, waits for them, and re-layouts  12.2 us (6%)
  other arithmetic  10.7 us (5%)
    psum x1, waiting for transfers between devices, body(): first_total, second_total = lax.psum((first_grad, second_grad), 'blocks')  84.3 us
    dot_general x54, matrix products, weight_gradient(): jnp.einsum('baop,bacp->oc', cotan, moved[:, step_a:step_a + count], prefe...  26.8 us
    dot_general x81, matrix products, convolve(): jnp.einsum('oc,bacp->baop', kernel, moved[:, step_a:step_a + count], pref...  26.8 us
    ppermute x8, starting transfers between devices, shifted_2(): return lax.ppermute(value, axis, pairs)  14.8 us
    dot_general x36, matrix products, plane_adjoint(): jnp.einsum('oc,bop->bcp', kernel, piece, preferred_element_type=jnp.float32)  8.82 us
  transfers between devices with their start and end apart: 9, of which 1 were waited for; matrix products, arithmetic and copies ran while one was open for 35% of the time, Pallas kernels for 0%

commit v1 on v0

v1 whole, which is shorter than its diff:
```python
import jax
import jax.numpy as jnp
from jax import lax
from jax.experimental import pallas as pl
from jax.experimental.pallas import tpu as pltpu
from jax.sharding import PartitionSpec as P

R_CELLS = 32
AXIS = "blocks"
F32 = jnp.float32
BF16 = jnp.bfloat16
VMEM_LIMIT = 40 * 1024 * 1024


def tap_masks(cells, vertical):
    lane = lax.broadcasted_iota(jnp.int32, (1, cells), 1)
    z = lane % vertical
    r = lane // vertical
    radial = cells // vertical
    masks = []
    for step_r in range(3):
        for step_z in range(3):
            ok = None
            if step_r == 0:
                ok = r >= 1
            if step_r == 2:
                ok = r < radial - 1
            if step_z == 0:
                ok = (z >= 1) if ok is None else ok & (z >= 1)
            if step_z == 2:
                ok = (z < vertical - 1) if ok is None else ok & (z < vertical - 1)
            masks.append(ok)
    return masks


def im2col(plane, store, masks, vertical):
    cells = plane.shape[1]
    wide = plane.astype(F32)
    for tap in range(9):
        offset = (tap // 3 - 1) * vertical + (tap % 3 - 1)
        if offset == 0:
            store(tap, plane)
            continue
        moved = pltpu.roll(wide, (-offset) % cells, 1)
        moved = jnp.where(masks[tap], moved, 0.0)
        store(tap, moved.astype(BF16))


def flipped_tap(tap, code):
    a, r, z = tap // 9, (tap // 3) % 3, tap % 3
    if code % 2 == 1:
        r = 2 - r
    if code // 2 == 1:
        z = 2 - z
    return 9 * a + 3 * r + z


(FW1_LO, FW1_HI, A2, A2_0, A2_7, A2_M, A2_P, A1, A1_0, A1_7) = range(10)


def prepare_kernel(codes_ref, w1_ref, w2_ref, out_ref):
    channels = w1_ref.shape[0]
    k_lo = codes_ref[0, 0]
    k_hi = codes_ref[0, 1]

    def block(tap):
        return slice(tap * channels, (tap + 1) * channels)

    for weight_ref, row in ((w1_ref, A1), (w2_ref, A2)):
        turned = weight_ref[...].astype(F32).T
        for tap in range(27):
            out_ref[row, :, block(tap)] = turned[block(26 - tap), :].astype(BF16)

    out_ref[A2_0, :, :] = out_ref[A2]
    out_ref[A2_7, :, :] = out_ref[A2]
    out_ref[A2_M, :, :] = out_ref[A2]
    out_ref[A2_P, :, :] = out_ref[A2]
    out_ref[A1_0, :, :] = out_ref[A1]
    out_ref[A1_7, :, :] = out_ref[A1]

    for code in range(4):

        @pl.when(k_lo == code)
        def _(code=code):
            for tap in range(27):
                source = flipped_tap(tap, code)
                out_ref[FW1_LO, :, block(tap)] = w1_ref[:, block(source)]
                if tap < 18:
                    out_ref[A2_M, :, block(tap)] = out_ref[A2, :, block(source)]
                if tap < 9:
                    out_ref[A2_0, :, block(tap)] = out_ref[A2, :, block(source)]
                    out_ref[A1_0, :, block(tap)] = out_ref[A1, :, block(source)]

        @pl.when(k_hi == code)
        def _(code=code):
            for tap in range(27):
                source = flipped_tap(tap, code)
                out_ref[FW1_HI, :, block(tap)] = w1_ref[:, block(source)]
                if tap >= 9:
                    out_ref[A2_P, :, block(tap)] = out_ref[A2, :, block(source)]
                if tap >= 18:
                    out_ref[A2_7, :, block(tap)] = out_ref[A2, :, block(source)]
                    out_ref[A1_7, :, block(tap)] = out_ref[A1, :, block(source)]


def dot(a, b):
    return jnp.dot(a, b, preferred_element_type=F32)


def dot_nt(a, b):
    return lax.dot_general(a, b, (((1,), (1,)), ((), ())), preferred_element_type=F32)


def flip_matrix(code, cells, vertical):
    row = lax.broadcasted_iota(jnp.int32, (cells, cells), 0)
    col = lax.broadcasted_iota(jnp.int32, (cells, cells), 1)
    bits = jnp.where(code % 2 == 1, cells - vertical, 0) + jnp.where(code // 2 == 1, vertical - 1, 0)
    return jnp.where(row == (col ^ bits), 1.0, 0.0).astype(BF16)


def make_main_kernel(count, channels, cells, vertical):
    span = 9 * channels

    def kernel(codes_ref, x_ref, g_ref, pair_ref, cross_ref, w1_ref, wp_ref,
               keep_ref, send_ref, pg_ref, xs_ref, cs_ref, h_ref, pr_ref):
        odd = lax.axis_index(AXIS) % 2
        masks = tap_masks(cells, vertical)

        def fill(ref, position, plane):
            def store(tap, value):
                start = position * span + tap * channels
                ref[start:start + channels, :] = value

            im2col(plane, store, masks, vertical)

        is_odd = odd == 1
        for side in range(2):
            lower = side == 0
            a_val = pair_ref[...].reshape(4 * channels, cells)
            b_val = cross_ref[...].reshape(4 * channels, cells)
            planes = jnp.where(is_odd, a_val, b_val) if lower else jnp.where(is_odd, b_val, a_val)
            turn = flip_matrix(codes_ref[0, side], cells, vertical)
            planes = dot(planes, turn).astype(BF16)
            base = 0 if lower else count + 2
            for index in range(2):
                fill(xs_ref, base + index, planes[index * channels:(index + 1) * channels])
                fill(cs_ref, base + index, planes[(index + 2) * channels:(index + 3) * channels])
        for a in range(count):
            fill(xs_ref, a + 2, x_ref[a])
            fill(cs_ref, a + 2, g_ref[a])

        zero = jnp.zeros((channels, cells), BF16)
        for a in range(-1, count + 1):
            low = (a + 1) * span
            window = slice(low, low + 3 * span)
            w_fwd = wp_ref[FW1_LO] if a == -1 else wp_ref[FW1_HI] if a == count else w1_ref[...]
            row = {-1: A2_M, 0: A2_0, count - 1: A2_7, count: A2_P}.get(a, A2)
            pre = dot(w_fwd, xs_ref[window, :])
            grad = dot(wp_ref[row], cs_ref[window, :])
            sig = jax.nn.sigmoid(pre)
            hidden = (pre * sig).astype(BF16)
            h_ref[(a + 1) * channels:(a + 2) * channels, :] = hidden
            pg = (grad * sig * (1.0 + pre * (1.0 - sig))).astype(BF16)
            pg_ref[a + 1, :, :] = pg
            place = count + 1 - a
            pr_ref[place * channels:(place + 1) * channels, :] = zero if a in (-1, count) else pg
        pr_ref[0:channels, :] = zero
        pr_ref[(count + 3) * channels:(count + 4) * channels, :] = zero

        grad_two = None
        for a in range(count):
            left = h_ref[a * channels:(a + 3) * channels, :]
            right = cs_ref[(a + 2) * span:(a + 3) * span, :]
            term = dot_nt(left, right)
            grad_two = term if grad_two is None else grad_two + term
        grad_one = None
        for a in range(-1, count + 1):
            start = (count - a) * channels
            left = pr_ref[start:start + 3 * channels, :]
            right = xs_ref[(a + 2) * span:(a + 3) * span, :]
            term = dot_nt(left, right)
            grad_one = term if grad_one is None else grad_one + term

        def put(ref, one):
            if one:
                for step in range(3):
                    ref[:, step * span:(step + 1) * span] = grad_one[step * channels:(step + 1) * channels]
            else:
                turned = grad_two.T
                for step in range(3):
                    for tap in range(9):
                        at = (9 * step + tap) * channels
                        ref[:, at:at + channels] = turned[
                            (8 - tap) * channels:(9 - tap) * channels, step * channels:(step + 1) * channels]

        @pl.when(odd == 0)
        def _():
            put(keep_ref, True)
            put(send_ref, False)

        @pl.when(odd == 1)
        def _():
            put(keep_ref, False)
            put(send_ref, True)

    return kernel


def make_input_kernel(count, channels, cells, vertical):
    span = 9 * channels

    def kernel(pg_ref, g_ref, wp_ref, out_ref, ps_ref):
        masks = tap_masks(cells, vertical)
        for a in range(count + 2):
            def store(tap, value, a=a):
                start = a * span + tap * channels
                ps_ref[start:start + channels, :] = value

            im2col(pg_ref[a], store, masks, vertical)
        for a in range(count):
            row = A1_0 if a == 0 else A1_7 if a == count - 1 else A1
            out_ref[a, :, :] = g_ref[a].astype(F32) + dot(wp_ref[row], ps_ref[a * span:(a + 3) * span, :])

    return kernel


def normalize_kernel(v_ref, o_ref):
    v = v_ref[...]
    o_ref[...] = v / jnp.sqrt(jnp.mean(v * v) + 1e-06)


VM = pl.BlockSpec(memory_space=pltpu.VMEM)
SM = pl.BlockSpec(memory_space=pltpu.SMEM)
PARAMS = pltpu.CompilerParams(vmem_limit_bytes=VMEM_LIMIT)


def body(snapshot, cotangent, first_weight, second_weight, face_codes):
    count, channels, cells = snapshot.shape[1:]
    vertical = cells // R_CELLS
    size = lax.axis_size(AXIS)
    x, g = snapshot[0], cotangent[0]
    odd = lax.axis_index(AXIS) % 2 == 1
    low = jnp.concatenate([x[:2], g[:2]], axis=0)
    high = jnp.concatenate([x[count - 2:], g[count - 2:]], axis=0)

    def cross_of(b):
        return (b + 1) % size if b % 2 == 1 else (b - 1) % size

    cross = lax.ppermute(jnp.where(odd, high, low), AXIS, [(b, cross_of(b)) for b in range(size)])
    pair = lax.ppermute(jnp.where(odd, low, high), AXIS, [(b, b ^ 1) for b in range(size)])

    weights = pl.pallas_call(
        prepare_kernel,
        out_shape=jax.ShapeDtypeStruct((10, channels, 27 * channels), BF16),
        in_specs=[SM, VM, VM], out_specs=VM, compiler_params=PARAMS, name="prepare",
    )(face_codes, first_weight, second_weight)

    grads = jax.ShapeDtypeStruct((channels, 27 * channels), F32)
    keep, send, pre_grad = pl.pallas_call(
        make_main_kernel(count, channels, cells, vertical),
        out_shape=(grads, grads, jax.ShapeDtypeStruct((count + 2, channels, cells), BF16)),
        in_specs=[SM, VM, VM, VM, VM, VM, VM], out_specs=(VM, VM, VM),
        scratch_shapes=[
            pltpu.VMEM(((count + 4) * 9 * channels, cells), BF16),
            pltpu.VMEM(((count + 4) * 9 * channels, cells), BF16),
            pltpu.VMEM(((count + 2) * channels, cells), BF16),
            pltpu.VMEM(((count + 4) * channels, cells), BF16),
        ],
        compiler_params=PARAMS, name="main",
    )(face_codes, x, g, pair, cross, first_weight, weights)

    def swap(value, bit):
        return lax.ppermute(value, AXIS, [(b, b ^ bit) for b in range(size)])

    total = keep + swap(send, 1)
    bit = 2
    while bit < size:
        total = total + swap(total, bit)
        bit *= 2

    input_grad = pl.pallas_call(
        make_input_kernel(count, channels, cells, vertical),
        out_shape=jax.ShapeDtypeStruct((count, channels, cells), F32),
        in_specs=[VM, VM, VM], out_specs=VM,
        scratch_shapes=[pltpu.VMEM(((count + 2) * 9 * channels, cells), BF16)],
        compiler_params=PARAMS, name="input_grad",
    )(pre_grad, g, weights)

    mine = pl.pallas_call(
        normalize_kernel, out_shape=grads, in_specs=[VM], out_specs=VM, compiler_params=PARAMS, name="normalize",
    )(total)
    other = swap(mine, 1)
    return (input_grad[None], jnp.where(odd, other, mine), jnp.where(odd, mine, other))


def solution(mesh):
    return jax.shard_map(
        body,
        mesh=mesh,
        in_specs=(
            P("groups", "blocks", None, None),
            P("groups", "blocks", None, None),
            P(),
            P(),
            P(("groups", "blocks"), None),
        ),
        out_specs=(P("groups", "blocks", None, None), P("groups", None), P("groups", None)),
        check_vma=False,
    )
```

time: 208 us -> 39 us (0.19)
  waiting for transfers between devices: 84.4 us -> 13.7 us
  matrix products: 62.4 us -> 0 us
  between operations: 21.7 us -> 0.73 us
  local copies, waits for them, and re-layouts: 12.2 us -> 0.98 us
  other arithmetic: 10.7 us -> 0.79 us
  Pallas kernels: 0 us -> 9.82 us
  starting transfers between devices: 14.9 us -> 12.7 us
    psum x1 -> x0, waiting for transfers between devices: 84.3 us -> none  [body(): first_total, second_total = lax.psum((first_grad, second_grad), 'blocks')]
    dot_general x171 -> x0, matrix products: 62.4 us -> none  [the longest x54 26.8 us: weight_gradient(): jnp.einsum('baop,bacp->oc', cotan, moved[:, step_a:step_a + count], prefe...]
    ppermute x8 -> x7, waiting for transfers between devices: 0.02 us -> 13.7 us  [the longest x5 12.5 us: swap(): return lax.ppermute(value, AXIS, [(b, b ^ bit) for b in range(size)])]
    pallas_call x0 -> x4, Pallas kernels: none -> 9.82 us  [the longest x1 5.86 us: body(): pl.pallas_call(make_main_kernel(count, channels, cells, vertical), out_sh...]
    select_n x20 -> x2, other arithmetic: 4.5 us -> 0.73 us  [the longest x1 0.7 us: body(): jnp.where(odd, mine, other)]
    unnamed x18 -> x10, local copies, waits for them, and re-layouts: 2.68 us -> 0.03 us
    reshape x8 -> x0, local copies, waits for them, and re-layouts: 2.57 us -> none  [the longest x4 1.66 us: flip_plane(): return grid.reshape(batch_count, channels, radial * vertical)]
    concatenate x2 -> x0, local copies, waits for them, and re-layouts: 2.55 us -> none  [weight_gradient(): return jnp.concatenate([found[index] for index in range(27)], axis=1)]
  transfers between devices with their start and end apart: 9 -> 7, of which waited for: 1 -> 5; matrix products, arithmetic and copies ran while one was open for 35% -> 0% of each run, Pallas kernels for 0% -> 10%
where the time goes in v1:
time: 39 us; the launch traced here: 38.8 us
  waiting for transfers between devices  13.7 us (35%)
  starting transfers between devices  12.7 us (33%)
  Pallas kernels  9.82 us (25%)
  local copies, waits for them, and re-layouts  0.98 us (3%)
  other arithmetic  0.79 us (2%)
  between operations  0.73 us (2%)
    ppermute x5, waiting for transfers between devices, swap(): return lax.ppermute(value, AXIS, [(b, b ^ bit) for b in range(size)])  12.5 us
    ppermute x5, starting transfers between devices, swap(): return lax.ppermute(value, AXIS, [(b, b ^ bit) for b in range(size)])  9.96 us
    pallas_call x1, Pallas kernels, body(): pl.pallas_call(make_main_kernel(count, channels, cells, vertical), out_sh...  5.86 us
    ppermute x1, starting transfers between devices, body(): lax.ppermute(jnp.where(odd, high, low), AXIS, [(b, cross_of(b)) for b in...  2.64 us
    pallas_call x1, Pallas kernels, body(): pl.pallas_call(make_input_kernel(count, channels, cells, vertical), out_s...  2.38 us
    pallas_call x1, Pallas kernels, body(): pl.pallas_call(prepare_kernel, out_shape=jax.ShapeDtypeStruct((10, channe...  1.39 us
    ppermute x1, waiting for transfers between devices, body(): lax.ppermute(jnp.where(odd, high, low), AXIS, [(b, cross_of(b)) for b in...  1.24 us
    slice x1, local copies, waits for them, and re-layouts, body(): low = jnp.concatenate([x[:2], g[:2]], axis=0)  0.96 us
  transfers between devices with their start and end apart: 7, of which 5 were waited for; matrix products, arithmetic and copies ran while one was open for 0% of the time, Pallas kernels for 10%

profile of v1, /device:TPU:1, one launch (start us, length us, event | category | flops | bytes accessed | tf_op | source)
XLA Modules:
  0.0 38.8 jit_solution(4494832946330036199)
XLA Ops:
  0.6 1.0 %slice_bitcast_fusion.2 = (bf16[2,32,512]{2,1,0:T(8,128)(2,1)S(1)}, bf16[2,32,512]{2,1,0:T(8,128)(2,1)S(1)}, bf16[2,32,512]{2,1,0:T(8,128)(2,1)S(1)}, bf16[2,32,512]{2,1,0:T(8,128)(2,1)S(1)}) fusion(bf16[1,8,32,512]{3,2,1,0:T(8,128)(2,1)} %param.6, bf16[1,8,32,512]{3,2,1,0:T(8,128)(2,1)} %param.5), kind=kLoop, calls=%fused_computation.6 | loop fusion | bytes 524288 | tf_op jit(solution)/shard_map/slice | solution.py:243
  1.6 0.0 copy-start.2
  1.6 0.0 copy-start.3
  1.7 0.0 copy-start.4
  1.7 0.1 collective-permute-start
  1.8 2.6 %collective-permute-start.1 = (bf16[4,32,512]{2,1,0:T(8,128)(2,1)S(1)}, bf16[4,32,512]{2,1,0:T(8,128)(2,1)S(1)}, u32[]{:S(2)}, u32[]{:S(2)}) collective-permute-start(bf16[4,32,512]{2,1,0:T(8,128)(2,1)S(1)} %get-tuple-element.9), channel_id=1, source_target_pairs={{0,15},{1,2},{2,1},{3,4},{4,3},{5,6},{6,5},{7,8},{8,7},{9,10},{10,... | collective-permute-start | bytes 393224 | tf_op jit(solution)/shard_map/ppermute | solution.py:249
  4.4 0.0 copy-done.2
  4.5 1.4 %prepare.1.wp_ref = bf16[10,32,864]{2,1,0:T(8,128)(2,1)S(1)} custom-call(s32[1,2]{1,0:T(1,128)S(1)} %copy-done.4, bf16[32,864]{1,0:T(8,128)(2,1)S(1)} %copy-done.2, bf16[32,864]{1,0:T(8,128)(2,1)S(1)} %copy-done.3), custom_call_target="tpu_custom_call" | custom-call | tf_op jit(solution)/shard_map/prepare/pallas_call | solution.py:252
  5.8 0.0 collective-permute-done.pair_ref
  5.9 1.2 %collective-permute-done.1.cross_ref = bf16[4,32,512]{2,1,0:T(8,128)(2,1)S(1)} collective-permute-done((bf16[4,32,512]{2,1,0:T(8,128)(2,1)S(1)}, bf16[4,32,512]{2,1,0:T(8,128)(2,1)S(1)}, u32[]{:S(2)}, u32[]{:S(2)}) %collective-permute-start.1) | collective-permute-done | bytes 131104 | tf_op jit(solution)/shard_map/ppermute | solution.py:249
  7.1 5.9 %main.1 = (f32[32,864]{1,0:T(8,128)S(1)}, f32[32,864]{1,0:T(8,128)S(1)}, bf16[10,32,512]{2,1,0:T(8,128)(2,1)S(1)}) custom-call(s32[1,2]{1,0:T(1,128)S(1)} %copy-done.4, bf16[8,32,512]{2,1,0:T(8,128)(2,1)S(1)} %bitcast.13, bf16[8,32,512]{2,1,0:T(8,128)(2,1)S(1)} %bitcast.11, bf16[4,32,512]{2,1,0:T(8,128)(2,1)S(1)} %collective-permute-done.pair_ref, ...), custom_call_target="tpu_custom_call" | custom-call | tf_op jit(solution)/shard_map/main/pallas_call | solution.py:259
  13.0 3.5 %collective-permute-start.2 = (f32[32,864]{1,0:T(8,128)S(1)}, f32[32,864]{1,0:T(8,128)S(1)}, u32[]{:S(2)}, u32[]{:S(2)}) collective-permute-start(f32[32,864]{1,0:T(8,128)S(1)} %get-tuple-element.8), channel_id=1, source_target_pairs={{0,1},{1,0},{2,3},{3,2},{4,5},{5,4},{6,7},{7,6},{8,9},{9,8},{10,11... | collective-permute-start | bytes 331784 | tf_op jit(solution)/shard_map/ppermute | solution.py:273
  16.5 1.0 %collective-permute-done.2 = f32[32,864]{1,0:T(8,128)S(1)} collective-permute-done((f32[32,864]{1,0:T(8,128)S(1)}, f32[32,864]{1,0:T(8,128)S(1)}, u32[]{:S(2)}, u32[]{:S(2)}) %collective-permute-start.2) | collective-permute-done | bytes 110624 | tf_op jit(solution)/shard_map/ppermute | solution.py:273
  17.4 0.1 collective-permute-start.3
  17.5 4.4 %collective-permute-done.3 = f32[32,864]{1,0:T(8,128)S(1)} collective-permute-done((f32[32,864]{1,0:T(8,128)S(1)}, f32[32,864]{1,0:T(8,128)S(1)}, u32[]{:S(2)}, u32[]{:S(2)}) %collective-permute-start.3) | collective-permute-done | bytes 110624 | tf_op jit(solution)/shard_map/ppermute | solution.py:273
  21.9 0.5 %collective-permute-start.4 = (f32[32,864]{1,0:T(8,128)S(1)}, f32[32,864]{1,0:T(8,128)S(1)}, u32[]{:S(2)}, u32[]{:S(2)}) collective-permute-start(f32[32,864]{1,0:T(8,128)S(1)} %add.18), channel_id=1, source_target_pairs={{0,4},{1,5},{2,6},{3,7},{4,0},{5,1},{6,2},{7,3},{8,12},{9,13},{10,... | collective-permute-start | bytes 331784 | tf_op jit(solution)/shard_map/ppermute | solution.py:273
  22.4 3.2 %collective-permute-done.4 = f32[32,864]{1,0:T(8,128)S(1)} collective-permute-done((f32[32,864]{1,0:T(8,128)S(1)}, f32[32,864]{1,0:T(8,128)S(1)}, u32[]{:S(2)}, u32[]{:S(2)}) %collective-permute-start.4) | collective-permute-done | bytes 110624 | tf_op jit(solution)/shard_map/ppermute | solution.py:273
  25.6 3.2 %collective-permute-start.5 = (f32[32,864]{1,0:T(8,128)S(1)}, f32[32,864]{1,0:T(8,128)S(1)}, u32[]{:S(2)}, u32[]{:S(2)}) collective-permute-start(f32[32,864]{1,0:T(8,128)S(1)} %add.19), channel_id=1, source_target_pairs={{0,8},{1,9},{2,10},{3,11},{4,12},{5,13},{6,14},{7,15},{8,0},{9,1},... | collective-permute-start | bytes 331784 | tf_op jit(solution)/shard_map/ppermute | solution.py:273
  28.8 3.9 %collective-permute-done.5 = f32[32,864]{1,0:T(8,128)S(1)} collective-permute-done((f32[32,864]{1,0:T(8,128)S(1)}, f32[32,864]{1,0:T(8,128)S(1)}, u32[]{:S(2)}, u32[]{:S(2)}) %collective-permute-start.5) | collective-permute-done | bytes 110624 | tf_op jit(solution)/shard_map/ppermute | solution.py:273
  32.8 0.2 normalize.1
  33.0 2.7 %collective-permute-start.6 = (f32[32,864]{1,0:T(8,128)S(1)}, f32[32,864]{1,0:T(8,128)S(1)}, u32[]{:S(2)}, u32[]{:S(2)}) collective-permute-start(f32[32,864]{1,0:T(8,128)S(1)} %normalize.1), channel_id=1, source_target_pairs={{0,1},{1,0},{2,3},{3,2},{4,5},{5,4},{6,7},{7,6},{8,9},{9,8},{10,11... | collective-permute-start | bytes 331784 | tf_op jit(solution)/shard_map/ppermute | solution.py:273
  35.7 2.4 %input_grad.1 = f32[8,32,512]{2,1,0:T(8,128)} custom-call(bf16[10,32,512]{2,1,0:T(8,128)(2,1)S(1)} %get-tuple-element.6.pg_ref, bf16[8,32,512]{2,1,0:T(8,128)(2,1)S(1)} %bitcast.12, bf16[10,32,864]{2,1,0:T(8,128)(2,1)S(1)} %prepare.1.wp_ref), custom_call_target="tpu_custom_call" | custom-call | tf_op jit(solution)/shard_map/input_grad/pallas_call | solution.py:281
  38.1 0.0 collective-permute-done.6
  38.1 0.7 %broadcast_select_fusion.2 = (f32[32,864]{1,0:T(8,128)}, f32[32,864]{1,0:T(8,128)}) fusion(f32[32,864]{1,0:T(8,128)S(1)} %normalize.1, f32[32,864]{1,0:T(8,128)S(1)} %collective-permute-done.6, pred[]{:T(512)S(6)} %eq.5), kind=kLoop, calls=%fused_computation.8 | loop fusion | flops 55296 | bytes 442369 | tf_op jit(solution)/shard_map/jit(_where)/select_n | solution.py:293
  (11 shorter events, 0.1 us)
Async XLA Ops:
  1.6 2.8 %copy-start.2 = (bf16[32,864]{1,0:T(8,128)(2,1)S(1)}, bf16[32,864]{1,0:T(8,128)(2,1)}, u32[]{:S(2)}) copy-start(bf16[32,864]{1,0:T(8,128)(2,1)} %w1_ref.3) | copy-start | bytes 165892
  1.6 2.8 %copy-start.3 = (bf16[32,864]{1,0:T(8,128)(2,1)S(1)}, bf16[32,864]{1,0:T(8,128)(2,1)}, u32[]{:S(2)}) copy-start(bf16[32,864]{1,0:T(8,128)(2,1)} %w2_ref.1) | copy-start | bytes 165892
  1.7 2.8 %copy-start.4 = (s32[1,2]{1,0:T(1,128)S(1)}, s32[1,2]{1,0:T(1,128)}, u32[]{:S(2)}) copy-start(s32[1,2]{1,0:T(1,128)} %codes_ref.3) | copy-start | bytes 28
  1.7 4.2 %collective-permute-start = (bf16[4,32,512]{2,1,0:T(8,128)(2,1)S(1)}, bf16[4,32,512]{2,1,0:T(8,128)(2,1)S(1)}, u32[]{:S(2)}, u32[]{:S(2)}) collective-permute-start(bf16[4,32,512]{2,1,0:T(8,128)(2,1)S(1)} %get-tuple-element.10), channel_id=1, source_target_pairs={{0,1},{1,0},{2,3},{3,2},{4,5},{5,4},{6,7},{7,6},{8,9},{9,8},{10,11... | collective-permute-start | bytes 393224 | tf_op jit(solution)/shard_map/ppermute | solution.py:250
  1.8 5.3 %copy-start = (bf16[1,8,32,512]{3,2,1,0:T(8,128)(2,1)S(1)}, bf16[1,8,32,512]{3,2,1,0:T(8,128)(2,1)}, u32[]{:S(2)}) copy-start(bf16[1,8,32,512]{3,2,1,0:T(8,128)(2,1)} %param.6) | copy-start | bytes 786436
  1.8 5.3 %copy-start.1 = (bf16[1,8,32,512]{3,2,1,0:T(8,128)(2,1)S(1)}, bf16[1,8,32,512]{3,2,1,0:T(8,128)(2,1)}, u32[]{:S(2)}) copy-start(bf16[1,8,32,512]{3,2,1,0:T(8,128)(2,1)} %param.5) | copy-start | bytes 786436
  1.8 5.3 %collective-permute-start.1 = (bf16[4,32,512]{2,1,0:T(8,128)(2,1)S(1)}, bf16[4,32,512]{2,1,0:T(8,128)(2,1)S(1)}, u32[]{:S(2)}, u32[]{:S(2)}) collective-permute-start(bf16[4,32,512]{2,1,0:T(8,128)(2,1)S(1)} %get-tuple-element.9), channel_id=1, source_target_pairs={{0,15},{1,2},{2,1},{3,4},{4,3},{5,6},{6,5},{7,8},{8,7},{9,10},{10,... | collective-permute-start | bytes 393224 | tf_op jit(solution)/shard_map/ppermute | solution.py:249
  13.0 4.5 %collective-permute-start.2 = (f32[32,864]{1,0:T(8,128)S(1)}, f32[32,864]{1,0:T(8,128)S(1)}, u32[]{:S(2)}, u32[]{:S(2)}) collective-permute-start(f32[32,864]{1,0:T(8,128)S(1)} %get-tuple-element.8), channel_id=1, source_target_pairs={{0,1},{1,0},{2,3},{3,2},{4,5},{5,4},{6,7},{7,6},{8,9},{9,8},{10,11... | collective-permute-start | bytes 331784 | tf_op jit(solution)/shard_map/ppermute | solution.py:273
  17.4 4.4 %collective-permute-start.3 = (f32[32,864]{1,0:T(8,128)S(1)}, f32[32,864]{1,0:T(8,128)S(1)}, u32[]{:S(2)}, u32[]{:S(2)}) collective-permute-start(f32[32,864]{1,0:T(8,128)S(1)} %add.17), channel_id=1, source_target_pairs={{0,2},{1,3},{2,0},{3,1},{4,6},{5,7},{6,4},{7,5},{8,10},{9,11},{10,... | collective-permute-start | bytes 331784 | tf_op jit(solution)/shard_map/ppermute | solution.py:273
  21.9 3.7 %collective-permute-start.4 = (f32[32,864]{1,0:T(8,128)S(1)}, f32[32,864]{1,0:T(8,128)S(1)}, u32[]{:S(2)}, u32[]{:S(2)}) collective-permute-start(f32[32,864]{1,0:T(8,128)S(1)} %add.18), channel_id=1, source_target_pairs={{0,4},{1,5},{2,6},{3,7},{4,0},{5,1},{6,2},{7,3},{8,12},{9,13},{10,... | collective-permute-start | bytes 331784 | tf_op jit(solution)/shard_map/ppermute | solution.py:273
  25.6 7.1 %collective-permute-start.5 = (f32[32,864]{1,0:T(8,128)S(1)}, f32[32,864]{1,0:T(8,128)S(1)}, u32[]{:S(2)}, u32[]{:S(2)}) collective-permute-start(f32[32,864]{1,0:T(8,128)S(1)} %add.19), channel_id=1, source_target_pairs={{0,8},{1,9},{2,10},{3,11},{4,12},{5,13},{6,14},{7,15},{8,0},{9,1},... | collective-permute-start | bytes 331784 | tf_op jit(solution)/shard_map/ppermute | solution.py:273
  33.0 5.1 %collective-permute-start.6 = (f32[32,864]{1,0:T(8,128)S(1)}, f32[32,864]{1,0:T(8,128)S(1)}, u32[]{:S(2)}, u32[]{:S(2)}) collective-permute-start(f32[32,864]{1,0:T(8,128)S(1)} %normalize.1), channel_id=1, source_target_pairs={{0,1},{1,0},{2,3},{3,2},{4,5},{5,4},{6,7},{7,6},{8,9},{9,8},{10,11... | collective-permute-start | bytes 331784 | tf_op jit(solution)/shard_map/ppermute | solution.py:273

commit v2 on v1

v2 whole, which is shorter than its diff:
```python
import jax
import jax.numpy as jnp
from jax import lax
from jax.experimental import pallas as pl
from jax.experimental.pallas import tpu as pltpu
from jax.sharding import PartitionSpec as P

R_CELLS = 32
AXIS = "blocks"
F32 = jnp.float32
BF16 = jnp.bfloat16
VMEM_LIMIT = 24 * 1024 * 1024


def tap_masks(cells, vertical):
    lane = lax.broadcasted_iota(jnp.int32, (1, cells), 1)
    z = lane % vertical
    r = lane // vertical
    radial = cells // vertical
    masks = []
    for step_r in range(3):
        for step_z in range(3):
            ok = None
            if step_r == 0:
                ok = r >= 1
            if step_r == 2:
                ok = r < radial - 1
            if step_z == 0:
                ok = (z >= 1) if ok is None else ok & (z >= 1)
            if step_z == 2:
                ok = (z < vertical - 1) if ok is None else ok & (z < vertical - 1)
            masks.append(ok)
    return masks


def im2col(plane, store, masks, vertical):
    cells = plane.shape[1]
    wide = plane.astype(F32)
    for tap in range(9):
        offset = (tap // 3 - 1) * vertical + (tap % 3 - 1)
        if offset == 0:
            store(tap, plane)
            continue
        moved = pltpu.roll(wide, (-offset) % cells, 1)
        moved = jnp.where(masks[tap], moved, 0.0)
        store(tap, moved.astype(BF16))


def dot(a, b):
    return jnp.dot(a, b, preferred_element_type=F32)


def dot_nt(a, b):
    return lax.dot_general(a, b, (((1,), (1,)), ((), ())), preferred_element_type=F32)


def flip_matrix(code, cells, vertical):
    row = lax.broadcasted_iota(jnp.int32, (cells, cells), 0)
    col = lax.broadcasted_iota(jnp.int32, (1, cells), 1)
    bits = jnp.where(code % 2 == 1, cells - vertical, 0) + jnp.where(code // 2 == 1, vertical - 1, 0)
    return jnp.where(row == (col ^ bits), 1.0, 0.0).astype(BF16)


def tap_flip_matrix(code, channels):
    size = 9 * channels
    row = lax.broadcasted_iota(jnp.int32, (size, size), 0)
    col = lax.broadcasted_iota(jnp.int32, (1, size), 1)
    tap = col // channels
    r, z = tap // 3, tap % 3
    r = jnp.where(code % 2 == 1, 2 - r, r)
    z = jnp.where(code // 2 == 1, 2 - z, z)
    return jnp.where(row == (3 * r + z) * channels + col % channels, 1.0, 0.0).astype(BF16)


def activation(pre, grad):
    sig = jax.nn.sigmoid(pre)
    hidden = (pre * sig).astype(BF16)
    return hidden, (grad * sig * (1.0 + pre * (1.0 - sig))).astype(BF16)


def filler(ref, channels, masks, vertical):
    def fill(position, plane):
        def store(tap, value):
            start = (9 * position + tap) * channels
            ref[start:start + channels, :] = value

        im2col(plane, store, masks, vertical)

    return fill


def make_pack_kernel(count, channels, cells):
    def kernel(codes_ref, x_ref, g_ref, w1_ref, w2_ref,
               cross_ref, pair_ref, codes_out, x_out, g_out, w1_out, w2_out, scalars, sems):
        copies = [
            pltpu.make_async_copy(source, target, sems.at[index])
            for index, (source, target) in enumerate(
                ((x_ref, x_out), (g_ref, g_out), (w1_ref, w1_out), (w2_ref, w2_out), (codes_ref, scalars)))
        ]
        for copy in copies:
            copy.start()
        is_odd = lax.axis_index(AXIS) % 2 == 1
        for index, field in enumerate((x_out, g_out)):
            copies[index].wait()
            low, high = field[0:2], field[count - 2:count]
            cross_ref[2 * index:2 * index + 2, :, :] = jnp.where(is_odd, high, low)
            pair_ref[2 * index:2 * index + 2, :, :] = jnp.where(is_odd, low, high)
        for copy in copies[2:]:
            copy.wait()
        for side in range(2):
            codes_out[side, :, :] = jnp.full((8, 128), scalars[0, side], jnp.int32)

    return kernel


def make_interior_kernel(count, channels, cells, vertical):
    span = 9 * channels
    wide = 3 * channels
    last = count - 1

    def kernel(codes_ref, x_ref, g_ref, w1_ref, w2_ref,
               ws_ref, lo_ref, hi_ref, turn_ref, pe_ref, ge_ref, xs_ref, cs_ref, pg_ref, g1_ref, g2_ref,
               h_ref, pr_ref):
        masks = tap_masks(cells, vertical)
        for step in range(3):
            ws_ref[step * channels:(step + 1) * channels, :] = w1_ref[:, step * span:(step + 1) * span]
        for weight_ref, base in ((w2_ref, wide), (w1_ref, 2 * wide)):
            turned = weight_ref[...].astype(F32).T
            for step in range(3):
                for tap in range(9):
                    at = (9 * (2 - step) + 8 - tap) * channels
                    ws_ref[base + step * channels:base + (step + 1) * channels, tap * channels:(tap + 1) * channels] = (
                        turned[at:at + channels, :].astype(BF16))
        lo_ref[...] = dot(ws_ref[...], tap_flip_matrix(codes_ref[0, 0:1, 0:1], channels)).astype(BF16)
        hi_ref[...] = dot(ws_ref[...], tap_flip_matrix(codes_ref[1, 0:1, 0:1], channels)).astype(BF16)
        for side in range(2):
            turn_ref[side, :, :] = flip_matrix(codes_ref[side, 0:1, 0:1], cells, vertical)

        fill_x = filler(xs_ref, channels, masks, vertical)
        fill_g = filler(cs_ref, channels, masks, vertical)
        for a in range(count):
            fill_x(a, x_ref[a])
            fill_g(a, g_ref[a])

        h_ref[...] = jnp.zeros_like(h_ref)
        pr_ref[...] = jnp.zeros_like(pr_ref)
        pre, grad = {}, {}

        def add(table, key, value):
            table[key] = value if key not in table else table[key] + value

        for a in range(count):
            columns = slice(a * span, (a + 1) * span)
            y = dot(ws_ref[0:wide, :], xs_ref[columns, :])
            v = dot(ws_ref[wide:2 * wide, :], cs_ref[columns, :])
            for step in range(3):
                target = a + 1 - step
                rows = slice(step * channels, (step + 1) * channels)
                add(grad, target, v[rows])
                if 0 <= target <= last:
                    add(pre, target, y[rows])
            if a == 0:
                pre[-1] = dot(lo_ref[2 * channels:wide, :], xs_ref[columns, :])
            if a == last:
                pre[count] = dot(hi_ref[0:channels, :], xs_ref[columns, :])
            done = a - 1
            if 1 <= done <= last - 1:
                hidden, pg = activation(pre.pop(done), grad.pop(done))
                h_ref[(done + 1) * channels:(done + 2) * channels, :] = hidden
                pg_ref[done - 1, :, :] = pg
                place = count + 1 - done
                pr_ref[place * channels:(place + 1) * channels, :] = pg
            if a == 1:
                for index, plane in ((0, -1), (1, 0)):
                    pe_ref[index, :, :] = pre.pop(plane)
                    ge_ref[index, :, :] = grad.pop(plane)
        for index, plane in ((2, last), (3, count)):
            pe_ref[index, :, :] = pre.pop(plane)
            ge_ref[index, :, :] = grad.pop(plane)

        grad_one, grad_two = None, None
        for a in range(count):
            term = dot_nt(cs_ref[a * span:(a + 1) * span, :], h_ref[a * channels:(a + 3) * channels, :])
            grad_two = term if grad_two is None else grad_two + term
            start = (count - a) * channels
            term = dot_nt(xs_ref[a * span:(a + 1) * span, :], pr_ref[start:start + wide, :])
            grad_one = term if grad_one is None else grad_one + term
        g2_ref[...] = grad_two
        turned = grad_one.T
        for step in range(3):
            g1_ref[:, step * span:(step + 1) * span] = turned[step * channels:(step + 1) * channels]

    return kernel


def make_edge_kernel(count, channels, cells, vertical):
    span = 9 * channels
    wide = 3 * channels
    last = count - 1

    def kernel(pair_ref, cross_ref, ws_ref, lo_ref, hi_ref, turn_ref, pe_ref, ge_ref, xs_ref, cs_ref, g1_ref, g2_ref,
               keep_ref, send_ref, pg_ref, xh_ref, ch_ref):
        odd = lax.axis_index(AXIS) % 2
        is_odd = odd == 1
        masks = tap_masks(cells, vertical)
        fill_x = filler(xh_ref, channels, masks, vertical)
        fill_c = filler(ch_ref, channels, masks, vertical)
        pair = pair_ref[...].reshape(4 * channels, cells)
        cross = cross_ref[...].reshape(4 * channels, cells)
        for side in range(2):
            planes = jnp.where(is_odd, pair, cross) if side == 0 else jnp.where(is_odd, cross, pair)
            planes = dot(planes, turn_ref[side]).astype(BF16)
            for index in range(2):
                fill_x(2 * side + index, planes[index * channels:(index + 1) * channels])
                fill_c(2 * side + index, planes[(index + 2) * channels:(index + 3) * channels])

        def halo(ref, index):
            return ref[index * span:(index + 1) * span, :]

        def rows(ref, part, first, end):
            return ref[part * wide + first * channels:part * wide + end * channels, :]

        near = dot(jnp.concatenate([rows(ws_ref, 0, 0, 1), rows(lo_ref, 0, 1, 2)], axis=0), halo(xh_ref, 1))
        pre_m = pe_ref[0] + near[channels:] + dot(rows(lo_ref, 0, 0, 1), halo(xh_ref, 0))
        pre_0 = pe_ref[1] + near[:channels]
        near = dot(rows(lo_ref, 1, 0, 2), halo(ch_ref, 1))
        grad_m = ge_ref[0] + near[channels:] + dot(rows(lo_ref, 1, 0, 1), halo(ch_ref, 0))
        grad_0 = ge_ref[1] + near[:channels]
        near = dot(jnp.concatenate([rows(hi_ref, 0, 1, 2), rows(ws_ref, 0, 2, 3)], axis=0), halo(xh_ref, 2))
        pre_p = pe_ref[3] + near[:channels] + dot(rows(hi_ref, 0, 2, 3), halo(xh_ref, 3))
        pre_7 = pe_ref[2] + near[channels:]
        near = dot(rows(hi_ref, 1, 1, 3), halo(ch_ref, 2))
        grad_p = ge_ref[3] + near[:channels] + dot(rows(hi_ref, 1, 2, 3), halo(ch_ref, 3))
        grad_7 = ge_ref[2] + near[channels:]

        hid_m, pg_m = activation(pre_m, grad_m)
        hid_0, pg_0 = activation(pre_0, grad_0)
        hid_7, pg_7 = activation(pre_7, grad_7)
        hid_p, pg_p = activation(pre_p, grad_p)
        for index, pg in enumerate((pg_m, pg_0, pg_7, pg_p)):
            pg_ref[index, :, :] = pg

        zero = jnp.zeros((channels, cells), BF16)
        grad_two = g2_ref[...]
        for a, stack in ((0, (hid_m, hid_0, zero)), (1, (hid_0, zero, zero)),
                         (last - 1, (zero, zero, hid_7)), (last, (zero, hid_7, hid_p))):
            grad_two = grad_two + dot_nt(cs_ref[a * span:(a + 1) * span, :], jnp.concatenate(stack, axis=0))
        low_end = dot_nt(pg_0, halo(xh_ref, 1))
        low_own = dot_nt(pg_0, xs_ref[0:2 * span, :])
        high_own = dot_nt(pg_7, xs_ref[(last - 1) * span:(last + 1) * span, :])
        high_end = dot_nt(pg_7, halo(xh_ref, 2))

        def put(ref, one):
            if one:
                ref[:, 0:span] = g1_ref[:, 0:span] + low_end + high_own[:, 0:span]
                ref[:, span:2 * span] = g1_ref[:, span:2 * span] + low_own[:, 0:span] + high_own[:, span:]
                ref[:, 2 * span:] = g1_ref[:, 2 * span:] + low_own[:, span:] + high_end
            else:
                for step in range(3):
                    for tap in range(9):
                        at = (9 * step + tap) * channels
                        ref[:, at:at + channels] = grad_two[
                            (8 - tap) * channels:(9 - tap) * channels, step * channels:(step + 1) * channels]

        @pl.when(odd == 0)
        def _():
            put(keep_ref, True)
            put(send_ref, False)

        @pl.when(odd == 1)
        def _():
            put(keep_ref, False)
            put(send_ref, True)

    return kernel


def make_input_kernel(count, channels, cells, vertical):
    span = 9 * channels
    wide = 3 * channels

    def kernel(pi_ref, pe_ref, g_ref, ws_ref, lo_ref, hi_ref, out_ref, ps_ref):
        fill = filler(ps_ref, channels, tap_masks(cells, vertical), vertical)
        total = {}
        for a in range(-1, count + 1):
            plane = pe_ref[a + 1] if a <= 0 else pe_ref[a - count + 3] if a >= count - 1 else pi_ref[a - 1]
            fill(a + 1, plane)
            columns = ps_ref[(a + 1) * span:(a + 2) * span, :]
            if a == -1:
                total[0] = dot(lo_ref[2 * wide:2 * wide + channels, :], columns)
            elif a == count:
                total[count - 1] = total[count - 1] + dot(hi_ref[3 * wide - channels:3 * wide, :], columns)
            else:
                y = dot(ws_ref[2 * wide:3 * wide, :], columns)
                for step in range(3):
                    target = a + 1 - step
                    if 0 <= target < count:
                        part = y[step * channels:(step + 1) * channels]
                        total[target] = part if target not in total else total[target] + part
            if a >= 1:
                out_ref[a - 1, :, :] = g_ref[a - 1].astype(F32) + total.pop(a - 1)

    return kernel


def normalize_kernel(mine_ref, other_ref, one_ref, two_ref):
    odd = lax.axis_index(AXIS) % 2

    def scaled(ref):
        v = ref[...]
        return v / jnp.sqrt(jnp.mean(v * v) + 1e-06)

    @pl.when(odd == 0)
    def _():
        one_ref[...] = scaled(mine_ref)
        two_ref[...] = scaled(other_ref)

    @pl.when(odd == 1)
    def _():
        one_ref[...] = scaled(other_ref)
        two_ref[...] = scaled(mine_ref)


VM = pl.BlockSpec(memory_space=pltpu.VMEM)
SM = pl.BlockSpec(memory_space=pltpu.SMEM)
HB = pl.BlockSpec(memory_space=pltpu.HBM)
PARAMS = pltpu.CompilerParams(vmem_limit_bytes=VMEM_LIMIT)


def body(snapshot, cotangent, first_weight, second_weight, face_codes):
    count, channels, cells = snapshot.shape[1:]
    vertical = cells // R_CELLS
    size = lax.axis_size(AXIS)
    x, g = snapshot[0], cotangent[0]
    def call(kernel, outs, operands, name, scratch=(), specs=None):
        return pl.pallas_call(
            kernel, out_shape=outs, in_specs=specs or [VM] * len(operands),
            out_specs=jax.tree.map(lambda _: VM, outs),
            scratch_shapes=list(scratch), compiler_params=PARAMS, name=name,
        )(*operands)

    span = 9 * channels
    shape = jax.ShapeDtypeStruct
    sizes = (count, channels, cells, vertical)
    stack = shape((span, span), BF16)
    edges = shape((4, channels, cells), F32)
    columns = shape((count * span, cells), BF16)
    grads = shape((channels, 27 * channels), F32)
    half = shape((4, channels, cells), BF16)
    cross, pair, codes, x, g, first_weight, second_weight = call(
        make_pack_kernel(count, channels, cells),
        (half, half, shape((2, 8, 128), jnp.int32), shape(x.shape, BF16), shape(x.shape, BF16),
         shape(first_weight.shape, BF16), shape(first_weight.shape, BF16)),
        tuple(pltpu.with_memory_space_constraint(v, pltpu.HBM) for v in (face_codes, x, g, first_weight, second_weight)),
        "pack", [pltpu.SMEM((1, 2), jnp.int32), pltpu.SemaphoreType.DMA((5,))], [HB] * 5)

    def cross_of(b):
        return (b + 1) % size if b % 2 == 1 else (b - 1) % size

    cross = lax.ppermute(cross, AXIS, [(b, cross_of(b)) for b in range(size)])
    pair = lax.ppermute(pair, AXIS, [(b, b ^ 1) for b in range(size)])
    ws, lo, hi, turn, pre_edge, grad_edge, xs, cs, pg_inner, part_one, part_two = call(
        make_interior_kernel(*sizes),
        (stack, stack, stack, shape((2, cells, cells), BF16), edges, edges, columns, columns,
         shape((count - 2, channels, cells), BF16), grads, shape((span, 3 * channels), F32)),
        (codes, x, g, first_weight, second_weight), "interior",
        [pltpu.VMEM(((count + 2) * channels, cells), BF16), pltpu.VMEM(((count + 3) * channels, cells), BF16)])
    keep, send, pg_edge = call(
        make_edge_kernel(*sizes), (grads, grads, shape((4, channels, cells), BF16)),
        (pair, cross, ws, lo, hi, turn, pre_edge, grad_edge, xs, cs, part_one, part_two), "edge",
        [pltpu.VMEM((4 * span, cells), BF16), pltpu.VMEM((4 * span, cells), BF16)])

    def swap(value, bit):
        return lax.ppermute(value, AXIS, [(b, b ^ bit) for b in range(size)])

    input_grad = call(
        make_input_kernel(*sizes), shape((count, channels, cells), F32), (pg_inner, pg_edge, g, ws, lo, hi),
        "input_grad", [pltpu.VMEM(((count + 2) * span, cells), BF16)])
    total = keep + swap(send, 1)
    bit = 2
    while bit < size:
        total = total + swap(total, bit)
        if bit == 2:
            total, input_grad = lax.optimization_barrier((total, input_grad))
        bit *= 2
    first, second = call(normalize_kernel, (grads, grads), (total, swap(total, 1)), "normalize")
    return (input_grad[None], first, second)


def solution(mesh):
    return jax.shard_map(
        body,
        mesh=mesh,
        in_specs=(
            P("groups", "blocks", None, None),
            P("groups", "blocks", None, None),
            P(),
            P(),
            P(("groups", "blocks"), None),
        ),
        out_specs=(P("groups", "blocks", None, None), P("groups", None), P("groups", None)),
        check_vma=False,
    )
```

time: 39 us -> 34.9 us (0.89)
  starting transfers between devices: 12.7 us -> 9.64 us
  local copies, waits for them, and re-layouts: 0.98 us -> 0 us
  other arithmetic: 0.79 us -> 0.05 us
    ppermute x5, starting transfers between devices: 9.96 us -> 6.89 us  [swap(): return lax.ppermute(value, AXIS, [(b, b ^ bit) for b in range(size)])]
    ppermute x5, waiting for transfers between devices: 12.5 us -> 13.9 us  [swap(): return lax.ppermute(value, AXIS, [(b, b ^ bit) for b in range(size)])]
    ppermute x2, waiting for transfers between devices: 1.24 us -> 0.01 us  [the longest x1 0.01 us: body(): cross = lax.ppermute(cross, AXIS, [(b, cross_of(b)) for b in range(size)])]
    slice x1 -> x0, local copies, waits for them, and re-layouts: 0.96 us -> none  [body(): low = jnp.concatenate([x[:2], g[:2]], axis=0)]
    select_n x2 -> x0, other arithmetic: 0.73 us -> none  [the longest x1 0.7 us: body(): jnp.where(odd, mine, other)]
    pallas_call x4 -> x5, Pallas kernels: 9.82 us -> 10.2 us  [call(): pl.pallas_call(kernel, out_shape=outs, in_specs=specs or [VM] * len(opera...]
  transfers between devices with their start and end apart: 7 -> 7, of which waited for: 5 -> 5; matrix products, arithmetic and copies ran while one was open for 0% -> 0% of each run, Pallas kernels for 10% -> 18%
where the time goes in v2:
time: 34.9 us; the launch traced here: 34.5 us
  waiting for transfers between devices  13.9 us (40%)
  Pallas kernels  10.2 us (29%)
  starting transfers between devices  9.64 us (28%)
  between operations  0.71 us (2%)
    ppermute x5, waiting for transfers between devices, swap(): return lax.ppermute(value, AXIS, [(b, b ^ bit) for b in range(size)])  13.9 us
    pallas_call x5, Pallas kernels, call(): pl.pallas_call(kernel, out_shape=outs, in_specs=specs or [VM] * len(opera...  10.2 us
    ppermute x5, starting transfers between devices, swap(): return lax.ppermute(value, AXIS, [(b, b ^ bit) for b in range(size)])  6.89 us
    ppermute x1, starting transfers between devices, body(): cross = lax.ppermute(cross, AXIS, [(b, cross_of(b)) for b in range(size)])  2.62 us
  transfers between devices with their start and end apart: 7, of which 5 were waited for; matrix products, arithmetic and copies ran while one was open for 0% of the time, Pallas kernels for 18%

profile of v2, /device:TPU:1, one launch (start us, length us, event | category | flops | bytes accessed | tf_op | source)
XLA Modules:
  0.0 34.5 jit_solution(18044603641283182375)
XLA Ops:
  0.6 1.1 %pack.1 = (bf16[4,32,512]{2,1,0:T(8,128)(2,1)S(1)}, bf16[4,32,512]{2,1,0:T(8,128)(2,1)S(1)}, s32[2,8,128]{2,1,0:T(8,128)S(1)}, bf16[8,32,512]{2,1,0:T(8,128)(2,1...) custom-call(s32[1,2]{1,0:T(1,128)} %codes_ref.1, ...), custom_call_target="tpu_custom_call" | custom-call | tf_op jit(solution)/shard_map/pack/pallas_call | solution.py:336
  1.7 0.1 collective-permute-start
  1.9 2.6 %collective-permute-start.1 = (bf16[4,32,512]{2,1,0:T(8,128)(2,1)S(1)}, bf16[4,32,512]{2,1,0:T(8,128)(2,1)S(1)}, u32[]{:S(2)}, u32[]{:S(2)}) collective-permute-start(bf16[4,32,512]{2,1,0:T(8,128)(2,1)S(1)} %get-tuple-element.29), channel_id=1, source_target_pairs={{0,15},{1,2},{2,1},{3,4},{4,3},{5,6},{6,5},{7,8},{8,7},{9,10},{10,... | collective-permute-start | bytes 393224 | tf_op jit(solution)/shard_map/ppermute | solution.py:360
  4.5 4.2 %interior.1 = (bf16[288,288]{1,0:T(8,128)(2,1)S(1)}, bf16[288,288]{1,0:T(8,128)(2,1)S(1)}, bf16[288,288]{1,0:T(8,128)(2,1)S(1)}, bf16[2,512,512]{2,1,0:T(8,128)(...) custom-call(s32[2,8,128]{2,1,0:T(8,128)S(1)} %get-tuple-element.30.c, ...), custom_call_target="tpu_custom_call" | custom-call | tf_op jit(solution)/shard_map/interior/pallas_call | solution.py:336
  8.7 0.0 collective-permute-done.pair_ref
  8.7 0.0 collective-permute-done.1.cross_ref
  8.8 2.1 %edge.1 = (f32[32,864]{1,0:T(8,128)S(1)}, f32[32,864]{1,0:T(8,128)S(1)}, bf16[4,32,512]{2,1,0:T(8,128)(2,1)S(1)}) custom-call(bf16[4,32,512]{2,1,0:T(8,128)(2,1)S(1)} %collective-permute-done.pair_ref, bf16[4,32,512]{2,1,0:T(8,128)(2,1)S(1)} %collective-permute-done.1.cross_ref, bf16[288,288]{1,0:T(8,128)(2,1)S(1)} %get-tuple-element.35.ws_ref, ...), custom_call_target="tpu_custom_call" | custom-call | tf_op jit(solution)/shard_map/edge/pallas_call | solution.py:336
  10.8 3.5 %collective-permute-start.2 = (f32[32,864]{1,0:T(8,128)S(1)}, f32[32,864]{1,0:T(8,128)S(1)}, u32[]{:S(2)}, u32[]{:S(2)}) collective-permute-start(f32[32,864]{1,0:T(8,128)S(1)} %get-tuple-element.46), channel_id=1, source_target_pairs={{0,1},{1,0},{2,3},{3,2},{4,5},{5,4},{6,7},{7,6},{8,9},{9,8},{10,11... | collective-permute-start | bytes 331784 | tf_op jit(solution)/shard_map/ppermute | solution.py:374
  14.4 1.0 %collective-permute-done.2 = f32[32,864]{1,0:T(8,128)S(1)} collective-permute-done((f32[32,864]{1,0:T(8,128)S(1)}, f32[32,864]{1,0:T(8,128)S(1)}, u32[]{:S(2)}, u32[]{:S(2)}) %collective-permute-start.2) | collective-permute-done | bytes 110624 | tf_op jit(solution)/shard_map/ppermute | solution.py:374
  15.3 0.1 collective-permute-start.3
  15.4 1.9 %input_grad.1 = f32[8,32,512]{2,1,0:T(8,128)} custom-call(bf16[6,32,512]{2,1,0:T(8,128)(2,1)S(1)} %get-tuple-element.47.pi_ref, bf16[4,32,512]{2,1,0:T(8,128)(2,1)S(1)} %get-tuple-element.48.pe_ref, bf16[8,32,512]{2,1,0:T(8,128)(2,1)S(1)} %get-tuple-element.32.g_ref, bf16[288,288]{1,0:T(8,128)(2,1)S(1)} %get-tuple-element.35.ws_ref, ...), custom_call_target="tpu_custom_call" | custom-call | tf_op jit(solution)/shard_map/input_grad/pallas_call | solution.py:336
  17.3 2.5 %collective-permute-done.3 = f32[32,864]{1,0:T(8,128)S(1)} collective-permute-done((f32[32,864]{1,0:T(8,128)S(1)}, f32[32,864]{1,0:T(8,128)S(1)}, u32[]{:S(2)}, u32[]{:S(2)}) %collective-permute-start.3) | collective-permute-done | bytes 110624 | tf_op jit(solution)/shard_map/ppermute | solution.py:374
  19.8 0.1 collective-permute-start.4
  19.9 3.6 %collective-permute-done.4 = f32[32,864]{1,0:T(8,128)S(1)} collective-permute-done((f32[32,864]{1,0:T(8,128)S(1)}, f32[32,864]{1,0:T(8,128)S(1)}, u32[]{:S(2)}, u32[]{:S(2)}) %collective-permute-start.4) | collective-permute-done | bytes 110624 | tf_op jit(solution)/shard_map/ppermute | solution.py:374
  23.5 1.6 %collective-permute-start.5 = (f32[32,864]{1,0:T(8,128)S(1)}, f32[32,864]{1,0:T(8,128)S(1)}, u32[]{:S(2)}, u32[]{:S(2)}) collective-permute-start(f32[32,864]{1,0:T(8,128)S(1)} %add.14), channel_id=1, source_target_pairs={{0,8},{1,9},{2,10},{3,11},{4,12},{5,13},{6,14},{7,15},{8,0},{9,1},... | collective-permute-start | bytes 331784 | tf_op jit(solution)/shard_map/ppermute | solution.py:374
  25.1 5.8 %collective-permute-done.5 = f32[32,864]{1,0:T(8,128)S(1)} collective-permute-done((f32[32,864]{1,0:T(8,128)S(1)}, f32[32,864]{1,0:T(8,128)S(1)}, u32[]{:S(2)}, u32[]{:S(2)}) %collective-permute-start.5) | collective-permute-done | bytes 110624 | tf_op jit(solution)/shard_map/ppermute | solution.py:374
  30.9 1.6 %collective-permute-start.6 = (f32[32,864]{1,0:T(8,128)S(1)}, f32[32,864]{1,0:T(8,128)S(1)}, u32[]{:S(2)}, u32[]{:S(2)}) collective-permute-start(f32[32,864]{1,0:T(8,128)S(1)} %add.15.mine_ref), channel_id=1, source_target_pairs={{0,1},{1,0},{2,3},{3,2},{4,5},{5,4},{6,7},{7,6},{8,9},{9,8},{10,11... | collective-permute-start | bytes 331784 | tf_op jit(solution)/shard_map/ppermute | solution.py:374
  32.6 1.0 %collective-permute-done.6.other_ref = f32[32,864]{1,0:T(8,128)S(1)} collective-permute-done((f32[32,864]{1,0:T(8,128)S(1)}, f32[32,864]{1,0:T(8,128)S(1)}, u32[]{:S(2)}, u32[]{:S(2)}) %collective-permute-start.6) | collective-permute-done | bytes 110624 | tf_op jit(solution)/shard_map/ppermute | solution.py:374
  33.5 0.9 %normalize.1 = (f32[32,864]{1,0:T(8,128)}, f32[32,864]{1,0:T(8,128)}) custom-call(f32[32,864]{1,0:T(8,128)S(1)} %add.15.mine_ref, f32[32,864]{1,0:T(8,128)S(1)} %collective-permute-done.6.other_ref), custom_call_target="tpu_custom_call" | custom-call | tf_op jit(solution)/shard_map/normalize/pallas_call | solution.py:336
  (4 shorter events, 0.1 us)
Async XLA Ops:
  1.7 7.0 %collective-permute-start = (bf16[4,32,512]{2,1,0:T(8,128)(2,1)S(1)}, bf16[4,32,512]{2,1,0:T(8,128)(2,1)S(1)}, u32[]{:S(2)}, u32[]{:S(2)}) collective-permute-start(bf16[4,32,512]{2,1,0:T(8,128)(2,1)S(1)} %get-tuple-element.28), channel_id=1, source_target_pairs={{0,1},{1,0},{2,3},{3,2},{4,5},{5,4},{6,7},{7,6},{8,9},{9,8},{10,11... | collective-permute-start | bytes 393224 | tf_op jit(solution)/shard_map/ppermute | solution.py:361
  1.9 6.9 %collective-permute-start.1 = (bf16[4,32,512]{2,1,0:T(8,128)(2,1)S(1)}, bf16[4,32,512]{2,1,0:T(8,128)(2,1)S(1)}, u32[]{:S(2)}, u32[]{:S(2)}) collective-permute-start(bf16[4,32,512]{2,1,0:T(8,128)(2,1)S(1)} %get-tuple-element.29), channel_id=1, source_target_pairs={{0,15},{1,2},{2,1},{3,4},{4,3},{5,6},{6,5},{7,8},{8,7},{9,10},{10,... | collective-permute-start | bytes 393224 | tf_op jit(solution)/shard_map/ppermute | solution.py:360
  10.8 4.5 %collective-permute-start.2 = (f32[32,864]{1,0:T(8,128)S(1)}, f32[32,864]{1,0:T(8,128)S(1)}, u32[]{:S(2)}, u32[]{:S(2)}) collective-permute-start(f32[32,864]{1,0:T(8,128)S(1)} %get-tuple-element.46), channel_id=1, source_target_pairs={{0,1},{1,0},{2,3},{3,2},{4,5},{5,4},{6,7},{7,6},{8,9},{9,8},{10,11... | collective-permute-start | bytes 331784 | tf_op jit(solution)/shard_map/ppermute | solution.py:374
  15.3 4.4 %collective-permute-start.3 = (f32[32,864]{1,0:T(8,128)S(1)}, f32[32,864]{1,0:T(8,128)S(1)}, u32[]{:S(2)}, u32[]{:S(2)}) collective-permute-start(f32[32,864]{1,0:T(8,128)S(1)} %add.12), channel_id=1, source_target_pairs={{0,2},{1,3},{2,0},{3,1},{4,6},{5,7},{6,4},{7,5},{8,10},{9,11},{10,... | collective-permute-start | bytes 331784 | tf_op jit(solution)/shard_map/ppermute | solution.py:374
  19.8 3.7 %collective-permute-start.4 = (f32[32,864]{1,0:T(8,128)S(1)}, f32[32,864]{1,0:T(8,128)S(1)}, u32[]{:S(2)}, u32[]{:S(2)}) collective-permute-start(f32[32,864]{1,0:T(8,128)S(1)} %add.13), channel_id=1, source_target_pairs={{0,4},{1,5},{2,6},{3,7},{4,0},{5,1},{6,2},{7,3},{8,12},{9,13},{10,... | collective-permute-start | bytes 331784 | tf_op jit(solution)/shard_map/ppermute | solution.py:374
  23.5 7.4 %collective-permute-start.5 = (f32[32,864]{1,0:T(8,128)S(1)}, f32[32,864]{1,0:T(8,128)S(1)}, u32[]{:S(2)}, u32[]{:S(2)}) collective-permute-start(f32[32,864]{1,0:T(8,128)S(1)} %add.14), channel_id=1, source_target_pairs={{0,8},{1,9},{2,10},{3,11},{4,12},{5,13},{6,14},{7,15},{8,0},{9,1},... | collective-permute-start | bytes 331784 | tf_op jit(solution)/shard_map/ppermute | solution.py:374
  30.9 2.6 %collective-permute-start.6 = (f32[32,864]{1,0:T(8,128)S(1)}, f32[32,864]{1,0:T(8,128)S(1)}, u32[]{:S(2)}, u32[]{:S(2)}) collective-permute-start(f32[32,864]{1,0:T(8,128)S(1)} %add.15.mine_ref), channel_id=1, source_target_pairs={{0,1},{1,0},{2,3},{3,2},{4,5},{5,4},{6,7},{7,6},{8,9},{9,8},{10,11... | collective-permute-start | bytes 331784 | tf_op jit(solution)/shard_map/ppermute | solution.py:374

commit v3 on v2

--- a/solution.py
+++ b/solution.py
@@ -9,6 +9,7 @@
 AXIS = "blocks"
 F32 = jnp.float32
 BF16 = jnp.bfloat16
+ORDER = (0, 1, 2, 3, 5, 6, 7, 8, 4)
 VMEM_LIMIT = 24 * 1024 * 1024
 
 
@@ -36,14 +37,14 @@
 def im2col(plane, store, masks, vertical):
     cells = plane.shape[1]
     wide = plane.astype(F32)
-    for tap in range(9):
+    for place, tap in enumerate(ORDER):
         offset = (tap // 3 - 1) * vertical + (tap % 3 - 1)
         if offset == 0:
-            store(tap, plane)
+            store(place, plane)
             continue
         moved = pltpu.roll(wide, (-offset) % cells, 1)
         moved = jnp.where(masks[tap], moved, 0.0)
-        store(tap, moved.astype(BF16))
+        store(place, moved.astype(BF16))
 
 
 def dot(a, b):
@@ -54,22 +55,30 @@
     return lax.dot_general(a, b, (((1,), (1,)), ((), ())), preferred_element_type=F32)
 
 
-def flip_matrix(code, cells, vertical):
-    row = lax.broadcasted_iota(jnp.int32, (cells, cells), 0)
-    col = lax.broadcasted_iota(jnp.int32, (1, cells), 1)
-    bits = jnp.where(code % 2 == 1, cells - vertical, 0) + jnp.where(code // 2 == 1, vertical - 1, 0)
-    return jnp.where(row == (col ^ bits), 1.0, 0.0).astype(BF16)
+def flip_planes(planes, code, vertical):
+    lanes = 128
+    parts = planes.shape[1] // lanes
+    wide = planes.astype(F32)
+    turn_r = code % 2 == 1
+    bits = jnp.where(turn_r, lanes - vertical, 0) + jnp.where(code // 2 == 1, vertical - 1, 0)
+    index = lax.broadcasted_iota(jnp.int32, (planes.shape[0], lanes), 1) ^ bits
+    moved = [jnp.take_along_axis(wide[:, j * lanes:(j + 1) * lanes], index, axis=1) for j in range(parts)]
+    return jnp.concatenate(
+        [jnp.where(turn_r, moved[parts - 1 - j], moved[j]) for j in range(parts)], axis=1).astype(BF16)
 
 
 def tap_flip_matrix(code, channels):
     size = 9 * channels
     row = lax.broadcasted_iota(jnp.int32, (size, size), 0)
     col = lax.broadcasted_iota(jnp.int32, (1, size), 1)
-    tap = col // channels
+    place = col // channels
+    tap = jnp.where(place == 8, 4, jnp.where(place >= 4, place + 1, place))
     r, z = tap // 3, tap % 3
     r = jnp.where(code % 2 == 1, 2 - r, r)
     z = jnp.where(code // 2 == 1, 2 - z, z)
-    return jnp.where(row == (3 * r + z) * channels + col % channels, 1.0, 0.0).astype(BF16)
+    tap = 3 * r + z
+    place = jnp.where(tap == 4, 8, jnp.where(tap > 4, tap - 1, tap))
+    return jnp.where(row == place * channels + col % channels, 1.0, 0.0).astype(BF16)
 
 
 def activation(pre, grad):
@@ -89,14 +98,11 @@
     return fill
 
 
-def make_pack_kernel(count, channels, cells):
+def make_pack_kernel(count):
     def kernel(codes_ref, x_ref, g_ref, w1_ref, w2_ref,
                cross_ref, pair_ref, codes_out, x_out, g_out, w1_out, w2_out, scalars, sems):
-        copies = [
-            pltpu.make_async_copy(source, target, sems.at[index])
-            for index, (source, target) in enumerate(
-                ((x_ref, x_out), (g_ref, g_out), (w1_ref, w1_out), (w2_ref, w2_out), (codes_ref, scalars)))
-        ]
+        moves = ((x_ref, x_out), (g_ref, g_out), (codes_ref, scalars), (w1_ref, w1_out), (w2_ref, w2_out))
+        copies = [pltpu.make_async_copy(*move, sems.at[index]) for index, move in enumerate(moves)]
         for copy in copies:
             copy.start()
         is_odd = lax.axis_index(AXIS) % 2 == 1
@@ -115,26 +121,37 @@
 
 def make_interior_kernel(count, channels, cells, vertical):
     span = 9 * channels
+    most = 8 * channels
     wide = 3 * channels
     last = count - 1
 
     def kernel(codes_ref, x_ref, g_ref, w1_ref, w2_ref,
-               ws_ref, lo_ref, hi_ref, turn_ref, pe_ref, ge_ref, xs_ref, cs_ref, pg_ref, g1_ref, g2_ref,
+               ws_ref, lo_ref, hi_ref, t1_ref, t2_ref, pe_ref, ge_ref, xs_ref, cs_ref, pg_ref, g1_ref, g2_ref,
                h_ref, pr_ref):
         masks = tap_masks(cells, vertical)
         for step in range(3):
-            ws_ref[step * channels:(step + 1) * channels, :] = w1_ref[:, step * span:(step + 1) * span]
+            rows = slice(step * channels, (step + 1) * channels)
+            base = step * span
+            half = 4 * channels
+            ws_ref[rows, 0:half] = w1_ref[:, base:base + half]
+            ws_ref[rows, half:most] = w1_ref[:, base + half + channels:base + span]
+            ws_ref[rows, most:span] = w1_ref[:, base + half:base + half + channels]
         for weight_ref, base in ((w2_ref, wide), (w1_ref, 2 * wide)):
             turned = weight_ref[...].astype(F32).T
             for step in range(3):
-                for tap in range(9):
+                for place, tap in enumerate(ORDER):
                     at = (9 * (2 - step) + 8 - tap) * channels
-                    ws_ref[base + step * channels:base + (step + 1) * channels, tap * channels:(tap + 1) * channels] = (
-                        turned[at:at + channels, :].astype(BF16))
+                    ws_ref[base + step * channels:base + (step + 1) * channels,
+                           place * channels:(place + 1) * channels] = turned[at:at + channels, :].astype(BF16)
         lo_ref[...] = dot(ws_ref[...], tap_flip_matrix(codes_ref[0, 0:1, 0:1], channels)).astype(BF16)
         hi_ref[...] = dot(ws_ref[...], tap_flip_matrix(codes_ref[1, 0:1, 0:1], channels)).astype(BF16)
-        for side in range(2):
-            turn_ref[side, :, :] = flip_matrix(codes_ref[side, 0:1, 0:1], cells, vertical)
+        for ref, base in ((t1_ref, 0), (t2_ref, wide)):
+            ref[...] = jnp.zeros_like(ref)
+            for step in range(3):
+                centre = ws_ref[base + step * channels:base + (step + 1) * channels, most:span]
+                for a in range(count):
+                    row = (a + 2 - step) * channels
+                    ref[row:row + channels, a * channels:(a + 1) * channels] = centre
 
         fill_x = filler(xs_ref, channels, masks, vertical)
         fill_g = filler(cs_ref, channels, masks, vertical)
@@ -144,25 +161,25 @@
 
         h_ref[...] = jnp.zeros_like(h_ref)
         pr_ref[...] = jnp.zeros_like(pr_ref)
-        pre, grad = {}, {}
-
-        def add(table, key, value):
-            table[key] = value if key not in table else table[key] + value
+        pre_all = dot(t1_ref[...], x_ref[...].reshape(count * channels, cells))
+        grad_all = dot(t2_ref[...], g_ref[...].reshape(count * channels, cells))
+        pre = {a: pre_all[(a + 1) * channels:(a + 2) * channels] for a in range(-1, count + 1)}
+        grad = {a: grad_all[(a + 1) * channels:(a + 2) * channels] for a in range(-1, count + 1)}
 
         for a in range(count):
-            columns = slice(a * span, (a + 1) * span)
-            y = dot(ws_ref[0:wide, :], xs_ref[columns, :])
-            v = dot(ws_ref[wide:2 * wide, :], cs_ref[columns, :])
+            columns = slice(a * span, a * span + most)
+            y = dot(ws_ref[0:wide, 0:most], xs_ref[columns, :])
+            v = dot(ws_ref[wide:2 * wide, 0:most], cs_ref[columns, :])
             for step in range(3):
                 target = a + 1 - step
                 rows = slice(step * channels, (step + 1) * channels)
-                add(grad, target, v[rows])
+                grad[target] = grad[target] + v[rows]
                 if 0 <= target <= last:
-                    add(pre, target, y[rows])
+                    pre[target] = pre[target] + y[rows]
             if a == 0:
-                pre[-1] = dot(lo_ref[2 * channels:wide, :], xs_ref[columns, :])
+                pre[-1] = pre[-1] + dot(lo_ref[2 * channels:wide, 0:most], xs_ref[columns, :])
             if a == last:
-                pre[count] = dot(hi_ref[0:channels, :], xs_ref[columns, :])
+                pre[count] = pre[count] + dot(hi_ref[0:channels, 0:most], xs_ref[columns, :])
             done = a - 1
             if 1 <= done <= last - 1:
                 hidden, pg = activation(pre.pop(done), grad.pop(done))
@@ -179,27 +196,31 @@
             ge_ref[index, :, :] = grad.pop(plane)
 
         grad_one, grad_two = None, None
-        for a in range(count):
-            term = dot_nt(cs_ref[a * span:(a + 1) * span, :], h_ref[a * channels:(a + 3) * channels, :])
+        for a in range(0, count, 2):
+            pairs = slice(a * span, (a + 2) * span)
+            term = dot_nt(cs_ref[pairs, :], h_ref[a * channels:(a + 4) * channels, :])
             grad_two = term if grad_two is None else grad_two + term
-            start = (count - a) * channels
-            term = dot_nt(xs_ref[a * span:(a + 1) * span, :], pr_ref[start:start + wide, :])
+            start = (count - 1 - a) * channels
+            term = dot_nt(xs_ref[pairs, :], pr_ref[start:start + 4 * channels, :])
             grad_one = term if grad_one is None else grad_one + term
         g2_ref[...] = grad_two
         turned = grad_one.T
         for step in range(3):
-            g1_ref[:, step * span:(step + 1) * span] = turned[step * channels:(step + 1) * channels]
+            first, second = (step + 1) * channels, step * channels
+            g1_ref[:, step * span:(step + 1) * span] = (
+                turned[first:first + channels, 0:span] + turned[second:second + channels, span:])
 
     return kernel
 
 
 def make_edge_kernel(count, channels, cells, vertical):
     span = 9 * channels
+    most = 8 * channels
     wide = 3 * channels
     last = count - 1
 
-    def kernel(pair_ref, cross_ref, ws_ref, lo_ref, hi_ref, turn_ref, pe_ref, ge_ref, xs_ref, cs_ref, g1_ref, g2_ref,
-               keep_ref, send_ref, pg_ref, xh_ref, ch_ref):
+    def kernel(cross_ref, pair_ref, ws_ref, lo_ref, hi_ref, t1_ref, t2_ref, codes_ref, pe_ref, ge_ref, xs_ref, cs_ref,
+               g1_ref, g2_ref, keep_ref, send_ref, pg_ref, xh_ref, ch_ref):
         odd = lax.axis_index(AXIS) % 2
         is_odd = odd == 1
         masks = tap_masks(cells, vertical)
@@ -207,31 +228,37 @@
         fill_c = filler(ch_ref, channels, masks, vertical)
         pair = pair_ref[...].reshape(4 * channels, cells)
         cross = cross_ref[...].reshape(4 * channels, cells)
+        centres = []
         for side in range(2):
             planes = jnp.where(is_odd, pair, cross) if side == 0 else jnp.where(is_odd, cross, pair)
-            planes = dot(planes, turn_ref[side]).astype(BF16)
+            planes = flip_planes(planes, codes_ref[side, 0:1, 0:1], vertical)
             for index in range(2):
                 fill_x(2 * side + index, planes[index * channels:(index + 1) * channels])
                 fill_c(2 * side + index, planes[(index + 2) * channels:(index + 3) * channels])
-
-        def halo(ref, index):
-            return ref[index * span:(index + 1) * span, :]
+            top = 2 * channels if side == 0 else 0
+            for index, ref in enumerate((t1_ref, t2_ref)):
+                centres.append(dot(ref[top:top + 2 * channels, 0:2 * channels],
+                                   planes[2 * index * channels:2 * (index + 1) * channels]))
+
+        def halo(ref, index, end=most):
+            return ref[index * span:index * span + end, :]
 
         def rows(ref, part, first, end):
-            return ref[part * wide + first * channels:part * wide + end * channels, :]
-
-        near = dot(jnp.concatenate([rows(ws_ref, 0, 0, 1), rows(lo_ref, 0, 1, 2)], axis=0), halo(xh_ref, 1))
-        pre_m = pe_ref[0] + near[channels:] + dot(rows(lo_ref, 0, 0, 1), halo(xh_ref, 0))
-        pre_0 = pe_ref[1] + near[:channels]
+            return ref[part * wide + first * channels:part * wide + end * channels, 0:most]
+
+        x_low, g_low, x_high, g_high = centres
+        near = dot(jnp.concatenate([rows(lo_ref, 0, 1, 2), rows(ws_ref, 0, 0, 1)], axis=0), halo(xh_ref, 1)) + x_low
+        pre_m = pe_ref[0] + near[:channels] + dot(rows(lo_ref, 0, 0, 1), halo(xh_ref, 0))
+        pre_0 = pe_ref[1] + near[channels:]
         near = dot(rows(lo_ref, 1, 0, 2), halo(ch_ref, 1))
-        grad_m = ge_ref[0] + near[channels:] + dot(rows(lo_ref, 1, 0, 1), halo(ch_ref, 0))
-        grad_0 = ge_ref[1] + near[:channels]
-        near = dot(jnp.concatenate([rows(hi_ref, 0, 1, 2), rows(ws_ref, 0, 2, 3)], axis=0), halo(xh_ref, 2))
-        pre_p = pe_ref[3] + near[:channels] + dot(rows(hi_ref, 0, 2, 3), halo(xh_ref, 3))
-        pre_7 = pe_ref[2] + near[channels:]
+        grad_m = ge_ref[0] + near[channels:] + g_low[:channels] + dot(rows(lo_ref, 1, 0, 1), halo(ch_ref, 0))
+        grad_0 = ge_ref[1] + near[:channels] + g_low[channels:]
+        near = dot(jnp.concatenate([rows(ws_ref, 0, 2, 3), rows(hi_ref, 0, 1, 2)], axis=0), halo(xh_ref, 2)) + x_high
+        pre_p = pe_ref[3] + near[channels:] + dot(rows(hi_ref, 0, 2, 3), halo(xh_ref, 3))
+        pre_7 = pe_ref[2] + near[:channels]
         near = dot(rows(hi_ref, 1, 1, 3), halo(ch_ref, 2))
-        grad_p = ge_ref[3] + near[:channels] + dot(rows(hi_ref, 1, 2, 3), halo(ch_ref, 3))
-        grad_7 = ge_ref[2] + near[channels:]
+        grad_p = ge_ref[3] + near[:channels] + g_high[channels:] + dot(rows(hi_ref, 1, 2, 3), halo(ch_ref, 3))
+        grad_7 = ge_ref[2] + near[channels:] + g_high[:channels]
 
         hid_m, pg_m = activation(pre_m, grad_m)
         hid_0, pg_0 = activation(pre_0, grad_0)
@@ -240,15 +267,14 @@
         for index, pg in enumerate((pg_m, pg_0, pg_7, pg_p)):
             pg_ref[index, :, :] = pg
 
-        zero = jnp.zeros((channels, cells), BF16)
+        zero = jnp.zeros((2 * channels, cells), BF16)
         grad_two = g2_ref[...]
-        for a, stack in ((0, (hid_m, hid_0, zero)), (1, (hid_0, zero, zero)),
-                         (last - 1, (zero, zero, hid_7)), (last, (zero, hid_7, hid_p))):
-            grad_two = grad_two + dot_nt(cs_ref[a * span:(a + 1) * span, :], jnp.concatenate(stack, axis=0))
-        low_end = dot_nt(pg_0, halo(xh_ref, 1))
+        for a, stack in ((0, (hid_m, hid_0, zero)), (last - 1, (zero, hid_7, hid_p))):
+            grad_two = grad_two + dot_nt(cs_ref[a * span:(a + 2) * span, :], jnp.concatenate(stack, axis=0))
+        low_end = dot_nt(pg_0, halo(xh_ref, 1, span))
         low_own = dot_nt(pg_0, xs_ref[0:2 * span, :])
         high_own = dot_nt(pg_7, xs_ref[(last - 1) * span:(last + 1) * span, :])
-        high_end = dot_nt(pg_7, halo(xh_ref, 2))
+        high_end = dot_nt(pg_7, halo(xh_ref, 2, span))
 
         def put(ref, one):
             if one:
@@ -257,10 +283,12 @@
                 ref[:, 2 * span:] = g1_ref[:, 2 * span:] + low_own[:, span:] + high_end
             else:
                 for step in range(3):
-                    for tap in range(9):
-                        at = (9 * step + tap) * channels
-                        ref[:, at:at + channels] = grad_two[
-                            (8 - tap) * channels:(9 - tap) * channels, step * channels:(step + 1) * channels]
+                    for place, tap in enumerate(ORDER):
+                        at = (9 * step + 8 - tap) * channels
+                        top = place * channels
+                        ref[:, at:at + channels] = (
+                            grad_two[top:top + channels, step * channels:(step + 1) * channels]
+                            + grad_two[span + top:span + top + channels, (step + 1) * channels:(step + 2) * channels])
 
         @pl.when(odd == 0)
         def _():
@@ -305,19 +333,28 @@
 
 def normalize_kernel(mine_ref, other_ref, one_ref, two_ref):
     odd = lax.axis_index(AXIS) % 2
+    span = mine_ref.shape[1] // 3
+    part = span // 9
 
     def scaled(ref):
         v = ref[...]
         return v / jnp.sqrt(jnp.mean(v * v) + 1e-06)
 
+    def put(ref, value):
+        for step in range(3):
+            base = step * span
+            ref[:, base:base + 4 * part] = value[:, base:base + 4 * part]
+            ref[:, base + 4 * part:base + 5 * part] = value[:, base + 8 * part:base + span]
+            ref[:, base + 5 * part:base + span] = value[:, base + 4 * part:base + 8 * part]
+
     @pl.when(odd == 0)
     def _():
-        one_ref[...] = scaled(mine_ref)
+        put(one_ref, scaled(mine_ref))
         two_ref[...] = scaled(other_ref)
 
     @pl.when(odd == 1)
     def _():
-        one_ref[...] = scaled(other_ref)
+        put(one_ref, scaled(other_ref))
         two_ref[...] = scaled(mine_ref)
 
 
@@ -343,31 +380,33 @@
     shape = jax.ShapeDtypeStruct
     sizes = (count, channels, cells, vertical)
     stack = shape((span, span), BF16)
+    band = shape(((count + 2) * channels, count * channels), BF16)
     edges = shape((4, channels, cells), F32)
     columns = shape((count * span, cells), BF16)
     grads = shape((channels, 27 * channels), F32)
     half = shape((4, channels, cells), BF16)
+    weight = shape(first_weight.shape, BF16)
+    pinned = [
+        pltpu.with_memory_space_constraint(v, pltpu.HBM) for v in (face_codes, x, g, first_weight, second_weight)]
     cross, pair, codes, x, g, first_weight, second_weight = call(
-        make_pack_kernel(count, channels, cells),
-        (half, half, shape((2, 8, 128), jnp.int32), shape(x.shape, BF16), shape(x.shape, BF16),
-         shape(first_weight.shape, BF16), shape(first_weight.shape, BF16)),
-        tuple(pltpu.with_memory_space_constraint(v, pltpu.HBM) for v in (face_codes, x, g, first_weight, second_weight)),
-        "pack", [pltpu.SMEM((1, 2), jnp.int32), pltpu.SemaphoreType.DMA((5,))], [HB] * 5)
+        make_pack_kernel(count),
+        (half, half, shape((2, 8, 128), jnp.int32), shape(x.shape, BF16), shape(x.shape, BF16), weight, weight),
+        pinned, "pack", [pltpu.SMEM((1, 2), jnp.int32), pltpu.SemaphoreType.DMA((5,))], [HB] * 5)
 
     def cross_of(b):
         return (b + 1) % size if b % 2 == 1 else (b - 1) % size
 
+    pair = lax.ppermute(pair, AXIS, [(b, b ^ 1) for b in range(size)])
     cross = lax.ppermute(cross, AXIS, [(b, cross_of(b)) for b in range(size)])
-    pair = lax.ppermute(pair, AXIS, [(b, b ^ 1) for b in range(size)])
-    ws, lo, hi, turn, pre_edge, grad_edge, xs, cs, pg_inner, part_one, part_two = call(
+    ws, lo, hi, band_one, band_two, pre_edge, grad_edge, xs, cs, pg_inner, part_one, part_two = call(
         make_interior_kernel(*sizes),
-        (stack, stack, stack, shape((2, cells, cells), BF16), edges, edges, columns, columns,
-         shape((count - 2, channels, cells), BF16), grads, shape((span, 3 * channels), F32)),
+        (stack, stack, stack, band, band, edges, edges, columns, columns,
+         shape((count - 2, channels, cells), BF16), grads, shape((2 * span, 4 * channels), F32)),
         (codes, x, g, first_weight, second_weight), "interior",
         [pltpu.VMEM(((count + 2) * channels, cells), BF16), pltpu.VMEM(((count + 3) * channels, cells), BF16)])
     keep, send, pg_edge = call(
         make_edge_kernel(*sizes), (grads, grads, shape((4, channels, cells), BF16)),
-        (pair, cross, ws, lo, hi, turn, pre_edge, grad_edge, xs, cs, part_one, part_two), "edge",
+        (cross, pair, ws, lo, hi, band_one, band_two, codes, pre_edge, grad_edge, xs, cs, part_one, part_two), "edge",
         [pltpu.VMEM((4 * span, cells), BF16), pltpu.VMEM((4 * span, cells), BF16)])
 
     def swap(value, bit):

time: 34.9 us -> 34.4 us (0.986)
  starting transfers between devices: 9.64 us -> 8.65 us
  waiting for transfers between devices: 13.9 us -> 14.8 us
  Pallas kernels: 10.2 us -> 9.74 us
    ppermute x5, starting transfers between devices: 6.89 us -> 3.11 us  [swap(): return lax.ppermute(value, AXIS, [(b, b ^ bit) for b in range(size)])]
    ppermute x1, starting transfers between devices: 0.12 us -> 2.87 us  [body(): pair = lax.ppermute(pair, AXIS, [(b, b ^ 1) for b in range(size)])]
    ppermute x5, waiting for transfers between devices: 13.9 us -> 14.8 us  [swap(): return lax.ppermute(value, AXIS, [(b, b ^ bit) for b in range(size)])]
    pallas_call x5, Pallas kernels: 10.2 us -> 9.74 us  [call(): pl.pallas_call(kernel, out_shape=outs, in_specs=specs or [VM] * len(opera...]
  transfers between devices with their start and end apart: 7 -> 7, of which waited for: 5 -> 5; matrix products, arithmetic and copies ran while one was open for 0% -> 0% of each run, Pallas kernels for 18% -> 17%
where the time goes in v3:
time: 34.4 us; the launch traced here: 33.9 us
  waiting for transfers between devices  14.8 us (43%)
  Pallas kernels  9.74 us (28%)
  starting transfers between devices  8.65 us (25%)
  between operations  0.71 us (2%)
    ppermute x5, waiting for transfers between devices, swap(): return lax.ppermute(value, AXIS, [(b, b ^ bit) for b in range(size)])  14.8 us
    pallas_call x5, Pallas kernels, call(): pl.pallas_call(kernel, out_shape=outs, in_specs=specs or [VM] * len(opera...  9.74 us
    ppermute x5, starting transfers between devices, swap(): return lax.ppermute(value, AXIS, [(b, b ^ bit) for b in range(size)])  3.11 us
    ppermute x1, starting transfers between devices, body(): pair = lax.ppermute(pair, AXIS, [(b, b ^ 1) for b in range(size)])  2.87 us
    ppermute x1, starting transfers between devices, body(): cross = lax.ppermute(cross, AXIS, [(b, cross_of(b)) for b in range(size)])  2.67 us
  transfers between devices with their start and end apart: 7, of which 5 were waited for; matrix products, arithmetic and copies ran while one was open for 0% of the time, Pallas kernels for 17%

profile of v3, /device:TPU:1, one launch (start us, length us, event | category | flops | bytes accessed | tf_op | source)
XLA Modules:
  0.0 33.9 jit_solution(13848945640673618429)
XLA Ops:
  0.6 1.1 %pack.1 = (bf16[4,32,512]{2,1,0:T(8,128)(2,1)S(1)}, bf16[4,32,512]{2,1,0:T(8,128)(2,1)S(1)}, s32[2,8,128]{2,1,0:T(8,128)S(1)}, bf16[8,32,512]{2,1,0:T(8,128)(2,1...) custom-call(s32[1,2]{1,0:T(1,128)} %codes_ref.1, ...), custom_call_target="tpu_custom_call" | custom-call | tf_op jit(solution)/shard_map/pack/pallas_call | solution.py:373
  1.7 2.7 %collective-permute-start = (bf16[4,32,512]{2,1,0:T(8,128)(2,1)S(1)}, bf16[4,32,512]{2,1,0:T(8,128)(2,1)S(1)}, u32[]{:S(2)}, u32[]{:S(2)}) collective-permute-start(bf16[4,32,512]{2,1,0:T(8,128)(2,1)S(1)} %get-tuple-element.29), channel_id=1, source_target_pairs={{0,15},{1,2},{2,1},{3,4},{4,3},{5,6},{6,5},{7,8},{8,7},{9,10},{10,... | collective-permute-start | bytes 393224 | tf_op jit(solution)/shard_map/ppermute | solution.py:400
  4.4 2.9 %collective-permute-start.1 = (bf16[4,32,512]{2,1,0:T(8,128)(2,1)S(1)}, bf16[4,32,512]{2,1,0:T(8,128)(2,1)S(1)}, u32[]{:S(2)}, u32[]{:S(2)}) collective-permute-start(bf16[4,32,512]{2,1,0:T(8,128)(2,1)S(1)} %get-tuple-element.30), channel_id=1, source_target_pairs={{0,1},{1,0},{2,3},{3,2},{4,5},{5,4},{6,7},{7,6},{8,9},{9,8},{10,11... | collective-permute-start | bytes 393224 | tf_op jit(solution)/shard_map/ppermute | solution.py:399
  7.3 3.8 %interior.1 = (bf16[288,288]{1,0:T(8,128)(2,1)S(1)}, bf16[288,288]{1,0:T(8,128)(2,1)S(1)}, bf16[288,288]{1,0:T(8,128)(2,1)S(1)}, bf16[320,256]{1,0:T(8,128)(2,1)...) custom-call(s32[2,8,128]{2,1,0:T(8,128)S(1)} %get-tuple-element.31.c, ...), custom_call_target="tpu_custom_call" | custom-call | tf_op jit(solution)/shard_map/interior/pallas_call | solution.py:373
  11.1 0.0 collective-permute-done.cross_ref
  11.1 0.0 collective-permute-done.1.pair_ref
  11.2 1.9 %edge.1 = (f32[32,864]{1,0:T(8,128)S(1)}, f32[32,864]{1,0:T(8,128)S(1)}, bf16[4,32,512]{2,1,0:T(8,128)(2,1)S(1)}) custom-call(bf16[4,32,512]{2,1,0:T(8,128)(2,1)S(1)} %collective-permute-done.cross_ref, bf16[4,32,512]{2,1,0:T(8,128)(2,1)S(1)} %collective-permute-done.1.pair_ref, bf16[288,288]{1,0:T(8,128)(2,1)S(1)} %get-tuple-element.36.ws_ref, ...), custom_call_target="tpu_custom_call" | custom-call | tf_op jit(solution)/shard_map/edge/pallas_call | solution.py:373
  13.1 0.1 collective-permute-start.2
  13.2 1.3 %collective-permute-done.2 = f32[32,864]{1,0:T(8,128)S(1)} collective-permute-done((f32[32,864]{1,0:T(8,128)S(1)}, f32[32,864]{1,0:T(8,128)S(1)}, u32[]{:S(2)}, u32[]{:S(2)}) %collective-permute-start.2) | collective-permute-done | bytes 110624 | tf_op jit(solution)/shard_map/ppermute | solution.py:413
  14.5 0.1 collective-permute-start.3
  14.6 1.9 %input_grad.1 = f32[8,32,512]{2,1,0:T(8,128)} custom-call(bf16[6,32,512]{2,1,0:T(8,128)(2,1)S(1)} %get-tuple-element.49.pi_ref, bf16[4,32,512]{2,1,0:T(8,128)(2,1)S(1)} %get-tuple-element.50.pe_ref, bf16[8,32,512]{2,1,0:T(8,128)(2,1)S(1)} %get-tuple-element.33.g_ref, bf16[288,288]{1,0:T(8,128)(2,1)S(1)} %get-tuple-element.36.ws_ref, ...), custom_call_target="tpu_custom_call" | custom-call | tf_op jit(solution)/shard_map/input_grad/pallas_call | solution.py:373
  16.5 2.7 %collective-permute-done.3 = f32[32,864]{1,0:T(8,128)S(1)} collective-permute-done((f32[32,864]{1,0:T(8,128)S(1)}, f32[32,864]{1,0:T(8,128)S(1)}, u32[]{:S(2)}, u32[]{:S(2)}) %collective-permute-start.3) | collective-permute-done | bytes 110624 | tf_op jit(solution)/shard_map/ppermute | solution.py:413
  19.2 0.1 collective-permute-start.4
  19.3 3.6 %collective-permute-done.4 = f32[32,864]{1,0:T(8,128)S(1)} collective-permute-done((f32[32,864]{1,0:T(8,128)S(1)}, f32[32,864]{1,0:T(8,128)S(1)}, u32[]{:S(2)}, u32[]{:S(2)}) %collective-permute-start.4) | collective-permute-done | bytes 110624 | tf_op jit(solution)/shard_map/ppermute | solution.py:413
  22.9 1.4 %collective-permute-start.5 = (f32[32,864]{1,0:T(8,128)S(1)}, f32[32,864]{1,0:T(8,128)S(1)}, u32[]{:S(2)}, u32[]{:S(2)}) collective-permute-start(f32[32,864]{1,0:T(8,128)S(1)} %add.14), channel_id=1, source_target_pairs={{0,8},{1,9},{2,10},{3,11},{4,12},{5,13},{6,14},{7,15},{8,0},{9,1},... | collective-permute-start | bytes 331784 | tf_op jit(solution)/shard_map/ppermute | solution.py:413
  24.3 6.2 %collective-permute-done.5 = f32[32,864]{1,0:T(8,128)S(1)} collective-permute-done((f32[32,864]{1,0:T(8,128)S(1)}, f32[32,864]{1,0:T(8,128)S(1)}, u32[]{:S(2)}, u32[]{:S(2)}) %collective-permute-start.5) | collective-permute-done | bytes 110624 | tf_op jit(solution)/shard_map/ppermute | solution.py:413
  30.5 1.5 %collective-permute-start.6 = (f32[32,864]{1,0:T(8,128)S(1)}, f32[32,864]{1,0:T(8,128)S(1)}, u32[]{:S(2)}, u32[]{:S(2)}) collective-permute-start(f32[32,864]{1,0:T(8,128)S(1)} %add.15.mine_ref), channel_id=1, source_target_pairs={{0,1},{1,0},{2,3},{3,2},{4,5},{5,4},{6,7},{7,6},{8,9},{9,8},{10,11... | collective-permute-start | bytes 331784 | tf_op jit(solution)/shard_map/ppermute | solution.py:413
  32.0 1.0 %collective-permute-done.6.other_ref = f32[32,864]{1,0:T(8,128)S(1)} collective-permute-done((f32[32,864]{1,0:T(8,128)S(1)}, f32[32,864]{1,0:T(8,128)S(1)}, u32[]{:S(2)}, u32[]{:S(2)}) %collective-permute-start.6) | collective-permute-done | bytes 110624 | tf_op jit(solution)/shard_map/ppermute | solution.py:413
  33.0 1.0 %normalize.1 = (f32[32,864]{1,0:T(8,128)}, f32[32,864]{1,0:T(8,128)}) custom-call(f32[32,864]{1,0:T(8,128)S(1)} %add.15.mine_ref, f32[32,864]{1,0:T(8,128)S(1)} %collective-permute-done.6.other_ref), custom_call_target="tpu_custom_call" | custom-call | tf_op jit(solution)/shard_map/normalize/pallas_call | solution.py:373
  (4 shorter events, 0.1 us)
Async XLA Ops:
  1.7 9.4 %collective-permute-start = (bf16[4,32,512]{2,1,0:T(8,128)(2,1)S(1)}, bf16[4,32,512]{2,1,0:T(8,128)(2,1)S(1)}, u32[]{:S(2)}, u32[]{:S(2)}) collective-permute-start(bf16[4,32,512]{2,1,0:T(8,128)(2,1)S(1)} %get-tuple-element.29), channel_id=1, source_target_pairs={{0,15},{1,2},{2,1},{3,4},{4,3},{5,6},{6,5},{7,8},{8,7},{9,10},{10,... | collective-permute-start | bytes 393224 | tf_op jit(solution)/shard_map/ppermute | solution.py:400
  4.4 6.7 %collective-permute-start.1 = (bf16[4,32,512]{2,1,0:T(8,128)(2,1)S(1)}, bf16[4,32,512]{2,1,0:T(8,128)(2,1)S(1)}, u32[]{:S(2)}, u32[]{:S(2)}) collective-permute-start(bf16[4,32,512]{2,1,0:T(8,128)(2,1)S(1)} %get-tuple-element.30), channel_id=1, source_target_pairs={{0,1},{1,0},{2,3},{3,2},{4,5},{5,4},{6,7},{7,6},{8,9},{9,8},{10,11... | collective-permute-start | bytes 393224 | tf_op jit(solution)/shard_map/ppermute | solution.py:399
  13.1 1.4 %collective-permute-start.2 = (f32[32,864]{1,0:T(8,128)S(1)}, f32[32,864]{1,0:T(8,128)S(1)}, u32[]{:S(2)}, u32[]{:S(2)}) collective-permute-start(f32[32,864]{1,0:T(8,128)S(1)} %get-tuple-element.48), channel_id=1, source_target_pairs={{0,1},{1,0},{2,3},{3,2},{4,5},{5,4},{6,7},{7,6},{8,9},{9,8},{10,11... | collective-permute-start | bytes 331784 | tf_op jit(solution)/shard_map/ppermute | solution.py:413
  14.5 4.7 %collective-permute-start.3 = (f32[32,864]{1,0:T(8,128)S(1)}, f32[32,864]{1,0:T(8,128)S(1)}, u32[]{:S(2)}, u32[]{:S(2)}) collective-permute-start(f32[32,864]{1,0:T(8,128)S(1)} %add.12), channel_id=1, source_target_pairs={{0,2},{1,3},{2,0},{3,1},{4,6},{5,7},{6,4},{7,5},{8,10},{9,11},{10,... | collective-permute-start | bytes 331784 | tf_op jit(solution)/shard_map/ppermute | solution.py:413
  19.2 3.7 %collective-permute-start.4 = (f32[32,864]{1,0:T(8,128)S(1)}, f32[32,864]{1,0:T(8,128)S(1)}, u32[]{:S(2)}, u32[]{:S(2)}) collective-permute-start(f32[32,864]{1,0:T(8,128)S(1)} %add.13), channel_id=1, source_target_pairs={{0,4},{1,5},{2,6},{3,7},{4,0},{5,1},{6,2},{7,3},{8,12},{9,13},{10,... | collective-permute-start | bytes 331784 | tf_op jit(solution)/shard_map/ppermute | solution.py:413
  22.9 7.6 %collective-permute-start.5 = (f32[32,864]{1,0:T(8,128)S(1)}, f32[32,864]{1,0:T(8,128)S(1)}, u32[]{:S(2)}, u32[]{:S(2)}) collective-permute-start(f32[32,864]{1,0:T(8,128)S(1)} %add.14), channel_id=1, source_target_pairs={{0,8},{1,9},{2,10},{3,11},{4,12},{5,13},{6,14},{7,15},{8,0},{9,1},... | collective-permute-start | bytes 331784 | tf_op jit(solution)/shard_map/ppermute | solution.py:413
  30.5 2.5 %collective-permute-start.6 = (f32[32,864]{1,0:T(8,128)S(1)}, f32[32,864]{1,0:T(8,128)S(1)}, u32[]{:S(2)}, u32[]{:S(2)}) collective-permute-start(f32[32,864]{1,0:T(8,128)S(1)} %add.15.mine_ref), channel_id=1, source_target_pairs={{0,1},{1,0},{2,3},{3,2},{4,5},{5,4},{6,7},{7,6},{8,9},{9,8},{10,11... | collective-permute-start | bytes 331784 | tf_op jit(solution)/shard_map/ppermute | solution.py:413

commit v4 on v3

v4 whole, which is shorter than its diff:
```python
import jax
import jax.numpy as jnp
from jax import lax
from jax.experimental import pallas as pl
from jax.experimental.pallas import tpu as pltpu
from jax.sharding import PartitionSpec as P

R_CELLS = 32
AXIS = "blocks"
F32 = jnp.float32
BF16 = jnp.bfloat16
ORDER = (0, 1, 2, 3, 5, 6, 7, 8, 4)
VMEM_LIMIT = 24 * 1024 * 1024


def tap_masks(cells, vertical):
    lane = lax.broadcasted_iota(jnp.int32, (1, cells), 1)
    z = lane % vertical
    r = lane // vertical
    radial = cells // vertical
    masks = []
    for step_r in range(3):
        for step_z in range(3):
            ok = None
            if step_r == 0:
                ok = r >= 1
            if step_r == 2:
                ok = r < radial - 1
            if step_z == 0:
                ok = (z >= 1) if ok is None else ok & (z >= 1)
            if step_z == 2:
                ok = (z < vertical - 1) if ok is None else ok & (z < vertical - 1)
            masks.append(ok)
    return masks


def im2col(plane, store, masks, vertical):
    cells = plane.shape[1]
    wide = plane.astype(F32)
    for place, tap in enumerate(ORDER):
        offset = (tap // 3 - 1) * vertical + (tap % 3 - 1)
        if offset == 0:
            store(place, plane)
            continue
        moved = pltpu.roll(wide, (-offset) % cells, 1)
        moved = jnp.where(masks[tap], moved, 0.0)
        store(place, moved.astype(BF16))


def dot(a, b):
    return jnp.dot(a, b, preferred_element_type=F32)


def dot_nt(a, b):
    return lax.dot_general(a, b, (((1,), (1,)), ((), ())), preferred_element_type=F32)


def flip_planes(planes, code, vertical):
    lanes = 128
    parts = planes.shape[1] // lanes
    wide = planes.astype(F32)
    turn_r = code % 2 == 1
    bits = jnp.where(turn_r, lanes - vertical, 0) + jnp.where(code // 2 == 1, vertical - 1, 0)
    index = lax.broadcasted_iota(jnp.int32, (planes.shape[0], lanes), 1) ^ bits
    moved = [jnp.take_along_axis(wide[:, j * lanes:(j + 1) * lanes], index, axis=1) for j in range(parts)]
    return jnp.concatenate(
        [jnp.where(turn_r, moved[parts - 1 - j], moved[j]) for j in range(parts)], axis=1).astype(BF16)


def flipped_places(code):
    flip_r, flip_z = code % 2, code // 2
    places = []
    for tap in ORDER:
        r, z = tap // 3, tap % 3
        moved = 3 * (r + (2 - 2 * r) * flip_r) + z + (2 - 2 * z) * flip_z
        places.append(8 if tap == 4 else moved - (moved > 4).astype(jnp.int32))
    return places


def activation(pre, grad):
    sig = jax.nn.sigmoid(pre)
    hidden = (pre * sig).astype(BF16)
    return hidden, (grad * sig * (1.0 + pre * (1.0 - sig))).astype(BF16)


def filler(ref, channels, masks, vertical):
    def fill(position, plane, places=None, also=None):
        def store(place, value):
            if places is None:
                start = (9 * position + place) * channels
            else:
                start = pl.multiple_of((9 * position + places[place]) * channels, channels)
            ref[pl.ds(start, channels), :] = value
            if also is not None:
                also[place * channels:(place + 1) * channels, :] = value

        im2col(plane, store, masks, vertical)

    return fill


def make_pack_kernel(count):
    def kernel(codes_ref, x_ref, g_ref, w1_ref, w2_ref, up_ref, codes_out, x_out, g_out, w1_out, w2_out, scalars, sems):
        moves = ((x_ref, x_out), (g_ref, g_out), (codes_ref, scalars), (w1_ref, w1_out), (w2_ref, w2_out))
        copies = [pltpu.make_async_copy(*move, sems.at[index]) for index, move in enumerate(moves)]
        for copy in copies:
            copy.start()
        for index, field in enumerate((x_out, g_out)):
            copies[index].wait()
            up_ref[2 * index:2 * index + 2, :, :] = field[count - 2:count]
        for copy in copies[2:]:
            copy.wait()
        for side in range(2):
            codes_out[side, :, :] = jnp.full((8, 128), scalars[0, side], jnp.int32)

    return kernel


def make_interior_kernel(count, channels, cells, vertical):
    span = 9 * channels
    most = 8 * channels
    wide = 3 * channels
    last = count - 1

    def kernel(x_ref, g_ref, w1_ref, w2_ref,
               ws_ref, t1_ref, t2_ref, pe_ref, ge_ref, xs_ref, cs_ref, pg_ref, g1_ref, g2_ref,
               h_ref, pr_ref):
        masks = tap_masks(cells, vertical)
        for step in range(3):
            rows = slice(step * channels, (step + 1) * channels)
            base = step * span
            half = 4 * channels
            ws_ref[rows, 0:half] = w1_ref[:, base:base + half]
            ws_ref[rows, half:most] = w1_ref[:, base + half + channels:base + span]
            ws_ref[rows, most:span] = w1_ref[:, base + half:base + half + channels]
        for weight_ref, base in ((w2_ref, wide), (w1_ref, 2 * wide)):
            turned = weight_ref[...].astype(F32).T
            for step in range(3):
                for place, tap in enumerate(ORDER):
                    at = (9 * (2 - step) + 8 - tap) * channels
                    ws_ref[base + step * channels:base + (step + 1) * channels,
                           place * channels:(place + 1) * channels] = turned[at:at + channels, :].astype(BF16)
        for ref, base in ((t1_ref, 0), (t2_ref, wide)):
            ref[...] = jnp.zeros_like(ref)
            for step in range(3):
                centre = ws_ref[base + step * channels:base + (step + 1) * channels, most:span]
                for a in range(count):
                    row = (a + 2 - step) * channels
                    ref[row:row + channels, a * channels:(a + 1) * channels] = centre

        fill_x = filler(xs_ref, channels, masks, vertical)
        fill_g = filler(cs_ref, channels, masks, vertical)
        for a in range(count):
            fill_x(a, x_ref[a])
            fill_g(a, g_ref[a])

        h_ref[...] = jnp.zeros_like(h_ref)
        pr_ref[...] = jnp.zeros_like(pr_ref)
        pre_all = dot(t1_ref[...], x_ref[...].reshape(count * channels, cells))
        grad_all = dot(t2_ref[...], g_ref[...].reshape(count * channels, cells))
        pre = {a: pre_all[(a + 1) * channels:(a + 2) * channels] for a in range(-1, last)}
        grad = {a: grad_all[(a + 1) * channels:(a + 2) * channels] for a in range(-1, last)}

        for a in range(count):
            columns = slice(a * span, a * span + most)
            first = max(0, a + 2 - last) * channels
            y = dot(ws_ref[first:wide, 0:most], xs_ref[columns, :])
            v = dot(ws_ref[wide + first:2 * wide, 0:most], cs_ref[columns, :])
            for step in range(3):
                target = a + 1 - step
                rows = slice(step * channels - first, (step + 1) * channels - first)
                if -1 <= target < last:
                    grad[target] = grad[target] + v[rows]
                if 0 <= target < last:
                    pre[target] = pre[target] + y[rows]
            done = a - 1
            if 1 <= done <= last - 1:
                hidden, pg = activation(pre.pop(done), grad.pop(done))
                h_ref[(done + 1) * channels:(done + 2) * channels, :] = hidden
                pg_ref[done - 1, :, :] = pg
                place = count + 1 - done
                pr_ref[place * channels:(place + 1) * channels, :] = pg
            if a == 1:
                for index, plane in ((0, -1), (1, 0)):
                    pe_ref[index, :, :] = pre.pop(plane)
                    ge_ref[index, :, :] = grad.pop(plane)
        grad_one, grad_two = None, None
        for a in range(0, count, 2):
            pairs = slice(a * span, (a + 2) * span)
            term = dot_nt(cs_ref[pairs, :], h_ref[a * channels:(a + 4) * channels, :])
            grad_two = term if grad_two is None else grad_two + term
            start = (count - 1 - a) * channels
            term = dot_nt(xs_ref[pairs, :], pr_ref[start:start + 4 * channels, :])
            grad_one = term if grad_one is None else grad_one + term
        g2_ref[...] = grad_two
        turned = grad_one.T
        for step in range(3):
            first, second = (step + 1) * channels, step * channels
            g1_ref[:, step * span:(step + 1) * span] = (
                turned[first:first + channels, 0:span] + turned[second:second + channels, span:])

    return kernel


def make_edge_kernel(count, channels, cells, vertical):
    span = 9 * channels
    most = 8 * channels
    wide = 3 * channels

    def kernel(up_ref, ws_ref, t1_ref, t2_ref, codes_ref, pe_ref, ge_ref, xs_ref, cs_ref, g1_ref, g2_ref,
               keep_ref, send_ref, pg_ref, xf_ref, xo_ref, cf_ref):
        odd = lax.axis_index(AXIS) % 2
        masks = tap_masks(cells, vertical)
        places = flipped_places(codes_ref[0, 0, 0])
        fill_x = filler(xf_ref, channels, masks, vertical)
        fill_c = filler(cf_ref, channels, masks, vertical)
        planes = flip_planes(up_ref[...].reshape(4 * channels, cells), codes_ref[0, 0:1, 0:1], vertical)
        fill_x(0, planes[0:channels], places)
        fill_x(1, planes[channels:2 * channels], places, xo_ref)
        for place in range(9):
            start = 2 * span + places[place] * channels
            xf_ref[pl.ds(pl.multiple_of(start, channels), channels), :] = xs_ref[place * channels:(place + 1) * channels, :]
        fill_c(0, planes[2 * channels:3 * channels], places)
        fill_c(1, planes[3 * channels:], places)

        def eight(ref, index):
            return ref[index * span:index * span + most, :]

        def rows(part, first, end):
            return ws_ref[part * wide + first * channels:part * wide + end * channels, 0:most]

        centre = slice(2 * channels, 4 * channels), slice(0, 2 * channels)
        x_mid = dot(t1_ref[centre], planes[:2 * channels])
        g_mid = dot(t2_ref[centre], planes[2 * channels:])
        pre_m = (pe_ref[0] + x_mid[:channels] + dot(rows(0, 0, 1), eight(xf_ref, 0))
                 + dot(rows(0, 1, 2), eight(xf_ref, 1)) + dot(rows(0, 2, 3), eight(xf_ref, 2)))
        pre_0 = pe_ref[1] + x_mid[channels:] + dot(rows(0, 0, 1), eight(xo_ref, 0))
        near = dot(rows(1, 0, 2), eight(cf_ref, 1))
        grad_m = ge_ref[0] + g_mid[:channels] + near[channels:] + dot(rows(1, 0, 1), eight(cf_ref, 0))
        grad_0 = ge_ref[1] + g_mid[channels:] + near[:channels]
        hid_m, pg_m = activation(pre_m, grad_m)
        hid_0, pg_0 = activation(pre_0, grad_0)
        pg_ref[0, :, :] = pg_m
        pg_ref[1, :, :] = pg_0

        zero = jnp.zeros((2 * channels, cells), BF16)
        grad_two = (g2_ref[...] + dot_nt(cf_ref[...], jnp.concatenate((zero, hid_m, hid_0), axis=0))
                    + dot_nt(cs_ref[0:2 * span, :], jnp.concatenate((hid_m, hid_0, zero), axis=0)))
        below = dot_nt(pg_m, xf_ref[...])
        own_end = dot_nt(pg_0, xo_ref[...])
        own = dot_nt(pg_0, xs_ref[0:2 * span, :])

        def put(ref, one):
            if one:
                ref[:, 0:span] = g1_ref[:, 0:span] + below[:, 0:span] + own_end
                ref[:, span:] = g1_ref[:, span:] + below[:, span:] + own
            else:
                total = grad_two[0:span] + pltpu.roll(grad_two[span:], 3 * channels, 1)
                for place, tap in enumerate(ORDER):
                    block = total[place * channels:(place + 1) * channels]
                    shift = ((8 - tap) * channels) % (4 * channels)
                    block = pltpu.roll(block, shift, 1) if shift else block
                    for step in range(3):
                        at = (9 * step + 8 - tap) * channels
                        lane = at % (4 * channels)
                        ref[:, at:at + channels] = block[:, lane:lane + channels]

        @pl.when(odd == 0)
        def _():
            put(keep_ref, True)
            put(send_ref, False)

        @pl.when(odd == 1)
        def _():
            put(keep_ref, False)
            put(send_ref, True)

    return kernel


def make_input_kernel(count, channels, cells, vertical):
    span = 9 * channels
    wide = 3 * channels

    def kernel(pi_ref, pe_ref, down_ref, codes_ref, g_ref, ws_ref, out_ref, ps_ref):
        fill = filler(ps_ref, channels, tap_masks(cells, vertical), vertical)
        above = flip_planes(down_ref[...].reshape(2 * channels, cells), codes_ref[1, 0:1, 0:1], vertical)
        weights = ws_ref[2 * wide:3 * wide, :]
        total = {}
        for a in range(-1, count + 1):
            if a <= 0:
                plane = pe_ref[a + 1]
            elif a >= count - 1:
                plane = above[(a - count + 1) * channels:(a - count + 2) * channels]
            else:
                plane = pi_ref[a - 1]
            side = {-1: 0, count: 1}.get(a)
            fill(a + 1, plane, None if side is None else flipped_places(codes_ref[side, 0, 0]))
            columns = ps_ref[(a + 1) * span:(a + 2) * span, :]
            if a == -1:
                total[0] = dot(weights[0:channels], columns)
            elif a == count:
                total[count - 1] = total[count - 1] + dot(weights[2 * channels:], columns)
            else:
                y = dot(weights, columns)
                for step in range(3):
                    target = a + 1 - step
                    if 0 <= target < count:
                        part = y[step * channels:(step + 1) * channels]
                        total[target] = part if target not in total else total[target] + part
            if a >= 1:
                out_ref[a - 1, :, :] = g_ref[a - 1].astype(F32) + total.pop(a - 1)

    return kernel


def normalize_kernel(mine_ref, other_ref, one_ref, two_ref):
    odd = lax.axis_index(AXIS) % 2
    span = mine_ref.shape[1] // 3
    part = span // 9

    def scaled(ref):
        v = ref[...]
        return v / jnp.sqrt(jnp.mean(v * v) + 1e-06)

    def put(ref, value):
        for step in range(3):
            base = step * span
            ref[:, base:base + 4 * part] = value[:, base:base + 4 * part]
            ref[:, base + 4 * part:base + 5 * part] = value[:, base + 8 * part:base + span]
            ref[:, base + 5 * part:base + span] = value[:, base + 4 * part:base + 8 * part]

    @pl.when(odd == 0)
    def _():
        put(one_ref, scaled(mine_ref))
        two_ref[...] = scaled(other_ref)

    @pl.when(odd == 1)
    def _():
        put(one_ref, scaled(other_ref))
        two_ref[...] = scaled(mine_ref)


VM = pl.BlockSpec(memory_space=pltpu.VMEM)
SM = pl.BlockSpec(memory_space=pltpu.SMEM)
HB = pl.BlockSpec(memory_space=pltpu.HBM)
PARAMS = pltpu.CompilerParams(vmem_limit_bytes=VMEM_LIMIT)


def body(snapshot, cotangent, first_weight, second_weight, face_codes):
    count, channels, cells = snapshot.shape[1:]
    vertical = cells // R_CELLS
    size = lax.axis_size(AXIS)
    x, g = snapshot[0], cotangent[0]
    def call(kernel, outs, operands, name, scratch=(), specs=None):
        return pl.pallas_call(
            kernel, out_shape=outs, in_specs=specs or [VM] * len(operands),
            out_specs=jax.tree.map(lambda _: VM, outs),
            scratch_shapes=list(scratch), compiler_params=PARAMS, name=name,
        )(*operands)

    span = 9 * channels
    shape = jax.ShapeDtypeStruct
    sizes = (count, channels, cells, vertical)
    stack = shape((span, span), BF16)
    band = shape(((count + 2) * channels, count * channels), BF16)
    edges = shape((2, channels, cells), F32)
    columns = shape((count * span, cells), BF16)
    grads = shape((channels, 27 * channels), F32)
    weight = shape(first_weight.shape, BF16)
    pinned = [
        pltpu.with_memory_space_constraint(v, pltpu.HBM) for v in (face_codes, x, g, first_weight, second_weight)]
    up, codes, x, g, first_weight, second_weight = call(
        make_pack_kernel(count),
        (shape((4, channels, cells), BF16), shape((2, 8, 128), jnp.int32), shape(x.shape, BF16), shape(x.shape, BF16),
         weight, weight),
        pinned, "pack", [pltpu.SMEM((1, 2), jnp.int32), pltpu.SemaphoreType.DMA((5,))], [HB] * 5)
    up = lax.ppermute(up, AXIS, [(b, (b + 1) % size) for b in range(size)])

    ws, band_one, band_two, pre_edge, grad_edge, xs, cs, pg_inner, part_one, part_two = call(
        make_interior_kernel(*sizes),
        (stack, band, band, edges, edges, columns, columns,
         shape((count - 2, channels, cells), BF16), grads, shape((2 * span, 4 * channels), F32)),
        (x, g, first_weight, second_weight), "interior",
        [pltpu.VMEM(((count + 2) * channels, cells), BF16), pltpu.VMEM(((count + 3) * channels, cells), BF16)])
    keep, send, pg_edge = call(
        make_edge_kernel(*sizes), (grads, grads, shape((2, channels, cells), BF16)),
        (up, ws, band_one, band_two, codes, pre_edge, grad_edge, xs, cs, part_one, part_two), "edge",
        [pltpu.VMEM((3 * span, cells), BF16), pltpu.VMEM((span, cells), BF16), pltpu.VMEM((2 * span, cells), BF16)])

    def swap(value, bit):
        return lax.ppermute(value, AXIS, [(b, b ^ bit) for b in range(size)])

    total, pg_sent = lax.optimization_barrier((keep + swap(send, 1), pg_edge))
    down = lax.ppermute(pg_sent, AXIS, [(b, (b - 1) % size) for b in range(size)])
    bit = 2
    while bit < size:
        total = total + swap(total, bit)
        if bit == 4:
            input_grad = call(
                make_input_kernel(*sizes), shape((count, channels, cells), F32),
                (pg_inner, pg_edge, down, codes, g, ws), "input_grad",
                [pltpu.VMEM(((count + 2) * span, cells), BF16)])
        if bit == 8:
            total, input_grad = lax.optimization_barrier((total, input_grad))
        bit *= 2
    first, second = call(normalize_kernel, (grads, grads), (total, swap(total, 1)), "normalize")
    return (input_grad[None], first, second)


def solution(mesh):
    return jax.shard_map(
        body,
        mesh=mesh,
        in_specs=(
            P("groups", "blocks", None, None),
            P("groups", "blocks", None, None),
            P(),
            P(),
            P(("groups", "blocks"), None),
        ),
        out_specs=(P("groups", "blocks", None, None), P("groups", None), P("groups", None)),
        check_vma=False,
    )
```

time: 34.4 us -> 33 us (0.959)
  waiting for transfers between devices: 14.8 us -> 13.6 us
    ppermute x5, waiting for transfers between devices: 14.8 us -> 10.3 us  [swap(): return lax.ppermute(value, AXIS, [(b, b ^ bit) for b in range(size)])]
    ppermute x2, waiting for transfers between devices: 0.01 us -> 3.34 us  [the longest x1 3.34 us: body(): lax.ppermute(pg_sent, AXIS, [(b, (b - 1) % size) for b in range(size)])]
  transfers between devices with their start and end apart: 7 -> 7, of which waited for: 5 -> 5; matrix products, arithmetic and copies ran while one was open for 0% -> 0% of each run, Pallas kernels for 17% -> 18%
where the time goes in v4:
time: 33 us; the launch traced here: 32.4 us
  waiting for transfers between devices  13.6 us (41%)
  Pallas kernels  9.74 us (30%)
  starting transfers between devices  8.35 us (25%)
  between operations  0.7 us (2%)
    ppermute x5, waiting for transfers between devices, swap(): return lax.ppermute(value, AXIS, [(b, b ^ bit) for b in range(size)])  10.3 us
    pallas_call x5, Pallas kernels, call(): pl.pallas_call(kernel, out_shape=outs, in_specs=specs or [VM] * len(opera...  9.74 us
    ppermute x1, waiting for transfers between devices, body(): lax.ppermute(pg_sent, AXIS, [(b, (b - 1) % size) for b in range(size)])  3.34 us
    ppermute x5, starting transfers between devices, swap(): return lax.ppermute(value, AXIS, [(b, b ^ bit) for b in range(size)])  3.07 us
    ppermute x1, starting transfers between devices, body(): up = lax.ppermute(up, AXIS, [(b, (b + 1) % size) for b in range(size)])  2.65 us
    ppermute x1, starting transfers between devices, body(): lax.ppermute(pg_sent, AXIS, [(b, (b - 1) % size) for b in range(size)])  2.62 us
  transfers between devices with their start and end apart: 7, of which 5 were waited for; matrix products, arithmetic and copies ran while one was open for 0% of the time, Pallas kernels for 18%

profile of v4, /device:TPU:1, one launch (start us, length us, event | category | flops | bytes accessed | tf_op | source)
XLA Modules:
  0.0 32.4 jit_solution(18101455094064980765)
XLA Ops:
  0.6 1.1 %pack.1 = (bf16[4,32,512]{2,1,0:T(8,128)(2,1)S(1)}, s32[2,8,128]{2,1,0:T(8,128)S(1)}, bf16[8,32,512]{2,1,0:T(8,128)(2,1)S(1)}, bf16[8,32,512]{2,1,0:T(8,128)(2,1...) custom-call(s32[1,2]{1,0:T(1,128)} %codes_ref.1, bf16[8,32,512]{2,1,0:T(8,128)(2,1)} %bitcast.4, ...), custom_call_target="tpu_custom_call" | custom-call | tf_op jit(solution)/shard_map/pack/pallas_call | solution.py:356
  1.7 2.7 %collective-permute-start = (bf16[4,32,512]{2,1,0:T(8,128)(2,1)S(1)}, bf16[4,32,512]{2,1,0:T(8,128)(2,1)S(1)}, u32[]{:S(2)}, u32[]{:S(2)}) collective-permute-start(bf16[4,32,512]{2,1,0:T(8,128)(2,1)S(1)} %get-tuple-element.28), channel_id=1, source_target_pairs={{0,1},{1,2},{2,3},{3,4},{4,5},{5,6},{6,7},{7,8},{8,9},{9,10},{10,1... | collective-permute-start | bytes 393224 | tf_op jit(solution)/shard_map/ppermute | solution.py:378
  4.4 3.8 %interior.1 = (bf16[288,288]{1,0:T(8,128)(2,1)S(1)}, bf16[320,256]{1,0:T(8,128)(2,1)S(1)}, bf16[320,256]{1,0:T(8,128)(2,1)S(1)}, f32[2,32,512]{2,1,0:T(8,128)S(1...) custom-call(bf16[8,32,512]{2,1,0:T(8,128)(2,1)S(1)} %get-tuple-eleme, ...), custom_call_target="tpu_custom_call" | custom-call | tf_op jit(solution)/shard_map/interior/pallas_call | solution.py:356
  8.2 0.0 collective-permute-done.up_ref
  8.2 1.8 %edge.1 = (f32[32,864]{1,0:T(8,128)S(1)}, f32[32,864]{1,0:T(8,128)S(1)}, bf16[2,32,512]{2,1,0:T(8,128)(2,1)S(1)}) custom-call(bf16[4,32,512]{2,1,0:T(8,128)(2,1)S(1)} %collective-permute-done.up_ref, bf16[288,288]{1,0:T(8,128)(2,1)S(1)} %get-tuple-element.33.ws_ref, bf16[320,256]{1,0:T(8,128)(2,1)S(1)} %get-tuple-element.34.t1_ref, ...), custom_call_target="tpu_custom_call" | custom-call | tf_op jit(solution)/shard_map/edge/pallas_call | solution.py:356
  10.0 1.8 %collective-permute-start.1 = (f32[32,864]{1,0:T(8,128)S(1)}, f32[32,864]{1,0:T(8,128)S(1)}, u32[]{:S(2)}, u32[]{:S(2)}) collective-permute-start(f32[32,864]{1,0:T(8,128)S(1)} %get-tuple-element.44), channel_id=1, source_target_pairs={{0,1},{1,0},{2,3},{3,2},{4,5},{5,4},{6,7},{7,6},{8,9},{9,8},{10,11... | collective-permute-start | bytes 331784 | tf_op jit(solution)/shard_map/ppermute | solution.py:392
  11.8 1.0 %collective-permute-done.1 = f32[32,864]{1,0:T(8,128)S(1)} collective-permute-done((f32[32,864]{1,0:T(8,128)S(1)}, f32[32,864]{1,0:T(8,128)S(1)}, u32[]{:S(2)}, u32[]{:S(2)}) %collective-permute-start.1) | collective-permute-done | bytes 110624 | tf_op jit(solution)/shard_map/ppermute | solution.py:392
  12.8 0.1 collective-permute-start.2
  12.9 4.4 %collective-permute-done.2 = f32[32,864]{1,0:T(8,128)S(1)} collective-permute-done((f32[32,864]{1,0:T(8,128)S(1)}, f32[32,864]{1,0:T(8,128)S(1)}, u32[]{:S(2)}, u32[]{:S(2)}) %collective-permute-start.2) | collective-permute-done | bytes 110624 | tf_op jit(solution)/shard_map/ppermute | solution.py:392
  17.3 0.1 collective-permute-start.3
  17.4 3.6 %collective-permute-done.3 = f32[32,864]{1,0:T(8,128)S(1)} collective-permute-done((f32[32,864]{1,0:T(8,128)S(1)}, f32[32,864]{1,0:T(8,128)S(1)}, u32[]{:S(2)}, u32[]{:S(2)}) %collective-permute-start.3) | collective-permute-done | bytes 110624 | tf_op jit(solution)/shard_map/ppermute | solution.py:392
  21.0 1.0 %collective-permute-start.4 = (f32[32,864]{1,0:T(8,128)S(1)}, f32[32,864]{1,0:T(8,128)S(1)}, u32[]{:S(2)}, u32[]{:S(2)}) collective-permute-start(f32[32,864]{1,0:T(8,128)S(1)} %add.14), channel_id=1, source_target_pairs={{0,8},{1,9},{2,10},{3,11},{4,12},{5,13},{6,14},{7,15},{8,0},{9,1},... | collective-permute-start | bytes 331784 | tf_op jit(solution)/shard_map/ppermute | solution.py:392
  22.0 2.6 %collective-permute-start.5 = (bf16[2,32,512]{2,1,0:T(8,128)(2,1)S(1)}, bf16[2,32,512]{2,1,0:T(8,128)(2,1)S(1)}, u32[]{:S(2)}, u32[]{:S(2)}) collective-permute-start(bf16[2,32,512]{2,1,0:T(8,128)(2,1)S(1)} %get-tuple-element.48.pe_ref), channel_id=1, source_target_pairs={{0,15},{1,0},{2,1},{3,2},{4,3},{5,4},{6,5},{7,6},{8,7},{9,8},{10,9... | collective-permute-start | bytes 196616 | tf_op jit(solution)/shard_map/ppermute | solution.py:395
  24.7 3.3 %collective-permute-done.5.down_ref = bf16[2,32,512]{2,1,0:T(8,128)(2,1)S(1)} collective-permute-done((bf16[2,32,512]{2,1,0:T(8,128)(2,1)S(1)}, bf16[2,32,512]{2,1,0:T(8,128)(2,1)S(1)}, u32[]{:S(2)}, u32[]{:S(2)}) %collective-permute-start.5) | collective-permute-done | bytes 65568 | tf_op jit(solution)/shard_map/ppermute | solution.py:395
  28.0 2.1 %input_grad.1 = f32[8,32,512]{2,1,0:T(8,128)} custom-call(bf16[6,32,512]{2,1,0:T(8,128)(2,1)S(1)} %get-tuple-element.47.pi_ref, bf16[2,32,512]{2,1,0:T(8,128)(2,1)S(1)} %get-tuple-element.48.pe_ref, bf16[2,32,512]{2,1,0:T(8,128)(2,1)S(1)} %collective-permute-done.5.down_ref, s32[2,8,128]{2,1,0:T(8,128)S(1)} %get-tuple-element.36.codes_ref, ...), custom_call_target="tpu_custom_call" | custom-call | tf_op jit(solution)/shard_map/input_grad/pallas_call | solution.py:356
  30.1 0.0 collective-permute-done.4
  30.1 0.1 collective-permute-start.6
  30.2 1.3 %collective-permute-done.6.other_ref = f32[32,864]{1,0:T(8,128)S(1)} collective-permute-done((f32[32,864]{1,0:T(8,128)S(1)}, f32[32,864]{1,0:T(8,128)S(1)}, u32[]{:S(2)}, u32[]{:S(2)}) %collective-permute-start.6) | collective-permute-done | bytes 110624 | tf_op jit(solution)/shard_map/ppermute | solution.py:392
  31.5 1.0 %normalize.1 = (f32[32,864]{1,0:T(8,128)}, f32[32,864]{1,0:T(8,128)}) custom-call(f32[32,864]{1,0:T(8,128)S(1)} %add.15.mine_ref, f32[32,864]{1,0:T(8,128)S(1)} %collective-permute-done.6.other_ref), custom_call_target="tpu_custom_call" | custom-call | tf_op jit(solution)/shard_map/normalize/pallas_call | solution.py:356
  (4 shorter events, 0.1 us)
Async XLA Ops:
  1.7 6.4 %collective-permute-start = (bf16[4,32,512]{2,1,0:T(8,128)(2,1)S(1)}, bf16[4,32,512]{2,1,0:T(8,128)(2,1)S(1)}, u32[]{:S(2)}, u32[]{:S(2)}) collective-permute-start(bf16[4,32,512]{2,1,0:T(8,128)(2,1)S(1)} %get-tuple-element.28), channel_id=1, source_target_pairs={{0,1},{1,2},{2,3},{3,4},{4,5},{5,6},{6,7},{7,8},{8,9},{9,10},{10,1... | collective-permute-start | bytes 393224 | tf_op jit(solution)/shard_map/ppermute | solution.py:378
  10.0 2.8 %collective-permute-start.1 = (f32[32,864]{1,0:T(8,128)S(1)}, f32[32,864]{1,0:T(8,128)S(1)}, u32[]{:S(2)}, u32[]{:S(2)}) collective-permute-start(f32[32,864]{1,0:T(8,128)S(1)} %get-tuple-element.44), channel_id=1, source_target_pairs={{0,1},{1,0},{2,3},{3,2},{4,5},{5,4},{6,7},{7,6},{8,9},{9,8},{10,11... | collective-permute-start | bytes 331784 | tf_op jit(solution)/shard_map/ppermute | solution.py:392
  12.8 4.4 %collective-permute-start.2 = (f32[32,864]{1,0:T(8,128)S(1)}, f32[32,864]{1,0:T(8,128)S(1)}, u32[]{:S(2)}, u32[]{:S(2)}) collective-permute-start(f32[32,864]{1,0:T(8,128)S(1)} %add.12), channel_id=1, source_target_pairs={{0,2},{1,3},{2,0},{3,1},{4,6},{5,7},{6,4},{7,5},{8,10},{9,11},{10,... | collective-permute-start | bytes 331784 | tf_op jit(solution)/shard_map/ppermute | solution.py:392
  17.3 3.7 %collective-permute-start.3 = (f32[32,864]{1,0:T(8,128)S(1)}, f32[32,864]{1,0:T(8,128)S(1)}, u32[]{:S(2)}, u32[]{:S(2)}) collective-permute-start(f32[32,864]{1,0:T(8,128)S(1)} %add.13), channel_id=1, source_target_pairs={{0,4},{1,5},{2,6},{3,7},{4,0},{5,1},{6,2},{7,3},{8,12},{9,13},{10,... | collective-permute-start | bytes 331784 | tf_op jit(solution)/shard_map/ppermute | solution.py:392
  21.0 9.1 %collective-permute-start.4 = (f32[32,864]{1,0:T(8,128)S(1)}, f32[32,864]{1,0:T(8,128)S(1)}, u32[]{:S(2)}, u32[]{:S(2)}) collective-permute-start(f32[32,864]{1,0:T(8,128)S(1)} %add.14), channel_id=1, source_target_pairs={{0,8},{1,9},{2,10},{3,11},{4,12},{5,13},{6,14},{7,15},{8,0},{9,1},... | collective-permute-start | bytes 331784 | tf_op jit(solution)/shard_map/ppermute | solution.py:392
  22.0 6.0 %collective-permute-start.5 = (bf16[2,32,512]{2,1,0:T(8,128)(2,1)S(1)}, bf16[2,32,512]{2,1,0:T(8,128)(2,1)S(1)}, u32[]{:S(2)}, u32[]{:S(2)}) collective-permute-start(bf16[2,32,512]{2,1,0:T(8,128)(2,1)S(1)} %get-tuple-element.48.pe_ref), channel_id=1, source_target_pairs={{0,15},{1,0},{2,1},{3,2},{4,3},{5,4},{6,5},{7,6},{8,7},{9,8},{10,9... | collective-permute-start | bytes 196616 | tf_op jit(solution)/shard_map/ppermute | solution.py:395
  30.1 1.4 %collective-permute-start.6 = (f32[32,864]{1,0:T(8,128)S(1)}, f32[32,864]{1,0:T(8,128)S(1)}, u32[]{:S(2)}, u32[]{:S(2)}) collective-permute-start(f32[32,864]{1,0:T(8,128)S(1)} %add.15.mine_ref), channel_id=1, source_target_pairs={{0,1},{1,0},{2,3},{3,2},{4,5},{5,4},{6,7},{7,6},{8,9},{9,8},{10,11... | collective-permute-start | bytes 331784 | tf_op jit(solution)/shard_map/ppermute | solution.py:392

commit v5 on v4

--- a/solution.py
+++ b/solution.py
@@ -123,8 +123,7 @@
     last = count - 1
 
     def kernel(x_ref, g_ref, w1_ref, w2_ref,
-               ws_ref, t1_ref, t2_ref, pe_ref, ge_ref, xs_ref, cs_ref, pg_ref, g1_ref, g2_ref,
-               h_ref, pr_ref):
+               ws_ref, t1_ref, t2_ref, pe_ref, ge_ref, xs_ref, cs_ref, ps_ref, g1_ref, g2_ref, h_ref):
         masks = tap_masks(cells, vertical)
         for step in range(3):
             rows = slice(step * channels, (step + 1) * channels)
@@ -150,12 +149,12 @@
 
         fill_x = filler(xs_ref, channels, masks, vertical)
         fill_g = filler(cs_ref, channels, masks, vertical)
+        fill_p = filler(ps_ref, channels, masks, vertical)
         for a in range(count):
             fill_x(a, x_ref[a])
             fill_g(a, g_ref[a])
 
         h_ref[...] = jnp.zeros_like(h_ref)
-        pr_ref[...] = jnp.zeros_like(pr_ref)
         pre_all = dot(t1_ref[...], x_ref[...].reshape(count * channels, cells))
         grad_all = dot(t2_ref[...], g_ref[...].reshape(count * channels, cells))
         pre = {a: pre_all[(a + 1) * channels:(a + 2) * channels] for a in range(-1, last)}
@@ -177,27 +176,20 @@
             if 1 <= done <= last - 1:
                 hidden, pg = activation(pre.pop(done), grad.pop(done))
                 h_ref[(done + 1) * channels:(done + 2) * channels, :] = hidden
-                pg_ref[done - 1, :, :] = pg
-                place = count + 1 - done
-                pr_ref[place * channels:(place + 1) * channels, :] = pg
+                fill_p(done - 1, pg)
             if a == 1:
                 for index, plane in ((0, -1), (1, 0)):
                     pe_ref[index, :, :] = pre.pop(plane)
                     ge_ref[index, :, :] = grad.pop(plane)
         grad_one, grad_two = None, None
         for a in range(0, count, 2):
-            pairs = slice(a * span, (a + 2) * span)
-            term = dot_nt(cs_ref[pairs, :], h_ref[a * channels:(a + 4) * channels, :])
+            term = dot_nt(cs_ref[a * span:(a + 2) * span, :], h_ref[a * channels:(a + 4) * channels, :])
             grad_two = term if grad_two is None else grad_two + term
-            start = (count - 1 - a) * channels
-            term = dot_nt(xs_ref[pairs, :], pr_ref[start:start + 4 * channels, :])
+        for a in range(1, last, 2):
+            term = dot_nt(ps_ref[(a - 1) * span:(a + 1) * span, :], x_ref[a - 1:a + 3].reshape(4 * channels, cells))
             grad_one = term if grad_one is None else grad_one + term
+        g1_ref[...] = grad_one
         g2_ref[...] = grad_two
-        turned = grad_one.T
-        for step in range(3):
-            first, second = (step + 1) * channels, step * channels
-            g1_ref[:, step * span:(step + 1) * span] = (
-                turned[first:first + channels, 0:span] + turned[second:second + channels, span:])
 
     return kernel
 
@@ -207,13 +199,14 @@
     most = 8 * channels
     wide = 3 * channels
 
-    def kernel(up_ref, ws_ref, t1_ref, t2_ref, codes_ref, pe_ref, ge_ref, xs_ref, cs_ref, g1_ref, g2_ref,
-               keep_ref, send_ref, pg_ref, xf_ref, xo_ref, cf_ref):
-        odd = lax.axis_index(AXIS) % 2
+    def kernel(up_ref, x_ref, ws_ref, t1_ref, t2_ref, codes_ref, pe_ref, ge_ref, xs_ref, cs_ref, g1_ref, g2_ref,
+               keep_ref, send_ref, pg_ref, ps_ref, xf_ref, xo_ref, cf_ref):
+        is_odd = lax.axis_index(AXIS) % 2 == 1
         masks = tap_masks(cells, vertical)
         places = flipped_places(codes_ref[0, 0, 0])
         fill_x = filler(xf_ref, channels, masks, vertical)
         fill_c = filler(cf_ref, channels, masks, vertical)
+        fill_p = filler(ps_ref, channels, masks, vertical)
         planes = flip_planes(up_ref[...].reshape(4 * channels, cells), codes_ref[0, 0:1, 0:1], vertical)
         fill_x(0, planes[0:channels], places)
         fill_x(1, planes[channels:2 * channels], places, xo_ref)
@@ -246,34 +239,28 @@
         zero = jnp.zeros((2 * channels, cells), BF16)
         grad_two = (g2_ref[...] + dot_nt(cf_ref[...], jnp.concatenate((zero, hid_m, hid_0), axis=0))
                     + dot_nt(cs_ref[0:2 * span, :], jnp.concatenate((hid_m, hid_0, zero), axis=0)))
-        below = dot_nt(pg_m, xf_ref[...])
-        own_end = dot_nt(pg_0, xo_ref[...])
-        own = dot_nt(pg_0, xs_ref[0:2 * span, :])
-
-        def put(ref, one):
-            if one:
-                ref[:, 0:span] = g1_ref[:, 0:span] + below[:, 0:span] + own_end
-                ref[:, span:] = g1_ref[:, span:] + below[:, span:] + own
-            else:
-                total = grad_two[0:span] + pltpu.roll(grad_two[span:], 3 * channels, 1)
-                for place, tap in enumerate(ORDER):
-                    block = total[place * channels:(place + 1) * channels]
-                    shift = ((8 - tap) * channels) % (4 * channels)
-                    block = pltpu.roll(block, shift, 1) if shift else block
-                    for step in range(3):
-                        at = (9 * step + 8 - tap) * channels
-                        lane = at % (4 * channels)
-                        ref[:, at:at + channels] = block[:, lane:lane + channels]
-
-        @pl.when(odd == 0)
-        def _():
-            put(keep_ref, True)
-            put(send_ref, False)
-
-        @pl.when(odd == 1)
-        def _():
-            put(keep_ref, False)
-            put(send_ref, True)
+        fill_p(0, pg_m, places)
+        fill_p(1, pg_0)
+        near = jnp.concatenate((planes[:2 * channels], x_ref[0:2].reshape(2 * channels, cells)), axis=0)
+        grad_one = g1_ref[...] + dot_nt(ps_ref[...], near)
+
+        def put(ref, pairs):
+            total = pairs[0:span] + pltpu.roll(pairs[span:], 3 * channels, 1)
+            moved = {}
+            for place, tap in enumerate(ORDER):
+                block = total[place * channels:(place + 1) * channels]
+                shift = ((8 - tap) * channels) % (4 * channels)
+                moved[8 - tap] = pltpu.roll(block, shift, 1) if shift else block
+            lane = lax.broadcasted_iota(jnp.int32, (channels, 4 * channels), 1) // channels
+            for first in range(0, 27, 4):
+                tile = moved[first % 9]
+                for n in range(first + 1, min(first + 4, 27)):
+                    tile = jnp.where(lane >= n - first, moved[n % 9], tile)
+                width = min(4, 27 - first) * channels
+                ref[:, first * channels:first * channels + width] = tile[:, :width]
+
+        put(keep_ref, jnp.where(is_odd, grad_two, grad_one))
+        put(send_ref, jnp.where(is_odd, grad_one, grad_two))
 
     return kernel
 
@@ -281,63 +268,72 @@
 def make_input_kernel(count, channels, cells, vertical):
     span = 9 * channels
     wide = 3 * channels
-
-    def kernel(pi_ref, pe_ref, down_ref, codes_ref, g_ref, ws_ref, out_ref, ps_ref):
-        fill = filler(ps_ref, channels, tap_masks(cells, vertical), vertical)
-        above = flip_planes(down_ref[...].reshape(2 * channels, cells), codes_ref[1, 0:1, 0:1], vertical)
+    last = count - 1
+
+    def kernel(inner_ref, edge_ref, g_ref, ws_ref, out_ref, rest_ref, done_ref, sems):
         weights = ws_ref[2 * wide:3 * wide, :]
         total = {}
-        for a in range(-1, count + 1):
-            if a <= 0:
-                plane = pe_ref[a + 1]
-            elif a >= count - 1:
-                plane = above[(a - count + 1) * channels:(a - count + 2) * channels]
-            else:
-                plane = pi_ref[a - 1]
-            side = {-1: 0, count: 1}.get(a)
-            fill(a + 1, plane, None if side is None else flipped_places(codes_ref[side, 0, 0]))
-            columns = ps_ref[(a + 1) * span:(a + 2) * span, :]
+        copies = []
+        for a in range(-1, last):
+            columns = edge_ref[(a + 1) * span:(a + 2) * span, :] if a <= 0 else inner_ref[(a - 1) * span:a * span, :]
             if a == -1:
                 total[0] = dot(weights[0:channels], columns)
-            elif a == count:
-                total[count - 1] = total[count - 1] + dot(weights[2 * channels:], columns)
-            else:
-                y = dot(weights, columns)
-                for step in range(3):
-                    target = a + 1 - step
-                    if 0 <= target < count:
-                        part = y[step * channels:(step + 1) * channels]
-                        total[target] = part if target not in total else total[target] + part
+                continue
+            y = dot(weights, columns)
+            for step in range(3):
+                target = a + 1 - step
+                if 0 <= target < count:
+                    part = y[step * channels:(step + 1) * channels]
+                    total[target] = part if target not in total else total[target] + part
             if a >= 1:
-                out_ref[a - 1, :, :] = g_ref[a - 1].astype(F32) + total.pop(a - 1)
+                done_ref[a - 1, :, :] = g_ref[a - 1].astype(F32) + total.pop(a - 1)
+                copies.append(pltpu.make_async_copy(done_ref.at[a - 1], out_ref.at[a - 1], sems.at[a - 1]))
+                copies[-1].start()
+        for index in range(2):
+            a = last - 1 + index
+            rest_ref[index, :, :] = g_ref[a].astype(F32) + total.pop(a)
+        for copy in copies:
+            copy.wait()
+
+    return kernel
+
+
+def make_upper_kernel(count, channels, cells, vertical):
+    span = 9 * channels
+    wide = 3 * channels
+    last = count - 1
+
+    def kernel(down_ref, codes_ref, ws_ref, rest_ref, _, out_ref, ps_ref, done_ref, sem):
+        fill = filler(ps_ref, channels, tap_masks(cells, vertical), vertical)
+        planes = flip_planes(down_ref[...].reshape(2 * channels, cells), codes_ref[1, 0:1, 0:1], vertical)
+        fill(0, planes[:channels])
+        fill(1, planes[channels:], flipped_places(codes_ref[1, 0, 0]))
+        weights = ws_ref[2 * wide + channels:3 * wide, :]
+        y = dot(weights, ps_ref[0:span, :])
+        done_ref[0, :, :] = rest_ref[0] + y[channels:]
+        done_ref[1, :, :] = rest_ref[1] + y[:channels] + dot(weights[channels:], ps_ref[span:, :])
+        copy = pltpu.make_async_copy(done_ref, out_ref.at[last - 1:count], sem)
+        copy.start()
+        copy.wait()
 
     return kernel
 
 
 def normalize_kernel(mine_ref, other_ref, one_ref, two_ref):
     odd = lax.axis_index(AXIS) % 2
-    span = mine_ref.shape[1] // 3
-    part = span // 9
 
     def scaled(ref):
         v = ref[...]
         return v / jnp.sqrt(jnp.mean(v * v) + 1e-06)
 
-    def put(ref, value):
-        for step in range(3):
-            base = step * span
-            ref[:, base:base + 4 * part] = value[:, base:base + 4 * part]
-            ref[:, base + 4 * part:base + 5 * part] = value[:, base + 8 * part:base + span]
-            ref[:, base + 5 * part:base + span] = value[:, base + 4 * part:base + 8 * part]
-
     @pl.when(odd == 0)
     def _():
-        put(one_ref, scaled(mine_ref))
+        one_ref[...] = scaled(mine_ref)
         two_ref[...] = scaled(other_ref)
 
     @pl.when(odd == 1)
     def _():
-        put(one_ref, scaled(other_ref))
+        one_ref[...] = scaled(other_ref)
         two_ref[...] = scaled(mine_ref)
 
 
@@ -352,10 +348,10 @@
     vertical = cells // R_CELLS
     size = lax.axis_size(AXIS)
     x, g = snapshot[0], cotangent[0]
-    def call(kernel, outs, operands, name, scratch=(), specs=None):
+    def call(kernel, outs, operands, name, scratch=(), specs=None, out_specs=None, aliases=None):
         return pl.pallas_call(
             kernel, out_shape=outs, in_specs=specs or [VM] * len(operands),
-            out_specs=jax.tree.map(lambda _: VM, outs),
+            out_specs=out_specs or jax.tree.map(lambda _: VM, outs), input_output_aliases=aliases or {},
             scratch_shapes=list(scratch), compiler_params=PARAMS, name=name,
         )(*operands)
 
@@ -377,15 +373,15 @@
         pinned, "pack", [pltpu.SMEM((1, 2), jnp.int32), pltpu.SemaphoreType.DMA((5,))], [HB] * 5)
     up = lax.ppermute(up, AXIS, [(b, (b + 1) % size) for b in range(size)])
 
-    ws, band_one, band_two, pre_edge, grad_edge, xs, cs, pg_inner, part_one, part_two = call(
+    sums = shape((2 * span, 4 * channels), F32)
+    ws, band_one, band_two, pre_edge, grad_edge, xs, cs, ps, part_one, part_two = call(
         make_interior_kernel(*sizes),
-        (stack, band, band, edges, edges, columns, columns,
-         shape((count - 2, channels, cells), BF16), grads, shape((2 * span, 4 * channels), F32)),
-        (x, g, first_weight, second_weight), "interior",
-        [pltpu.VMEM(((count + 2) * channels, cells), BF16), pltpu.VMEM(((count + 3) * channels, cells), BF16)])
-    keep, send, pg_edge = call(
-        make_edge_kernel(*sizes), (grads, grads, shape((2, channels, cells), BF16)),
-        (up, ws, band_one, band_two, codes, pre_edge, grad_edge, xs, cs, part_one, part_two), "edge",
+        (stack, band, band, edges, edges, columns, columns, shape(((count - 2) * span, cells), BF16), sums, sums),
+        (x, g, first_weight, second_weight), "interior", [pltpu.VMEM(((count + 2) * channels, cells), BF16)])
+    keep, send, pg_edge, ps_edge = call(
+        make_edge_kernel(*sizes),
+        (grads, grads, shape((2, channels, cells), BF16), shape((2 * span, cells), BF16)),
+        (up, x, ws, band_one, band_two, codes, pre_edge, grad_edge, xs, cs, part_one, part_two), "edge",
         [pltpu.VMEM((3 * span, cells), BF16), pltpu.VMEM((span, cells), BF16), pltpu.VMEM((2 * span, cells), BF16)])
 
     def swap(value, bit):
@@ -393,18 +389,25 @@
 
     total, pg_sent = lax.optimization_barrier((keep + swap(send, 1), pg_edge))
     down = lax.ppermute(pg_sent, AXIS, [(b, (b - 1) % size) for b in range(size)])
-    bit = 2
-    while bit < size:
-        total = total + swap(total, bit)
-        if bit == 4:
-            input_grad = call(
-                make_input_kernel(*sizes), shape((count, channels, cells), F32),
-                (pg_inner, pg_edge, down, codes, g, ws), "input_grad",
-                [pltpu.VMEM(((count + 2) * span, cells), BF16)])
-        if bit == 8:
-            total, input_grad = lax.optimization_barrier((total, input_grad))
-        bit *= 2
-    first, second = call(normalize_kernel, (grads, grads), (total, swap(total, 1)), "normalize")
+    most_done, rest = call(
+        make_input_kernel(*sizes), (shape((count, channels, cells), F32), edges),
+        (ps, ps_edge, g, ws), "input_grad",
+        [pltpu.VMEM((count - 2, channels, cells), F32),
+         pltpu.SemaphoreType.DMA((count - 2,))], out_specs=(HB, VM))
+    bits = [1 << power for power in range(1, size.bit_length() - 1)]
+    rounds = list(zip(bits[-1:] + bits[:-1], bits))
+    for index, choice in enumerate(rounds):
+        total = total + lax.ppermute(total, AXIS, [(b, b ^ choice[b % 2]) for b in range(size)])
+        if index == len(rounds) - 2:
+            total, most_done, rest = lax.optimization_barrier((total, most_done, rest))
+        if index == len(rounds) - 1:
+            total, down = lax.optimization_barrier((total, down))
+    other = swap(total, 1)
+    input_grad = call(
+        make_upper_kernel(*sizes), shape((count, channels, cells), F32), (down, codes, ws, rest, most_done), "upper_planes",
+        [pltpu.VMEM((2 * span, cells), BF16), pltpu.VMEM((2, channels, cells), F32), pltpu.SemaphoreType.DMA],
+        [VM, VM, VM, VM, HB], out_specs=HB, aliases={4: 0})
+    first, second = call(normalize_kernel, (grads, grads), (total, other), "normalize")
     return (input_grad[None], first, second)
 
 

time: 33 us -> 31.7 us (0.961); the launches traced: 32.4 us -> 31.6 us
  waiting for transfers between devices: 13.6 us -> 9.12 us
  starting transfers between devices: 8.35 us -> 11.8 us
    ppermute x5 -> x2, waiting for transfers between devices: 10.3 us -> 0.97 us  [swap(): return lax.ppermute(value, AXIS, [(b, b ^ bit) for b in range(size)])]
    ppermute x0 -> x3, waiting for transfers between devices: none -> 7.22 us  [body(): lax.ppermute(total, AXIS, [(b, b ^ choice[b % 2]) for b in range(size)])]
    ppermute x1, waiting for transfers between devices: 3.34 us -> 0.93 us  [body(): lax.ppermute(pg_sent, AXIS, [(b, (b - 1) % size) for b in range(size)])]
    ppermute x5 -> x2, starting transfers between devices: 3.07 us -> 4.55 us  [swap(): return lax.ppermute(value, AXIS, [(b, b ^ bit) for b in range(size)])]
    ppermute x0 -> x3, starting transfers between devices: none -> 1.05 us  [body(): lax.ppermute(total, AXIS, [(b, b ^ choice[b % 2]) for b in range(size)])]
    ppermute x1, starting transfers between devices: 2.62 us -> 3.57 us  [body(): lax.ppermute(pg_sent, AXIS, [(b, (b - 1) % size) for b in range(size)])]
    pallas_call x5 -> x6, Pallas kernels: 9.74 us -> 9.87 us  [call(): pl.pallas_call(kernel, out_shape=outs, in_specs=specs or [VM] * len(opera...]
  transfers between devices with their start and end apart: 7 -> 7, of which waited for: 5 -> 5; matrix products, arithmetic and copies ran while one was open for 0% -> 0% of each run, Pallas kernels for 18% -> 20%
where the time goes in v5:
time: 31.7 us; the launch traced here: 31.6 us
  starting transfers between devices  11.8 us (37%)
  Pallas kernels  9.87 us (31%)
  waiting for transfers between devices  9.12 us (29%)
  between operations  0.72 us (2%)
    pallas_call x6, Pallas kernels, call(): pl.pallas_call(kernel, out_shape=outs, in_specs=specs or [VM] * len(opera...  9.87 us
    ppermute x3, waiting for transfers between devices, body(): lax.ppermute(total, AXIS, [(b, b ^ choice[b % 2]) for b in range(size)])  7.22 us
    ppermute x2, starting transfers between devices, swap(): return lax.ppermute(value, AXIS, [(b, b ^ bit) for b in range(size)])  4.55 us
    ppermute x1, starting transfers between devices, body(): lax.ppermute(pg_sent, AXIS, [(b, (b - 1) % size) for b in range(size)])  3.57 us
    ppermute x1, starting transfers between devices, body(): up = lax.ppermute(up, AXIS, [(b, (b + 1) % size) for b in range(size)])  2.65 us
    ppermute x3, starting transfers between devices, body(): lax.ppermute(total, AXIS, [(b, b ^ choice[b % 2]) for b in range(size)])  1.05 us
    ppermute x2, waiting for transfers between devices, swap(): return lax.ppermute(value, AXIS, [(b, b ^ bit) for b in range(size)])  0.97 us
    ppermute x1, waiting for transfers between devices, body(): lax.ppermute(pg_sent, AXIS, [(b, (b - 1) % size) for b in range(size)])  0.93 us
  transfers between devices with their start and end apart: 7, of which 5 were waited for; matrix products, arithmetic and copies ran while one was open for 0% of the time, Pallas kernels for 20%

profile of v5, /device:TPU:1, one launch (start us, length us, event | category | flops | bytes accessed | tf_op | source)
XLA Modules:
  0.0 31.6 jit_solution(12418102620479234562)
XLA Ops:
  0.6 1.1 %pack.1 = (bf16[4,32,512]{2,1,0:T(8,128)(2,1)S(1)}, s32[2,8,128]{2,1,0:T(8,128)S(1)}, bf16[8,32,512]{2,1,0:T(8,128)(2,1)S(1)}, bf16[8,32,512]{2,1,0:T(8,128)(2,1...) custom-call(s32[1,2]{1,0:T(1,128)} %codes_ref.1, bf16[8,32,512]{2,1,0:T(8,128)(2,1)} %bitcast.4, ...), custom_call_target="tpu_custom_call" | custom-call | tf_op jit(solution)/shard_map/pack/pallas_call | solution.py:352
  1.7 2.7 %collective-permute-start = (bf16[4,32,512]{2,1,0:T(8,128)(2,1)S(1)}, bf16[4,32,512]{2,1,0:T(8,128)(2,1)S(1)}, u32[]{:S(2)}, u32[]{:S(2)}) collective-permute-start(bf16[4,32,512]{2,1,0:T(8,128)(2,1)S(1)} %get-tuple-element.34), channel_id=1, source_target_pairs={{0,1},{1,2},{2,3},{3,4},{4,5},{5,6},{6,7},{7,8},{8,9},{9,10},{10,1... | collective-permute-start | bytes 393224 | tf_op jit(solution)/shard_map/ppermute | solution.py:374
  4.4 3.7 %interior.1 = (bf16[288,288]{1,0:T(8,128)(2,1)S(1)}, bf16[320,256]{1,0:T(8,128)(2,1)S(1)}, bf16[320,256]{1,0:T(8,128)(2,1)S(1)}, f32[2,32,512]{2,1,0:T(8,128)S(1...) custom-call(bf16[8,32,512]{2,1,0:T(8,128)(2,1)S(1)} %get-tuple-eleme, ...), custom_call_target="tpu_custom_call" | custom-call | tf_op jit(solution)/shard_map/interior/pallas_call | solution.py:352
  8.1 0.0 collective-permute-done.up_ref
  8.1 1.5 %edge.1 = (f32[32,864]{1,0:T(8,128)S(1)}, f32[32,864]{1,0:T(8,128)S(1)}, bf16[2,32,512]{2,1,0:T(8,128)(2,1)S(1)}, bf16[576,512]{1,0:T(8,128)(2,1)S(1)}) custom-call(bf16[4,32,512]{2,1,0:T(8,128)(2,1)S(1)} %collective-permute-done.up_ref, bf16[8,32,512]{2,1,0:T(8,128)(2,1)S(1)} %get-tuple-element.35.x_ref, bf16[288,288]{1,0:T(8,128)(2,1)S(1)} %get-tuple-element.39.ws_ref, ...), custom_call_target="tpu_custom_call" | custom-call | tf_op jit(solution)/shard_map/edge/pallas_call | solution.py:352
  9.6 1.9 %collective-permute-start.1 = (f32[32,864]{1,0:T(8,128)S(1)}, f32[32,864]{1,0:T(8,128)S(1)}, u32[]{:S(2)}, u32[]{:S(2)}) collective-permute-start(f32[32,864]{1,0:T(8,128)S(1)} %get-tuple-element.50), channel_id=1, source_target_pairs={{0,1},{1,0},{2,3},{3,2},{4,5},{5,4},{6,7},{7,6},{8,9},{9,8},{10,11... | collective-permute-start | bytes 331784 | tf_op jit(solution)/shard_map/ppermute | solution.py:388
  11.5 1.0 %collective-permute-done.1 = f32[32,864]{1,0:T(8,128)S(1)} collective-permute-done((f32[32,864]{1,0:T(8,128)S(1)}, f32[32,864]{1,0:T(8,128)S(1)}, u32[]{:S(2)}, u32[]{:S(2)}) %collective-permute-start.1) | collective-permute-done | bytes 110624 | tf_op jit(solution)/shard_map/ppermute | solution.py:388
  12.5 0.1 collective-permute-start.2
  12.6 3.6 %collective-permute-done.2 = f32[32,864]{1,0:T(8,128)S(1)} collective-permute-done((f32[32,864]{1,0:T(8,128)S(1)}, f32[32,864]{1,0:T(8,128)S(1)}, u32[]{:S(2)}, u32[]{:S(2)}) %collective-permute-start.2) | collective-permute-done | bytes 110624 | tf_op jit(solution)/shard_map/ppermute | solution.py:400
  16.2 0.1 collective-permute-start.3
  16.3 1.4 %input_grad.1 = (f32[8,32,512]{2,1,0:T(8,128)}, f32[2,32,512]{2,1,0:T(8,128)S(1)}) custom-call(bf16[1728,512]{1,0:T(8,128)(2,1)S(1)} %get-tuple-element.53.inner_ref, bf16[576,512]{1,0:T(8,128)(2,1)S(1)} %get-tuple-element.54.edge_ref, bf16[8,32,512]{2,1,0:T(8,128)(2,1)S(1)} %get-tuple-element.36.g_ref, bf16[288,288]{1,0:T(8,128)(2,1)S(1)} %get-tuple-element.39.ws_ref), custom_call_target="tpu_custom_call" | custom-call | tf_op jit(solution)/shard_map/input_grad/pallas_call | solution.py:352
  17.7 2.4 %collective-permute-done.3 = f32[32,864]{1,0:T(8,128)S(1)} collective-permute-done((f32[32,864]{1,0:T(8,128)S(1)}, f32[32,864]{1,0:T(8,128)S(1)}, u32[]{:S(2)}, u32[]{:S(2)}) %collective-permute-start.3) | collective-permute-done | bytes 110624 | tf_op jit(solution)/shard_map/ppermute | solution.py:400
  20.1 0.9 %collective-permute-start.4 = (f32[32,864]{1,0:T(8,128)S(1)}, f32[32,864]{1,0:T(8,128)S(1)}, u32[]{:S(2)}, u32[]{:S(2)}) collective-permute-start(f32[32,864]{1,0:T(8,128)S(1)} %add.14), channel_id=1, source_target_pairs={{0,4},{1,9},{2,6},{3,11},{4,0},{5,13},{6,2},{7,15},{8,12},{9,1},{1... | collective-permute-start | bytes 331784 | tf_op jit(solution)/shard_map/ppermute | solution.py:400
  21.0 3.6 %collective-permute-start.5 = (bf16[2,32,512]{2,1,0:T(8,128)(2,1)S(1)}, bf16[2,32,512]{2,1,0:T(8,128)(2,1)S(1)}, u32[]{:S(2)}, u32[]{:S(2)}) collective-permute-start(bf16[2,32,512]{2,1,0:T(8,128)(2,1)S(1)} %get-tuple-element.58), channel_id=1, source_target_pairs={{0,15},{1,0},{2,1},{3,2},{4,3},{5,4},{6,5},{7,6},{8,7},{9,8},{10,9... | collective-permute-start | bytes 196616 | tf_op jit(solution)/shard_map/ppermute | solution.py:391
  24.6 1.2 %collective-permute-done.4 = f32[32,864]{1,0:T(8,128)S(1)} collective-permute-done((f32[32,864]{1,0:T(8,128)S(1)}, f32[32,864]{1,0:T(8,128)S(1)}, u32[]{:S(2)}, u32[]{:S(2)}) %collective-permute-start.4) | collective-permute-done | bytes 110624 | tf_op jit(solution)/shard_map/ppermute | solution.py:400
  25.8 0.9 %collective-permute-done.5.down_ref = bf16[2,32,512]{2,1,0:T(8,128)(2,1)S(1)} collective-permute-done((bf16[2,32,512]{2,1,0:T(8,128)(2,1)S(1)}, bf16[2,32,512]{2,1,0:T(8,128)(2,1)S(1)}, u32[]{:S(2)}, u32[]{:S(2)}) %collective-permute-start.5) | collective-permute-done | bytes 65568 | tf_op jit(solution)/shard_map/ppermute | solution.py:391
  26.7 2.7 %collective-permute-start.6 = (f32[32,864]{1,0:T(8,128)S(1)}, f32[32,864]{1,0:T(8,128)S(1)}, u32[]{:S(2)}, u32[]{:S(2)}) collective-permute-start(f32[32,864]{1,0:T(8,128)S(1)} %add.15.mine_ref), channel_id=1, source_target_pairs={{0,1},{1,0},{2,3},{3,2},{4,5},{5,4},{6,7},{7,6},{8,9},{9,8},{10,11... | collective-permute-start | bytes 331784 | tf_op jit(solution)/shard_map/ppermute | solution.py:388
  29.4 1.2 %upper_planes.1 = f32[8,32,512]{2,1,0:T(8,128)} custom-call(bf16[2,32,512]{2,1,0:T(8,128)(2,1)S(1)} %collective-permute-done.5.down_ref, s32[2,8,128]{2,1,0:T(8,128)S(1)} %get-tuple-element.42.codes_ref, bf16[288,288]{1,0:T(8,128)(2,1)S(1)} %get-tuple-element.39.ws_ref, ...), custom_call_target="tpu_custom_call", output_to_operand_aliasing={{}: (4, {})} | custom-call | tf_op jit(solution)/shard_map/upper_planes/pallas_call | solution.py:352
  30.6 0.0 collective-permute-done.6.other_ref
  30.6 1.0 %normalize.1 = (f32[32,864]{1,0:T(8,128)}, f32[32,864]{1,0:T(8,128)}) custom-call(f32[32,864]{1,0:T(8,128)S(1)} %add.15.mine_ref, f32[32,864]{1,0:T(8,128)S(1)} %collective-permute-done.6.other_ref), custom_call_target="tpu_custom_call" | custom-call | tf_op jit(solution)/shard_map/normalize/pallas_call | solution.py:352
  (4 shorter events, 0.1 us)
Async XLA Ops:
  1.7 6.4 %collective-permute-start = (bf16[4,32,512]{2,1,0:T(8,128)(2,1)S(1)}, bf16[4,32,512]{2,1,0:T(8,128)(2,1)S(1)}, u32[]{:S(2)}, u32[]{:S(2)}) collective-permute-start(bf16[4,32,512]{2,1,0:T(8,128)(2,1)S(1)} %get-tuple-element.34), channel_id=1, source_target_pairs={{0,1},{1,2},{2,3},{3,4},{4,5},{5,6},{6,7},{7,8},{8,9},{9,10},{10,1... | collective-permute-start | bytes 393224 | tf_op jit(solution)/shard_map/ppermute | solution.py:374
  9.6 2.8 %collective-permute-start.1 = (f32[32,864]{1,0:T(8,128)S(1)}, f32[32,864]{1,0:T(8,128)S(1)}, u32[]{:S(2)}, u32[]{:S(2)}) collective-permute-start(f32[32,864]{1,0:T(8,128)S(1)} %get-tuple-element.50), channel_id=1, source_target_pairs={{0,1},{1,0},{2,3},{3,2},{4,5},{5,4},{6,7},{7,6},{8,9},{9,8},{10,11... | collective-permute-start | bytes 331784 | tf_op jit(solution)/shard_map/ppermute | solution.py:388
  12.5 3.7 %collective-permute-start.2 = (f32[32,864]{1,0:T(8,128)S(1)}, f32[32,864]{1,0:T(8,128)S(1)}, u32[]{:S(2)}, u32[]{:S(2)}) collective-permute-start(f32[32,864]{1,0:T(8,128)S(1)} %add.12), channel_id=1, source_target_pairs={{0,8},{1,3},{2,10},{3,1},{4,12},{5,7},{6,14},{7,5},{8,0},{9,11},{1... | collective-permute-start | bytes 331784 | tf_op jit(solution)/shard_map/ppermute | solution.py:400
  16.2 3.8 %collective-permute-start.3 = (f32[32,864]{1,0:T(8,128)S(1)}, f32[32,864]{1,0:T(8,128)S(1)}, u32[]{:S(2)}, u32[]{:S(2)}) collective-permute-start(f32[32,864]{1,0:T(8,128)S(1)} %add.13), channel_id=1, source_target_pairs={{0,2},{1,5},{2,0},{3,7},{4,6},{5,1},{6,4},{7,3},{8,10},{9,13},{10,... | collective-permute-start | bytes 331784 | tf_op jit(solution)/shard_map/ppermute | solution.py:400
  20.1 5.7 %collective-permute-start.4 = (f32[32,864]{1,0:T(8,128)S(1)}, f32[32,864]{1,0:T(8,128)S(1)}, u32[]{:S(2)}, u32[]{:S(2)}) collective-permute-start(f32[32,864]{1,0:T(8,128)S(1)} %add.14), channel_id=1, source_target_pairs={{0,4},{1,9},{2,6},{3,11},{4,0},{5,13},{6,2},{7,15},{8,12},{9,1},{1... | collective-permute-start | bytes 331784 | tf_op jit(solution)/shard_map/ppermute | solution.py:400
  21.0 5.7 %collective-permute-start.5 = (bf16[2,32,512]{2,1,0:T(8,128)(2,1)S(1)}, bf16[2,32,512]{2,1,0:T(8,128)(2,1)S(1)}, u32[]{:S(2)}, u32[]{:S(2)}) collective-permute-start(bf16[2,32,512]{2,1,0:T(8,128)(2,1)S(1)} %get-tuple-element.58), channel_id=1, source_target_pairs={{0,15},{1,0},{2,1},{3,2},{4,3},{5,4},{6,5},{7,6},{8,7},{9,8},{10,9... | collective-permute-start | bytes 196616 | tf_op jit(solution)/shard_map/ppermute | solution.py:391
  26.7 3.9 %collective-permute-start.6 = (f32[32,864]{1,0:T(8,128)S(1)}, f32[32,864]{1,0:T(8,128)S(1)}, u32[]{:S(2)}, u32[]{:S(2)}) collective-permute-start(f32[32,864]{1,0:T(8,128)S(1)} %add.15.mine_ref), channel_id=1, source_target_pairs={{0,1},{1,0},{2,3},{3,2},{4,5},{5,4},{6,7},{7,6},{8,9},{9,8},{10,11... | collective-permute-start | bytes 331784 | tf_op jit(solution)/shard_map/ppermute | solution.py:388

commit v6 on v5

--- a/solution.py
+++ b/solution.py
@@ -194,19 +194,64 @@
     return kernel
 
 
+def put_blocks(ref, pairs, channels):
+    span = 9 * channels
+    total = pairs[0:span] + pltpu.roll(pairs[span:], 3 * channels, 1)
+    moved = {}
+    for place, tap in enumerate(ORDER):
+        block = total[place * channels:(place + 1) * channels]
+        shift = ((8 - tap) * channels) % (4 * channels)
+        moved[8 - tap] = pltpu.roll(block, shift, 1) if shift else block
+    lane = lax.broadcasted_iota(jnp.int32, (channels, 4 * channels), 1) // channels
+    for first in range(0, 27, 4):
+        tile = moved[first % 9]
+        for n in range(first + 1, min(first + 4, 27)):
+            tile = jnp.where(lane >= n - first, moved[n % 9], tile)
+        width = min(4, 27 - first) * channels
+        ref[:, first * channels:first * channels + width] = tile[:, :width]
+
+
+def first_terms(sum_ref, ps_ref, low_ref, x_ref, channels):
+    near = jnp.concatenate((low_ref[...], x_ref[0:2].reshape(low_ref.shape)), axis=0)
+    return sum_ref[...] + dot_nt(ps_ref[...], near)
+
+
+def second_terms(sum_ref, cf_ref, cs_ref, hidden, channels):
+    zero = jnp.zeros_like(hidden)
+    return (sum_ref[...] + dot_nt(cf_ref[...], jnp.concatenate((zero, hidden), axis=0))
+            + dot_nt(cs_ref[0:18 * channels, :], jnp.concatenate((hidden, zero), axis=0)))
+
+
+def make_keep_kernel(channels, cells, vertical):
+    def kernel(x_ref, codes_ref, cs_ref, g1_ref, g2_ref, pg_ref, h_ref, low_ref, cf_ref, keep_ref, ps_ref):
+        is_odd = lax.axis_index(AXIS) % 2 == 1
+        fill_p = filler(ps_ref, channels, tap_masks(cells, vertical), vertical)
+        fill_p(0, pg_ref[0], flipped_places(codes_ref[0, 0, 0]))
+        fill_p(1, pg_ref[1])
+
+        @pl.when(jnp.logical_not(is_odd))
+        def _():
+            put_blocks(keep_ref, first_terms(g1_ref, ps_ref, low_ref, x_ref, channels), channels)
+
+        @pl.when(is_odd)
+        def _():
+            put_blocks(keep_ref, second_terms(g2_ref, cf_ref, cs_ref, h_ref[...], channels), channels)
+
+    return kernel
+
+
 def make_edge_kernel(count, channels, cells, vertical):
     span = 9 * channels
     most = 8 * channels
     wide = 3 * channels
 
     def kernel(up_ref, x_ref, ws_ref, t1_ref, t2_ref, codes_ref, pe_ref, ge_ref, xs_ref, cs_ref, g1_ref, g2_ref,
-               keep_ref, send_ref, pg_ref, ps_ref, xf_ref, xo_ref, cf_ref):
+               send_ref, pg_ref, h_ref, low_ref, cf_ref, xf_ref, xo_ref, ps_ref):
         is_odd = lax.axis_index(AXIS) % 2 == 1
         masks = tap_masks(cells, vertical)
         places = flipped_places(codes_ref[0, 0, 0])
         fill_x = filler(xf_ref, channels, masks, vertical)
         fill_c = filler(cf_ref, channels, masks, vertical)
-        fill_p = filler(ps_ref, channels, masks, vertical)
         planes = flip_planes(up_ref[...].reshape(4 * channels, cells), codes_ref[0, 0:1, 0:1], vertical)
         fill_x(0, planes[0:channels], places)
         fill_x(1, planes[channels:2 * channels], places, xo_ref)
@@ -236,31 +281,20 @@
         pg_ref[0, :, :] = pg_m
         pg_ref[1, :, :] = pg_0
 
-        zero = jnp.zeros((2 * channels, cells), BF16)
-        grad_two = (g2_ref[...] + dot_nt(cf_ref[...], jnp.concatenate((zero, hid_m, hid_0), axis=0))
-                    + dot_nt(cs_ref[0:2 * span, :], jnp.concatenate((hid_m, hid_0, zero), axis=0)))
-        fill_p(0, pg_m, places)
-        fill_p(1, pg_0)
-        near = jnp.concatenate((planes[:2 * channels], x_ref[0:2].reshape(2 * channels, cells)), axis=0)
-        grad_one = g1_ref[...] + dot_nt(ps_ref[...], near)
-
-        def put(ref, pairs):
-            total = pairs[0:span] + pltpu.roll(pairs[span:], 3 * channels, 1)
-            moved = {}
-            for place, tap in enumerate(ORDER):
-                block = total[place * channels:(place + 1) * channels]
-                shift = ((8 - tap) * channels) % (4 * channels)
-                moved[8 - tap] = pltpu.roll(block, shift, 1) if shift else block
-            lane = lax.broadcasted_iota(jnp.int32, (channels, 4 * channels), 1) // channels
-            for first in range(0, 27, 4):
-                tile = moved[first % 9]
-                for n in range(first + 1, min(first + 4, 27)):
-                    tile = jnp.where(lane >= n - first, moved[n % 9], tile)
-                width = min(4, 27 - first) * channels
-                ref[:, first * channels:first * channels + width] = tile[:, :width]
-
-        put(keep_ref, jnp.where(is_odd, grad_two, grad_one))
-        put(send_ref, jnp.where(is_odd, grad_one, grad_two))
+        h_ref[0:channels, :] = hid_m
+        h_ref[channels:, :] = hid_0
+        low_ref[...] = planes[:2 * channels]
+
+        @pl.when(jnp.logical_not(is_odd))
+        def _():
+            put_blocks(send_ref, second_terms(g2_ref, cf_ref, cs_ref, h_ref[...], channels), channels)
+
+        @pl.when(is_odd)
+        def _():
+            fill_p = filler(ps_ref, channels, masks, vertical)
+            fill_p(0, pg_m, places)
+            fill_p(1, pg_0)
+            put_blocks(send_ref, first_terms(g1_ref, ps_ref, low_ref, x_ref, channels), channels)
 
     return kernel
 
@@ -298,12 +332,30 @@
     return kernel
 
 
+def write_update(scaled_ref, sum_ref, one_ref, two_ref, sems, swapped, finish):
+    own = lax.axis_index(AXIS) % 2
+    if not finish:
+        v = sum_ref[...]
+        scaled_ref[...] = v / jnp.sqrt(jnp.mean(v * v) + 1e-06)
+    for index, target in enumerate((one_ref, two_ref)):
+
+        @pl.when(own == (index ^ swapped))
+        def _(index=index, target=target):
+            copy = pltpu.make_async_copy(scaled_ref, target, sems.at[index])
+            if finish:
+                copy.wait()
+            else:
+                copy.start()
+
+
 def make_upper_kernel(count, channels, cells, vertical):
     span = 9 * channels
     wide = 3 * channels
     last = count - 1
 
-    def kernel(down_ref, codes_ref, ws_ref, rest_ref, _, out_ref, ps_ref, done_ref, sem):
+    def kernel(down_ref, codes_ref, ws_ref, rest_ref, mine_ref, _, out_ref, one_ref, two_ref,
+               ps_ref, done_ref, scaled_ref, sem, sems):
+        write_update(scaled_ref, mine_ref, one_ref, two_ref, sems, 0, False)
         fill = filler(ps_ref, channels, tap_masks(cells, vertical), vertical)
         planes = flip_planes(down_ref[...].reshape(2 * channels, cells), codes_ref[1, 0:1, 0:1], vertical)
         fill(0, planes[:channels])
@@ -314,27 +366,15 @@
         done_ref[1, :, :] = rest_ref[1] + y[:channels] + dot(weights[channels:], ps_ref[span:, :])
         copy = pltpu.make_async_copy(done_ref, out_ref.at[last - 1:count], sem)
         copy.start()
+        write_update(scaled_ref, mine_ref, one_ref, two_ref, sems, 0, True)
         copy.wait()
 
     return kernel
 
 
-def normalize_kernel(mine_ref, other_ref, one_ref, two_ref):
-    odd = lax.axis_index(AXIS) % 2
-
-    def scaled(ref):
-        v = ref[...]
-        return v / jnp.sqrt(jnp.mean(v * v) + 1e-06)
-
-    @pl.when(odd == 0)
-    def _():
-        one_ref[...] = scaled(mine_ref)
-        two_ref[...] = scaled(other_ref)
-
-    @pl.when(odd == 1)
-    def _():
-        one_ref[...] = scaled(other_ref)
-        two_ref[...] = scaled(mine_ref)
+def normalize_kernel(other_ref, _, __, one_ref, two_ref, scaled_ref, sems):
+    write_update(scaled_ref, other_ref, one_ref, two_ref, sems, 1, False)
+    write_update(scaled_ref, other_ref, one_ref, two_ref, sems, 1, True)
 
 
 VM = pl.BlockSpec(memory_space=pltpu.VMEM)
@@ -378,11 +418,15 @@
         make_interior_kernel(*sizes),
         (stack, band, band, edges, edges, columns, columns, shape(((count - 2) * span, cells), BF16), sums, sums),
         (x, g, first_weight, second_weight), "interior", [pltpu.VMEM(((count + 2) * channels, cells), BF16)])
-    keep, send, pg_edge, ps_edge = call(
+    two = shape((2 * channels, cells), BF16)
+    send, pg_edge, h_edge, low, cf = call(
         make_edge_kernel(*sizes),
-        (grads, grads, shape((2, channels, cells), BF16), shape((2 * span, cells), BF16)),
+        (grads, shape((2, channels, cells), BF16), two, two, shape((2 * span, cells), BF16)),
         (up, x, ws, band_one, band_two, codes, pre_edge, grad_edge, xs, cs, part_one, part_two), "edge",
         [pltpu.VMEM((3 * span, cells), BF16), pltpu.VMEM((span, cells), BF16), pltpu.VMEM((2 * span, cells), BF16)])
+    keep, ps_edge = call(
+        make_keep_kernel(channels, cells, vertical), (grads, shape((2 * span, cells), BF16)),
+        (x, codes, cs, part_one, part_two, pg_edge, h_edge, low, cf), "keep")
 
     def swap(value, bit):
         return lax.ppermute(value, AXIS, [(b, b ^ bit) for b in range(size)])
@@ -403,11 +447,15 @@
         if index == len(rounds) - 1:
             total, down = lax.optimization_barrier((total, down))
     other = swap(total, 1)
-    input_grad = call(
-        make_upper_kernel(*sizes), shape((count, channels, cells), F32), (down, codes, ws, rest, most_done), "upper_planes",
-        [pltpu.VMEM((2 * span, cells), BF16), pltpu.VMEM((2, channels, cells), F32), pltpu.SemaphoreType.DMA],
-        [VM, VM, VM, VM, HB], out_specs=HB, aliases={4: 0})
-    first, second = call(normalize_kernel, (grads, grads), (total, other), "normalize")
+    input_grad, first, second = call(
+        make_upper_kernel(*sizes), (shape((count, channels, cells), F32), grads, grads),
+        (down, codes, ws, rest, total, most_done), "upper_planes",
+        [pltpu.VMEM((2 * span, cells), BF16), pltpu.VMEM((2, channels, cells), F32), pltpu.VMEM(grads.shape, F32),
+         pltpu.SemaphoreType.DMA, pltpu.SemaphoreType.DMA((2,))],
+        [VM, VM, VM, VM, VM, HB], out_specs=(HB, HB, HB), aliases={5: 0})
+    first, second = call(
+        normalize_kernel, (grads, grads), (other, first, second), "normalize",
+        [pltpu.VMEM(grads.shape, F32), pltpu.SemaphoreType.DMA((2,))], [VM, HB, HB], out_specs=(HB, HB), aliases={1: 0, 2: 1})
     return (input_grad[None], first, second)
 
 

time: 31.7 us -> 31.7 us (level)
  waiting for transfers between devices: 9.12 us -> 8.31 us
  Pallas kernels: 9.87 us -> 10.6 us
    ppermute x2, waiting for transfers between devices: 0.97 us -> 0.16 us  [swap(): return lax.ppermute(value, AXIS, [(b, b ^ bit) for b in range(size)])]
    pallas_call x6 -> x7, Pallas kernels: 9.87 us -> 10.6 us  [call(): pl.pallas_call(kernel, out_shape=outs, in_specs=specs or [VM] * len(opera...]
  transfers between devices with their start and end apart: 7 -> 7, of which waited for: 5 -> 5; matrix products, arithmetic and copies ran while one was open for 0% -> 0% of each run, Pallas kernels for 20% -> 23%
where the time goes in v6:
time: 31.7 us; the launch traced here: 31.5 us
  starting transfers between devices  11.8 us (37%)
  Pallas kernels  10.6 us (33%)
  waiting for transfers between devices  8.31 us (26%)
  between operations  0.72 us (2%)
    pallas_call x7, Pallas kernels, call(): pl.pallas_call(kernel, out_shape=outs, in_specs=specs or [VM] * len(opera...  10.6 us
    ppermute x3, waiting for transfers between devices, body(): lax.ppermute(total, AXIS, [(b, b ^ choice[b % 2]) for b in range(size)])  7.22 us
    ppermute x2, starting transfers between devices, swap(): return lax.ppermute(value, AXIS, [(b, b ^ bit) for b in range(size)])  4.56 us
    ppermute x1, starting transfers between devices, body(): lax.ppermute(pg_sent, AXIS, [(b, (b - 1) % size) for b in range(size)])  3.57 us
    ppermute x1, starting transfers between devices, body(): up = lax.ppermute(up, AXIS, [(b, (b + 1) % size) for b in range(size)])  2.65 us
    ppermute x3, starting transfers between devices, body(): lax.ppermute(total, AXIS, [(b, b ^ choice[b % 2]) for b in range(size)])  1.05 us
    ppermute x1, waiting for transfers between devices, body(): lax.ppermute(pg_sent, AXIS, [(b, (b - 1) % size) for b in range(size)])  0.93 us
  transfers between devices with their start and end apart: 7, of which 5 were waited for; matrix products, arithmetic and copies ran while one was open for 0% of the time, Pallas kernels for 23%

profile of v6, /device:TPU:1, one launch (start us, length us, event | category | flops | bytes accessed | tf_op | source)
XLA Modules:
  0.0 31.5 jit_solution(17207149673602056056)
XLA Ops:
  0.6 1.1 %pack.1 = (bf16[4,32,512]{2,1,0:T(8,128)(2,1)S(1)}, s32[2,8,128]{2,1,0:T(8,128)S(1)}, bf16[8,32,512]{2,1,0:T(8,128)(2,1)S(1)}, bf16[8,32,512]{2,1,0:T(8,128)(2,1...) custom-call(s32[1,2]{1,0:T(1,128)} %codes_ref.1, bf16[8,32,512]{2,1,0:T(8,128)(2,1)} %bitcast.4, ...), custom_call_target="tpu_custom_call" | custom-call | tf_op jit(solution)/shard_map/pack/pallas_call | solution.py:392
  1.7 2.7 %collective-permute-start = (bf16[4,32,512]{2,1,0:T(8,128)(2,1)S(1)}, bf16[4,32,512]{2,1,0:T(8,128)(2,1)S(1)}, u32[]{:S(2)}, u32[]{:S(2)}) collective-permute-start(bf16[4,32,512]{2,1,0:T(8,128)(2,1)S(1)} %get-tuple-element.48), channel_id=1, source_target_pairs={{0,1},{1,2},{2,3},{3,4},{4,5},{5,6},{6,7},{7,8},{8,9},{9,10},{10,1... | collective-permute-start | bytes 393224 | tf_op jit(solution)/shard_map/ppermute | solution.py:414
  4.4 3.7 %interior.1 = (bf16[288,288]{1,0:T(8,128)(2,1)S(1)}, bf16[320,256]{1,0:T(8,128)(2,1)S(1)}, bf16[320,256]{1,0:T(8,128)(2,1)S(1)}, f32[2,32,512]{2,1,0:T(8,128)S(1...) custom-call(bf16[8,32,512]{2,1,0:T(8,128)(2,1)S(1)} %get-tuple-eleme, ...), custom_call_target="tpu_custom_call" | custom-call | tf_op jit(solution)/shard_map/interior/pallas_call | solution.py:392
  8.1 0.0 collective-permute-done.up_ref
  8.1 1.4 %edge.1 = (f32[32,864]{1,0:T(8,128)S(1)}, bf16[2,32,512]{2,1,0:T(8,128)(2,1)S(1)}, bf16[64,512]{1,0:T(8,128)(2,1)S(1)}, bf16[64,512]{1,0:T(8,128)(2,1)S(1)}, bf16[576,512]{1,0:T(8,128)(2,1)S(1)}) custom-call(bf16[4,32,512]{2,1,0:T(8,128)(2,1)S(1)} %collective-permute-done.up_ref, bf16[8,32,512]{2,1,0:T(8,128)(2,1)S(1)} %get-tuple-element.40.x_ref, ...), custom_call_target="tpu_custom_call" | custom-call | tf_op jit(solution)/shard_map/edge/pallas_call | solution.py:392
  9.5 1.9 %collective-permute-start.1 = (f32[32,864]{1,0:T(8,128)S(1)}, f32[32,864]{1,0:T(8,128)S(1)}, u32[]{:S(2)}, u32[]{:S(2)}) collective-permute-start(f32[32,864]{1,0:T(8,128)S(1)} %get-tuple-element.60), channel_id=1, source_target_pairs={{0,1},{1,0},{2,3},{3,2},{4,5},{5,4},{6,7},{7,6},{8,9},{9,8},{10,11... | collective-permute-start | bytes 331784 | tf_op jit(solution)/shard_map/ppermute | solution.py:432
  11.4 0.8 %keep.1 = (f32[32,864]{1,0:T(8,128)S(1)}, bf16[576,512]{1,0:T(8,128)(2,1)S(1)}) custom-call(bf16[8,32,512]{2,1,0:T(8,128)(2,1)S(1)} %get-tuple-element.40.x_ref, s32[2,8,128]{2,1,0:T(8,128)S(1)} %get-tuple-element.41.codes_ref, bf16[2304,512]{1,0:T(8,128)(2,1)S(1)} %get-tuple-element.45.cs_ref, f32[576,128]{1,0:T(8,128)S(1)} %get-tuple-element.46.g1_ref, ...), custom_call_target="tpu_custom_call" | custom-call | tf_op jit(solution)/shard_map/keep/pallas_call | solution.py:392
  12.2 0.2 collective-permute-done.1
  12.3 0.1 collective-permute-start.2
  12.4 3.6 %collective-permute-done.2 = f32[32,864]{1,0:T(8,128)S(1)} collective-permute-done((f32[32,864]{1,0:T(8,128)S(1)}, f32[32,864]{1,0:T(8,128)S(1)}, u32[]{:S(2)}, u32[]{:S(2)}) %collective-permute-start.2) | collective-permute-done | bytes 110624 | tf_op jit(solution)/shard_map/ppermute | solution.py:444
  16.1 0.1 collective-permute-start.3
  16.1 1.4 %input_grad.1 = (f32[8,32,512]{2,1,0:T(8,128)}, f32[2,32,512]{2,1,0:T(8,128)S(1)}) custom-call(bf16[1728,512]{1,0:T(8,128)(2,1)S(1)} %get-tuple-element.62.inner_ref, bf16[576,512]{1,0:T(8,128)(2,1)S(1)} %get-tuple-element.63.edge_ref, bf16[8,32,512]{2,1,0:T(8,128)(2,1)S(1)} %get-tuple-element.42.g_ref, bf16[288,288]{1,0:T(8,128)(2,1)S(1)} %get-tuple-element.49.ws_ref), custom_call_target="tpu_custom_call" | custom-call | tf_op jit(solution)/shard_map/input_grad/pallas_call | solution.py:392
  17.5 2.4 %collective-permute-done.3 = f32[32,864]{1,0:T(8,128)S(1)} collective-permute-done((f32[32,864]{1,0:T(8,128)S(1)}, f32[32,864]{1,0:T(8,128)S(1)}, u32[]{:S(2)}, u32[]{:S(2)}) %collective-permute-start.3) | collective-permute-done | bytes 110624 | tf_op jit(solution)/shard_map/ppermute | solution.py:444
  19.9 0.9 %collective-permute-start.4 = (f32[32,864]{1,0:T(8,128)S(1)}, f32[32,864]{1,0:T(8,128)S(1)}, u32[]{:S(2)}, u32[]{:S(2)}) collective-permute-start(f32[32,864]{1,0:T(8,128)S(1)} %add.14), channel_id=1, source_target_pairs={{0,4},{1,9},{2,6},{3,11},{4,0},{5,13},{6,2},{7,15},{8,12},{9,1},{1... | collective-permute-start | bytes 331784 | tf_op jit(solution)/shard_map/ppermute | solution.py:444
  20.8 3.6 %collective-permute-start.5 = (bf16[2,32,512]{2,1,0:T(8,128)(2,1)S(1)}, bf16[2,32,512]{2,1,0:T(8,128)(2,1)S(1)}, u32[]{:S(2)}, u32[]{:S(2)}) collective-permute-start(bf16[2,32,512]{2,1,0:T(8,128)(2,1)S(1)} %get-tuple-element.67.pg_ref), channel_id=1, source_target_pairs={{0,15},{1,0},{2,1},{3,2},{4,3},{5,4},{6,5},{7,6},{8,7},{9,8},{10,9... | collective-permute-start | bytes 196616 | tf_op jit(solution)/shard_map/ppermute | solution.py:435
  24.4 1.2 %collective-permute-done.4 = f32[32,864]{1,0:T(8,128)S(1)} collective-permute-done((f32[32,864]{1,0:T(8,128)S(1)}, f32[32,864]{1,0:T(8,128)S(1)}, u32[]{:S(2)}, u32[]{:S(2)}) %collective-permute-start.4) | collective-permute-done | bytes 110624 | tf_op jit(solution)/shard_map/ppermute | solution.py:444
  25.6 0.9 %collective-permute-done.5.down_ref = bf16[2,32,512]{2,1,0:T(8,128)(2,1)S(1)} collective-permute-done((bf16[2,32,512]{2,1,0:T(8,128)(2,1)S(1)}, bf16[2,32,512]{2,1,0:T(8,128)(2,1)S(1)}, u32[]{:S(2)}, u32[]{:S(2)}) %collective-permute-start.5) | collective-permute-done | bytes 65568 | tf_op jit(solution)/shard_map/ppermute | solution.py:435
  26.5 2.7 %collective-permute-start.6 = (f32[32,864]{1,0:T(8,128)S(1)}, f32[32,864]{1,0:T(8,128)S(1)}, u32[]{:S(2)}, u32[]{:S(2)}) collective-permute-start(f32[32,864]{1,0:T(8,128)S(1)} %add.15.mine_ref), channel_id=1, source_target_pairs={{0,1},{1,0},{2,3},{3,2},{4,5},{5,4},{6,7},{7,6},{8,9},{9,8},{10,11... | collective-permute-start | bytes 331784 | tf_op jit(solution)/shard_map/ppermute | solution.py:432
  29.2 1.4 %upper_planes.1 = (f32[8,32,512]{2,1,0:T(8,128)}, f32[32,864]{1,0:T(8,128)}, f32[32,864]{1,0:T(8,128)}) custom-call(bf16[2,32,512]{2,1,0:T(8,128)(2,1)S(1)} %collective-permute-done.5.down_ref, s32[2,8,128]{2,1,0:T(8,128)S(1)} %get-tuple-element.41.codes_ref, bf16[288,288]{1,0:T(8,128)(2,1)S(1)} %get-tuple-element.49.ws_ref, ...), custom_call_target="tpu_custom_call", output_to_operand_aliasing={{0}: (5, {})} | custom-call | tf_op jit(solution)/shard_map/upper_planes/pallas_call | solution.py:392
  30.6 0.0 collective-permute-done.6.other_ref
  30.7 0.9 %normalize.1 = (f32[32,864]{1,0:T(8,128)}, f32[32,864]{1,0:T(8,128)}) custom-call(f32[32,864]{1,0:T(8,128)S(1)} %collective-permute-done.6.other_ref, f32[32,864]{1,0:T(8,128)} %get-tuple-element.73._, f32[32,864]{1,0:T(8,128)} %get-tuple-element.74.__), custom_call_target="tpu_custom_call", output_to_operand_aliasing={{0}: (1, {}), {1}: (2, {})} | custom-call | tf_op jit(solution)/shard_map/normalize/pallas_call | solution.py:392
  (4 shorter events, 0.1 us)
Async XLA Ops:
  1.7 6.4 %collective-permute-start = (bf16[4,32,512]{2,1,0:T(8,128)(2,1)S(1)}, bf16[4,32,512]{2,1,0:T(8,128)(2,1)S(1)}, u32[]{:S(2)}, u32[]{:S(2)}) collective-permute-start(bf16[4,32,512]{2,1,0:T(8,128)(2,1)S(1)} %get-tuple-element.48), channel_id=1, source_target_pairs={{0,1},{1,2},{2,3},{3,4},{4,5},{5,6},{6,7},{7,8},{8,9},{9,10},{10,1... | collective-permute-start | bytes 393224 | tf_op jit(solution)/shard_map/ppermute | solution.py:414
  9.5 2.8 %collective-permute-start.1 = (f32[32,864]{1,0:T(8,128)S(1)}, f32[32,864]{1,0:T(8,128)S(1)}, u32[]{:S(2)}, u32[]{:S(2)}) collective-permute-start(f32[32,864]{1,0:T(8,128)S(1)} %get-tuple-element.60), channel_id=1, source_target_pairs={{0,1},{1,0},{2,3},{3,2},{4,5},{5,4},{6,7},{7,6},{8,9},{9,8},{10,11... | collective-permute-start | bytes 331784 | tf_op jit(solution)/shard_map/ppermute | solution.py:432
  12.3 3.7 %collective-permute-start.2 = (f32[32,864]{1,0:T(8,128)S(1)}, f32[32,864]{1,0:T(8,128)S(1)}, u32[]{:S(2)}, u32[]{:S(2)}) collective-permute-start(f32[32,864]{1,0:T(8,128)S(1)} %add.12), channel_id=1, source_target_pairs={{0,8},{1,3},{2,10},{3,1},{4,12},{5,7},{6,14},{7,5},{8,0},{9,11},{1... | collective-permute-start | bytes 331784 | tf_op jit(solution)/shard_map/ppermute | solution.py:444
  16.1 3.8 %collective-permute-start.3 = (f32[32,864]{1,0:T(8,128)S(1)}, f32[32,864]{1,0:T(8,128)S(1)}, u32[]{:S(2)}, u32[]{:S(2)}) collective-permute-start(f32[32,864]{1,0:T(8,128)S(1)} %add.13), channel_id=1, source_target_pairs={{0,2},{1,5},{2,0},{3,7},{4,6},{5,1},{6,4},{7,3},{8,10},{9,13},{10,... | collective-permute-start | bytes 331784 | tf_op jit(solution)/shard_map/ppermute | solution.py:444
  19.9 5.7 %collective-permute-start.4 = (f32[32,864]{1,0:T(8,128)S(1)}, f32[32,864]{1,0:T(8,128)S(1)}, u32[]{:S(2)}, u32[]{:S(2)}) collective-permute-start(f32[32,864]{1,0:T(8,128)S(1)} %add.14), channel_id=1, source_target_pairs={{0,4},{1,9},{2,6},{3,11},{4,0},{5,13},{6,2},{7,15},{8,12},{9,1},{1... | collective-permute-start | bytes 331784 | tf_op jit(solution)/shard_map/ppermute | solution.py:444
  20.8 5.7 %collective-permute-start.5 = (bf16[2,32,512]{2,1,0:T(8,128)(2,1)S(1)}, bf16[2,32,512]{2,1,0:T(8,128)(2,1)S(1)}, u32[]{:S(2)}, u32[]{:S(2)}) collective-permute-start(bf16[2,32,512]{2,1,0:T(8,128)(2,1)S(1)} %get-tuple-element.67.pg_ref), channel_id=1, source_target_pairs={{0,15},{1,0},{2,1},{3,2},{4,3},{5,4},{6,5},{7,6},{8,7},{9,8},{10,9... | collective-permute-start | bytes 196616 | tf_op jit(solution)/shard_map/ppermute | solution.py:435
  26.5 4.1 %collective-permute-start.6 = (f32[32,864]{1,0:T(8,128)S(1)}, f32[32,864]{1,0:T(8,128)S(1)}, u32[]{:S(2)}, u32[]{:S(2)}) collective-permute-start(f32[32,864]{1,0:T(8,128)S(1)} %add.15.mine_ref), channel_id=1, source_target_pairs={{0,1},{1,0},{2,3},{3,2},{4,5},{5,4},{6,7},{7,6},{8,9},{9,8},{10,11... | collective-permute-start | bytes 331784 | tf_op jit(solution)/shard_map/ppermute | solution.py:432

commit v7 on v6

--- a/solution.py
+++ b/solution.py
@@ -116,6 +116,15 @@
     return kernel
 
 
+def stack_adjoint(weight_ref, out_ref, base, channels):
+    turned = weight_ref[...].astype(F32).T
+    for step in range(3):
+        for place, tap in enumerate(ORDER):
+            at = (9 * (2 - step) + 8 - tap) * channels
+            out_ref[base + step * channels:base + (step + 1) * channels,
+                    place * channels:(place + 1) * channels] = turned[at:at + channels, :].astype(BF16)
+
+
 def make_interior_kernel(count, channels, cells, vertical):
     span = 9 * channels
     most = 8 * channels
@@ -132,13 +141,7 @@
             ws_ref[rows, 0:half] = w1_ref[:, base:base + half]
             ws_ref[rows, half:most] = w1_ref[:, base + half + channels:base + span]
             ws_ref[rows, most:span] = w1_ref[:, base + half:base + half + channels]
-        for weight_ref, base in ((w2_ref, wide), (w1_ref, 2 * wide)):
-            turned = weight_ref[...].astype(F32).T
-            for step in range(3):
-                for place, tap in enumerate(ORDER):
-                    at = (9 * (2 - step) + 8 - tap) * channels
-                    ws_ref[base + step * channels:base + (step + 1) * channels,
-                           place * channels:(place + 1) * channels] = turned[at:at + channels, :].astype(BF16)
+        stack_adjoint(w2_ref, ws_ref, wide, channels)
         for ref, base in ((t1_ref, 0), (t2_ref, wide)):
             ref[...] = jnp.zeros_like(ref)
             for step in range(3):
@@ -304,8 +307,9 @@
     wide = 3 * channels
     last = count - 1
 
-    def kernel(inner_ref, edge_ref, g_ref, ws_ref, out_ref, rest_ref, done_ref, sems):
-        weights = ws_ref[2 * wide:3 * wide, :]
+    def kernel(inner_ref, edge_ref, g_ref, w1_ref, out_ref, rest_ref, ws_ref, done_ref, sems):
+        stack_adjoint(w1_ref, ws_ref, 0, channels)
+        weights = ws_ref[...]
         total = {}
         copies = []
         for a in range(-1, last):
@@ -360,7 +364,7 @@
         planes = flip_planes(down_ref[...].reshape(2 * channels, cells), codes_ref[1, 0:1, 0:1], vertical)
         fill(0, planes[:channels])
         fill(1, planes[channels:], flipped_places(codes_ref[1, 0, 0]))
-        weights = ws_ref[2 * wide + channels:3 * wide, :]
+        weights = ws_ref[channels:3 * channels, :]
         y = dot(weights, ps_ref[0:span, :])
         done_ref[0, :, :] = rest_ref[0] + y[channels:]
         done_ref[1, :, :] = rest_ref[1] + y[:channels] + dot(weights[channels:], ps_ref[span:, :])
@@ -398,7 +402,7 @@
     span = 9 * channels
     shape = jax.ShapeDtypeStruct
     sizes = (count, channels, cells, vertical)
-    stack = shape((span, span), BF16)
+    stack = shape((6 * channels, span), BF16)
     band = shape(((count + 2) * channels, count * channels), BF16)
     edges = shape((2, channels, cells), F32)
     columns = shape((count * span, cells), BF16)
@@ -433,23 +437,23 @@
 
     total, pg_sent = lax.optimization_barrier((keep + swap(send, 1), pg_edge))
     down = lax.ppermute(pg_sent, AXIS, [(b, (b - 1) % size) for b in range(size)])
-    most_done, rest = call(
-        make_input_kernel(*sizes), (shape((count, channels, cells), F32), edges),
-        (ps, ps_edge, g, ws), "input_grad",
+    most_done, rest, back = call(
+        make_input_kernel(*sizes), (shape((count, channels, cells), F32), edges, shape((3 * channels, span), BF16)),
+        (ps, ps_edge, g, first_weight), "input_grad",
         [pltpu.VMEM((count - 2, channels, cells), F32),
-         pltpu.SemaphoreType.DMA((count - 2,))], out_specs=(HB, VM))
+         pltpu.SemaphoreType.DMA((count - 2,))], out_specs=(HB, VM, VM))
     bits = [1 << power for power in range(1, size.bit_length() - 1)]
     rounds = list(zip(bits[-1:] + bits[:-1], bits))
     for index, choice in enumerate(rounds):
         total = total + lax.ppermute(total, AXIS, [(b, b ^ choice[b % 2]) for b in range(size)])
         if index == len(rounds) - 2:
-            total, most_done, rest = lax.optimization_barrier((total, most_done, rest))
+            total, most_done, rest, back = lax.optimization_barrier((total, most_done, rest, back))
         if index == len(rounds) - 1:
             total, down = lax.optimization_barrier((total, down))
     other = swap(total, 1)
     input_grad, first, second = call(
         make_upper_kernel(*sizes), (shape((count, channels, cells), F32), grads, grads),
-        (down, codes, ws, rest, total, most_done), "upper_planes",
+        (down, codes, back, rest, total, most_done), "upper_planes",
         [pltpu.VMEM((2 * span, cells), BF16), pltpu.VMEM((2, channels, cells), F32), pltpu.VMEM(grads.shape, F32),
          pltpu.SemaphoreType.DMA, pltpu.SemaphoreType.DMA((2,))],
         [VM, VM, VM, VM, VM, HB], out_specs=(HB, HB, HB), aliases={5: 0})

time: 31.7 us -> 31.7 us (level)
  transfers between devices with their start and end apart: 7 -> 7, of which waited for: 5 -> 5; matrix products, arithmetic and copies ran while one was open for 0% -> 0% of each run, Pallas kernels for 23% -> 24%
where the time goes in v7:
time: 31.7 us; the launch traced here: 31.5 us
  starting transfers between devices  12 us (38%)
  Pallas kernels  10.8 us (34%)
  waiting for transfers between devices  8.01 us (25%)
  between operations  0.73 us (2%)
    pallas_call x7, Pallas kernels, call(): pl.pallas_call(kernel, out_shape=outs, in_specs=specs or [VM] * len(opera...  10.8 us
    ppermute x3, waiting for transfers between devices, body(): lax.ppermute(total, AXIS, [(b, b ^ choice[b % 2]) for b in range(size)])  7 us
    ppermute x2, starting transfers between devices, swap(): return lax.ppermute(value, AXIS, [(b, b ^ bit) for b in range(size)])  4.7 us
    ppermute x1, starting transfers between devices, body(): lax.ppermute(pg_sent, AXIS, [(b, (b - 1) % size) for b in range(size)])  3.57 us
    ppermute x1, starting transfers between devices, body(): up = lax.ppermute(up, AXIS, [(b, (b + 1) % size) for b in range(size)])  2.65 us
    ppermute x3, starting transfers between devices, body(): lax.ppermute(total, AXIS, [(b, b ^ choice[b % 2]) for b in range(size)])  1.05 us
    ppermute x1, waiting for transfers between devices, body(): lax.ppermute(pg_sent, AXIS, [(b, (b - 1) % size) for b in range(size)])  0.85 us
  transfers between devices with their start and end apart: 7, of which 5 were waited for; matrix products, arithmetic and copies ran while one was open for 0% of the time, Pallas kernels for 24%

profile of v7, /device:TPU:1, one launch (start us, length us, event | category | flops | bytes accessed | tf_op | source)
XLA Modules:
  0.0 31.5 jit_solution(16206381910470393906)
XLA Ops:
  0.6 1.1 %pack.1 = (bf16[4,32,512]{2,1,0:T(8,128)(2,1)S(1)}, s32[2,8,128]{2,1,0:T(8,128)S(1)}, bf16[8,32,512]{2,1,0:T(8,128)(2,1)S(1)}, bf16[8,32,512]{2,1,0:T(8,128)(2,1...) custom-call(s32[1,2]{1,0:T(1,128)} %codes_ref.1, bf16[8,32,512]{2,1,0:T(8,128)(2,1)} %bitcast.4, ...), custom_call_target="tpu_custom_call" | custom-call | tf_op jit(solution)/shard_map/pack/pallas_call | solution.py:396
  1.7 2.7 %collective-permute-start = (bf16[4,32,512]{2,1,0:T(8,128)(2,1)S(1)}, bf16[4,32,512]{2,1,0:T(8,128)(2,1)S(1)}, u32[]{:S(2)}, u32[]{:S(2)}) collective-permute-start(bf16[4,32,512]{2,1,0:T(8,128)(2,1)S(1)} %get-tuple-element.50), channel_id=1, source_target_pairs={{0,1},{1,2},{2,3},{3,4},{4,5},{5,6},{6,7},{7,8},{8,9},{9,10},{10,1... | collective-permute-start | bytes 393224 | tf_op jit(solution)/shard_map/ppermute | solution.py:418
  4.4 3.6 %interior.1 = (bf16[192,288]{1,0:T(8,128)(2,1)S(1)}, bf16[320,256]{1,0:T(8,128)(2,1)S(1)}, bf16[320,256]{1,0:T(8,128)(2,1)S(1)}, f32[2,32,512]{2,1,0:T(8,128)S(1...) custom-call(bf16[8,32,512]{2,1,0:T(8,128)(2,1)S(1)} %get-tuple-eleme, ...), custom_call_target="tpu_custom_call" | custom-call | tf_op jit(solution)/shard_map/interior/pallas_call | solution.py:396
  8.0 0.0 collective-permute-done.up_ref
  8.0 1.4 %edge.1 = (f32[32,864]{1,0:T(8,128)S(1)}, bf16[2,32,512]{2,1,0:T(8,128)(2,1)S(1)}, bf16[64,512]{1,0:T(8,128)(2,1)S(1)}, bf16[64,512]{1,0:T(8,128)(2,1)S(1)}, bf16[576,512]{1,0:T(8,128)(2,1)S(1)}) custom-call(bf16[4,32,512]{2,1,0:T(8,128)(2,1)S(1)} %collective-permute-done.up_ref, bf16[8,32,512]{2,1,0:T(8,128)(2,1)S(1)} %get-tuple-element.42.x_ref, ...), custom_call_target="tpu_custom_call" | custom-call | tf_op jit(solution)/shard_map/edge/pallas_call | solution.py:396
  9.4 1.9 %collective-permute-start.1 = (f32[32,864]{1,0:T(8,128)S(1)}, f32[32,864]{1,0:T(8,128)S(1)}, u32[]{:S(2)}, u32[]{:S(2)}) collective-permute-start(f32[32,864]{1,0:T(8,128)S(1)} %get-tuple-element.62), channel_id=1, source_target_pairs={{0,1},{1,0},{2,3},{3,2},{4,5},{5,4},{6,7},{7,6},{8,9},{9,8},{10,11... | collective-permute-start | bytes 331784 | tf_op jit(solution)/shard_map/ppermute | solution.py:436
  11.4 0.8 %keep.1 = (f32[32,864]{1,0:T(8,128)S(1)}, bf16[576,512]{1,0:T(8,128)(2,1)S(1)}) custom-call(bf16[8,32,512]{2,1,0:T(8,128)(2,1)S(1)} %get-tuple-element.42.x_ref, s32[2,8,128]{2,1,0:T(8,128)S(1)} %get-tuple-element.43.codes_ref, bf16[2304,512]{1,0:T(8,128)(2,1)S(1)} %get-tuple-element.47.cs_ref, f32[576,128]{1,0:T(8,128)S(1)} %get-tuple-element.48.g1_ref, ...), custom_call_target="tpu_custom_call" | custom-call | tf_op jit(solution)/shard_map/keep/pallas_call | solution.py:396
  12.2 0.2 collective-permute-done.1
  12.3 0.1 collective-permute-start.2
  12.4 3.6 %collective-permute-done.2 = f32[32,864]{1,0:T(8,128)S(1)} collective-permute-done((f32[32,864]{1,0:T(8,128)S(1)}, f32[32,864]{1,0:T(8,128)S(1)}, u32[]{:S(2)}, u32[]{:S(2)}) %collective-permute-start.2) | collective-permute-done | bytes 110624 | tf_op jit(solution)/shard_map/ppermute | solution.py:448
  16.1 0.1 collective-permute-start.3
  16.1 1.6 %input_grad.1 = (f32[8,32,512]{2,1,0:T(8,128)}, f32[2,32,512]{2,1,0:T(8,128)S(1)}, bf16[96,288]{1,0:T(8,128)(2,1)S(1)}) custom-call(bf16[1728,512]{1,0:T(8,128)(2,1)S(1)} %get-tuple-element.64.inner_ref, bf16[576,512]{1,0:T(8,128)(2,1)S(1)} %get-tuple-element.65.edge_ref, bf16[8,32,512]{2,1,0:T(8,128)(2,1)S(1)} %get-tuple-element.44.g_ref, ...), custom_call_target="tpu_custom_call" | custom-call | tf_op jit(solution)/shard_map/input_grad/pallas_call | solution.py:396
  17.7 2.2 %collective-permute-done.3 = f32[32,864]{1,0:T(8,128)S(1)} collective-permute-done((f32[32,864]{1,0:T(8,128)S(1)}, f32[32,864]{1,0:T(8,128)S(1)}, u32[]{:S(2)}, u32[]{:S(2)}) %collective-permute-start.3) | collective-permute-done | bytes 110624 | tf_op jit(solution)/shard_map/ppermute | solution.py:448
  19.9 0.9 %collective-permute-start.4 = (f32[32,864]{1,0:T(8,128)S(1)}, f32[32,864]{1,0:T(8,128)S(1)}, u32[]{:S(2)}, u32[]{:S(2)}) collective-permute-start(f32[32,864]{1,0:T(8,128)S(1)} %add.14), channel_id=1, source_target_pairs={{0,4},{1,9},{2,6},{3,11},{4,0},{5,13},{6,2},{7,15},{8,12},{9,1},{1... | collective-permute-start | bytes 331784 | tf_op jit(solution)/shard_map/ppermute | solution.py:448
  20.8 3.6 %collective-permute-start.5 = (bf16[2,32,512]{2,1,0:T(8,128)(2,1)S(1)}, bf16[2,32,512]{2,1,0:T(8,128)(2,1)S(1)}, u32[]{:S(2)}, u32[]{:S(2)}) collective-permute-start(bf16[2,32,512]{2,1,0:T(8,128)(2,1)S(1)} %get-tuple-element.70.pg_ref), channel_id=1, source_target_pairs={{0,15},{1,0},{2,1},{3,2},{4,3},{5,4},{6,5},{7,6},{8,7},{9,8},{10,9... | collective-permute-start | bytes 196616 | tf_op jit(solution)/shard_map/ppermute | solution.py:439
  24.4 1.2 %collective-permute-done.4 = f32[32,864]{1,0:T(8,128)S(1)} collective-permute-done((f32[32,864]{1,0:T(8,128)S(1)}, f32[32,864]{1,0:T(8,128)S(1)}, u32[]{:S(2)}, u32[]{:S(2)}) %collective-permute-start.4) | collective-permute-done | bytes 110624 | tf_op jit(solution)/shard_map/ppermute | solution.py:448
  25.6 0.8 %collective-permute-done.5.down_ref = bf16[2,32,512]{2,1,0:T(8,128)(2,1)S(1)} collective-permute-done((bf16[2,32,512]{2,1,0:T(8,128)(2,1)S(1)}, bf16[2,32,512]{2,1,0:T(8,128)(2,1)S(1)}, u32[]{:S(2)}, u32[]{:S(2)}) %collective-permute-start.5) | collective-permute-done | bytes 65568 | tf_op jit(solution)/shard_map/ppermute | solution.py:439
  26.5 2.8 %collective-permute-start.6 = (f32[32,864]{1,0:T(8,128)S(1)}, f32[32,864]{1,0:T(8,128)S(1)}, u32[]{:S(2)}, u32[]{:S(2)}) collective-permute-start(f32[32,864]{1,0:T(8,128)S(1)} %add.15.mine_ref), channel_id=1, source_target_pairs={{0,1},{1,0},{2,3},{3,2},{4,5},{5,4},{6,7},{7,6},{8,9},{9,8},{10,11... | collective-permute-start | bytes 331784 | tf_op jit(solution)/shard_map/ppermute | solution.py:436
  29.2 1.4 %upper_planes.1 = (f32[8,32,512]{2,1,0:T(8,128)}, f32[32,864]{1,0:T(8,128)}, f32[32,864]{1,0:T(8,128)}) custom-call(bf16[2,32,512]{2,1,0:T(8,128)(2,1)S(1)} %collective-permute-done.5.down_ref, s32[2,8,128]{2,1,0:T(8,128)S(1)} %get-tuple-element.43.codes_ref, bf16[96,288]{1,0:T(8,128)(2,1)S(1)} %get-tuple-element.72.ws_ref, ...), custom_call_target="tpu_custom_call", output_to_operand_aliasing={{0}: (5, {})} | custom-call | tf_op jit(solution)/shard_map/upper_planes/pallas_call | solution.py:396
  30.6 0.0 collective-permute-done.6.other_ref
  30.7 0.9 %normalize.1 = (f32[32,864]{1,0:T(8,128)}, f32[32,864]{1,0:T(8,128)}) custom-call(f32[32,864]{1,0:T(8,128)S(1)} %collective-permute-done.6.other_ref, f32[32,864]{1,0:T(8,128)} %get-tuple-element.77._, f32[32,864]{1,0:T(8,128)} %get-tuple-element.78.__), custom_call_target="tpu_custom_call", output_to_operand_aliasing={{0}: (1, {}), {1}: (2, {})} | custom-call | tf_op jit(solution)/shard_map/normalize/pallas_call | solution.py:396
  (4 shorter events, 0.1 us)
Async XLA Ops:
  1.7 6.3 %collective-permute-start = (bf16[4,32,512]{2,1,0:T(8,128)(2,1)S(1)}, bf16[4,32,512]{2,1,0:T(8,128)(2,1)S(1)}, u32[]{:S(2)}, u32[]{:S(2)}) collective-permute-start(bf16[4,32,512]{2,1,0:T(8,128)(2,1)S(1)} %get-tuple-element.50), channel_id=1, source_target_pairs={{0,1},{1,2},{2,3},{3,4},{4,5},{5,6},{6,7},{7,8},{8,9},{9,10},{10,1... | collective-permute-start | bytes 393224 | tf_op jit(solution)/shard_map/ppermute | solution.py:418
  9.4 2.9 %collective-permute-start.1 = (f32[32,864]{1,0:T(8,128)S(1)}, f32[32,864]{1,0:T(8,128)S(1)}, u32[]{:S(2)}, u32[]{:S(2)}) collective-permute-start(f32[32,864]{1,0:T(8,128)S(1)} %get-tuple-element.62), channel_id=1, source_target_pairs={{0,1},{1,0},{2,3},{3,2},{4,5},{5,4},{6,7},{7,6},{8,9},{9,8},{10,11... | collective-permute-start | bytes 331784 | tf_op jit(solution)/shard_map/ppermute | solution.py:436
  12.3 3.7 %collective-permute-start.2 = (f32[32,864]{1,0:T(8,128)S(1)}, f32[32,864]{1,0:T(8,128)S(1)}, u32[]{:S(2)}, u32[]{:S(2)}) collective-permute-start(f32[32,864]{1,0:T(8,128)S(1)} %add.12), channel_id=1, source_target_pairs={{0,8},{1,3},{2,10},{3,1},{4,12},{5,7},{6,14},{7,5},{8,0},{9,11},{1... | collective-permute-start | bytes 331784 | tf_op jit(solution)/shard_map/ppermute | solution.py:448
  16.1 3.8 %collective-permute-start.3 = (f32[32,864]{1,0:T(8,128)S(1)}, f32[32,864]{1,0:T(8,128)S(1)}, u32[]{:S(2)}, u32[]{:S(2)}) collective-permute-start(f32[32,864]{1,0:T(8,128)S(1)} %add.13), channel_id=1, source_target_pairs={{0,2},{1,5},{2,0},{3,7},{4,6},{5,1},{6,4},{7,3},{8,10},{9,13},{10,... | collective-permute-start | bytes 331784 | tf_op jit(solution)/shard_map/ppermute | solution.py:448
  19.9 5.7 %collective-permute-start.4 = (f32[32,864]{1,0:T(8,128)S(1)}, f32[32,864]{1,0:T(8,128)S(1)}, u32[]{:S(2)}, u32[]{:S(2)}) collective-permute-start(f32[32,864]{1,0:T(8,128)S(1)} %add.14), channel_id=1, source_target_pairs={{0,4},{1,9},{2,6},{3,11},{4,0},{5,13},{6,2},{7,15},{8,12},{9,1},{1... | collective-permute-start | bytes 331784 | tf_op jit(solution)/shard_map/ppermute | solution.py:448
  20.8 5.6 %collective-permute-start.5 = (bf16[2,32,512]{2,1,0:T(8,128)(2,1)S(1)}, bf16[2,32,512]{2,1,0:T(8,128)(2,1)S(1)}, u32[]{:S(2)}, u32[]{:S(2)}) collective-permute-start(bf16[2,32,512]{2,1,0:T(8,128)(2,1)S(1)} %get-tuple-element.70.pg_ref), channel_id=1, source_target_pairs={{0,15},{1,0},{2,1},{3,2},{4,3},{5,4},{6,5},{7,6},{8,7},{9,8},{10,9... | collective-permute-start | bytes 196616 | tf_op jit(solution)/shard_map/ppermute | solution.py:439
  26.5 4.2 %collective-permute-start.6 = (f32[32,864]{1,0:T(8,128)S(1)}, f32[32,864]{1,0:T(8,128)S(1)}, u32[]{:S(2)}, u32[]{:S(2)}) collective-permute-start(f32[32,864]{1,0:T(8,128)S(1)} %add.15.mine_ref), channel_id=1, source_target_pairs={{0,1},{1,0},{2,3},{3,2},{4,5},{5,4},{6,7},{7,6},{8,9},{9,8},{10,11... | collective-permute-start | bytes 331784 | tf_op jit(solution)/shard_map/ppermute | solution.py:436

commit v8 on v6

--- a/solution.py
+++ b/solution.py
@@ -100,18 +100,14 @@
 
 
 def make_pack_kernel(count):
-    def kernel(codes_ref, x_ref, g_ref, w1_ref, w2_ref, up_ref, codes_out, x_out, g_out, w1_out, w2_out, scalars, sems):
-        moves = ((x_ref, x_out), (g_ref, g_out), (codes_ref, scalars), (w1_ref, w1_out), (w2_ref, w2_out))
+    def kernel(x_ref, g_ref, up_ref, x_out, g_out, sems):
+        moves = ((x_ref, x_out), (g_ref, g_out))
         copies = [pltpu.make_async_copy(*move, sems.at[index]) for index, move in enumerate(moves)]
         for copy in copies:
             copy.start()
         for index, field in enumerate((x_out, g_out)):
             copies[index].wait()
             up_ref[2 * index:2 * index + 2, :, :] = field[count - 2:count]
-        for copy in copies[2:]:
-            copy.wait()
-        for side in range(2):
-            codes_out[side, :, :] = jnp.full((8, 128), scalars[0, side], jnp.int32)
 
     return kernel
 
@@ -122,9 +118,25 @@
     wide = 3 * channels
     last = count - 1
 
-    def kernel(x_ref, g_ref, w1_ref, w2_ref,
-               ws_ref, t1_ref, t2_ref, pe_ref, ge_ref, xs_ref, cs_ref, ps_ref, g1_ref, g2_ref, h_ref):
+    def kernel(x_ref, g_ref, codes_hbm, w1_hbm, w2_hbm,
+               codes_ref, ws_ref, t1_ref, t2_ref, pe_ref, ge_ref, xs_ref, cs_ref, ps_ref, g1_ref, g2_ref, h_ref,
+               scalars, w1_ref, w2_ref, sems):
+        moves = ((codes_hbm, scalars), (w1_hbm, w1_ref), (w2_hbm, w2_ref))
+        copies = [pltpu.make_async_copy(*move, sems.at[index]) for index, move in enumerate(moves)]
+        for copy in copies:
+            copy.start()
         masks = tap_masks(cells, vertical)
+        fill_x = filler(xs_ref, channels, masks, vertical)
+        fill_g = filler(cs_ref, channels, masks, vertical)
+        fill_p = filler(ps_ref, channels, masks, vertical)
+        for a in range(count):
+            fill_x(a, x_ref[a])
+            fill_g(a, g_ref[a])
+
+        for copy in copies:
+            copy.wait()
+        for side in range(2):
+            codes_ref[side, :, :] = jnp.full((8, 128), scalars[0, side], jnp.int32)
         for step in range(3):
             rows = slice(step * channels, (step + 1) * channels)
             base = step * span
@@ -146,13 +158,6 @@
                 for a in range(count):
                     row = (a + 2 - step) * channels
                     ref[row:row + channels, a * channels:(a + 1) * channels] = centre
-
-        fill_x = filler(xs_ref, channels, masks, vertical)
-        fill_g = filler(cs_ref, channels, masks, vertical)
-        fill_p = filler(ps_ref, channels, masks, vertical)
-        for a in range(count):
-            fill_x(a, x_ref[a])
-            fill_g(a, g_ref[a])
 
         h_ref[...] = jnp.zeros_like(h_ref)
         pre_all = dot(t1_ref[...], x_ref[...].reshape(count * channels, cells))
@@ -406,18 +411,21 @@
     weight = shape(first_weight.shape, BF16)
     pinned = [
         pltpu.with_memory_space_constraint(v, pltpu.HBM) for v in (face_codes, x, g, first_weight, second_weight)]
-    up, codes, x, g, first_weight, second_weight = call(
+    face_codes, x, g, first_weight, second_weight = pinned
+    up, x, g = call(
         make_pack_kernel(count),
-        (shape((4, channels, cells), BF16), shape((2, 8, 128), jnp.int32), shape(x.shape, BF16), shape(x.shape, BF16),
-         weight, weight),
-        pinned, "pack", [pltpu.SMEM((1, 2), jnp.int32), pltpu.SemaphoreType.DMA((5,))], [HB] * 5)
+        (shape((4, channels, cells), BF16), shape(x.shape, BF16), shape(x.shape, BF16)),
+        (x, g), "pack", [pltpu.SemaphoreType.DMA((2,))], [HB] * 2)
     up = lax.ppermute(up, AXIS, [(b, (b + 1) % size) for b in range(size)])
 
     sums = shape((2 * span, 4 * channels), F32)
-    ws, band_one, band_two, pre_edge, grad_edge, xs, cs, ps, part_one, part_two = call(
+    codes, ws, band_one, band_two, pre_edge, grad_edge, xs, cs, ps, part_one, part_two = call(
         make_interior_kernel(*sizes),
-        (stack, band, band, edges, edges, columns, columns, shape(((count - 2) * span, cells), BF16), sums, sums),
-        (x, g, first_weight, second_weight), "interior", [pltpu.VMEM(((count + 2) * channels, cells), BF16)])
+        (shape((2, 8, 128), jnp.int32), stack, band, band, edges, edges, columns, columns, shape(((count - 2) * span, cells), BF16), sums, sums),
+        (x, g, face_codes, first_weight, second_weight), "interior",
+        [pltpu.VMEM(((count + 2) * channels, cells), BF16), pltpu.SMEM((1, 2), jnp.int32),
+         pltpu.VMEM(weight.shape, BF16), pltpu.VMEM(weight.shape, BF16), pltpu.SemaphoreType.DMA((3,))],
+        [VM, VM, HB, HB, HB])
     two = shape((2 * channels, cells), BF16)
     send, pg_edge, h_edge, low, cf = call(
         make_edge_kernel(*sizes),

time: 31.7 us -> 31.6 us (level)
  no operation moved by 1% of the time
where the time goes in v8:
time: 31.6 us; the launch traced here: 31.5 us
  starting transfers between devices  12.1 us (38%)
  Pallas kernels  10.4 us (33%)
  waiting for transfers between devices  8.19 us (26%)
  between operations  0.73 us (2%)
    pallas_call x7, Pallas kernels, call(): pl.pallas_call(kernel, out_shape=outs, in_specs=specs or [VM] * len(opera...  10.4 us
    ppermute x3, waiting for transfers between devices, body(): lax.ppermute(total, AXIS, [(b, b ^ choice[b % 2]) for b in range(size)])  7.23 us
    ppermute x2, starting transfers between devices, swap(): return lax.ppermute(value, AXIS, [(b, b ^ bit) for b in range(size)])  4.8 us
    ppermute x1, starting transfers between devices, body(): lax.ppermute(pg_sent, AXIS, [(b, (b - 1) % size) for b in range(size)])  3.57 us
    ppermute x1, starting transfers between devices, body(): up = lax.ppermute(up, AXIS, [(b, (b + 1) % size) for b in range(size)])  2.65 us
    ppermute x3, starting transfers between devices, body(): lax.ppermute(total, AXIS, [(b, b ^ choice[b % 2]) for b in range(size)])  1.05 us
    ppermute x1, waiting for transfers between devices, body(): lax.ppermute(pg_sent, AXIS, [(b, (b - 1) % size) for b in range(size)])  0.8 us
  transfers between devices with their start and end apart: 7, of which 5 were waited for; matrix products, arithmetic and copies ran while one was open for 0% of the time, Pallas kernels for 23%

profile of v8, /device:TPU:1, one launch (start us, length us, event | category | flops | bytes accessed | tf_op | source)
XLA Modules:
  0.0 31.5 jit_solution(4392070792026812741)
XLA Ops:
  0.6 1.1 %pack.1 = (bf16[4,32,512]{2,1,0:T(8,128)(2,1)S(1)}, bf16[8,32,512]{2,1,0:T(8,128)(2,1)S(1)}, bf16[8,32,512]{2,1,0:T(8,128)(2,1)S(1)}) custom-call(bf16[8,32,512]{2,1,0:T(8,128)(2,1)} %bitcast.4, bf16[8,32,512]{2,1,0:T(8,128)(2,1)} %bitcast.5), custom_call_target="tpu_custom_call" | custom-call | tf_op jit(solution)/shard_map/pack/pallas_call | solution.py:397
  1.7 2.7 %collective-permute-start = (bf16[4,32,512]{2,1,0:T(8,128)(2,1)S(1)}, bf16[4,32,512]{2,1,0:T(8,128)(2,1)S(1)}, u32[]{:S(2)}, u32[]{:S(2)}) collective-permute-start(bf16[4,32,512]{2,1,0:T(8,128)(2,1)S(1)} %get-tuple-element.44), channel_id=1, source_target_pairs={{0,1},{1,2},{2,3},{3,4},{4,5},{5,6},{6,7},{7,8},{8,9},{9,10},{10,1... | collective-permute-start | bytes 393224 | tf_op jit(solution)/shard_map/ppermute | solution.py:419
  4.3 3.6 %interior.1 = (s32[2,8,128]{2,1,0:T(8,128)S(1)}, bf16[288,288]{1,0:T(8,128)(2,1)S(1)}, bf16[320,256]{1,0:T(8,128)(2,1)S(1)}, bf16[320,256]{1,0:T(8,128)(2,1)S(1)...) custom-call(bf16[8,32,512]{2,1,0:T(8,128)(2,1)S(1)} %get-tuple-eleme, ...), custom_call_target="tpu_custom_call" | custom-call | tf_op jit(solution)/shard_map/interior/pallas_call | solution.py:397
  7.9 0.0 collective-permute-done.up_ref
  7.9 1.4 %edge.1 = (f32[32,864]{1,0:T(8,128)S(1)}, bf16[2,32,512]{2,1,0:T(8,128)(2,1)S(1)}, bf16[64,512]{1,0:T(8,128)(2,1)S(1)}, bf16[64,512]{1,0:T(8,128)(2,1)S(1)}, bf16[576,512]{1,0:T(8,128)(2,1)S(1)}) custom-call(bf16[4,32,512]{2,1,0:T(8,128)(2,1)S(1)} %collective-permute-done.up_ref, bf16[8,32,512]{2,1,0:T(8,128)(2,1)S(1)} %get-tuple-element.38.x_ref, ...), custom_call_target="tpu_custom_call" | custom-call | tf_op jit(solution)/shard_map/edge/pallas_call | solution.py:397
  9.3 2.0 %collective-permute-start.1 = (f32[32,864]{1,0:T(8,128)S(1)}, f32[32,864]{1,0:T(8,128)S(1)}, u32[]{:S(2)}, u32[]{:S(2)}) collective-permute-start(f32[32,864]{1,0:T(8,128)S(1)} %get-tuple-element.56), channel_id=1, source_target_pairs={{0,1},{1,0},{2,3},{3,2},{4,5},{5,4},{6,7},{7,6},{8,9},{9,8},{10,11... | collective-permute-start | bytes 331784 | tf_op jit(solution)/shard_map/ppermute | solution.py:440
  11.3 0.8 %keep.1 = (f32[32,864]{1,0:T(8,128)S(1)}, bf16[576,512]{1,0:T(8,128)(2,1)S(1)}) custom-call(bf16[8,32,512]{2,1,0:T(8,128)(2,1)S(1)} %get-tuple-element.38.x_ref, s32[2,8,128]{2,1,0:T(8,128)S(1)} %get-tuple-element.40.codes_ref, bf16[2304,512]{1,0:T(8,128)(2,1)S(1)} %get-tuple-element.41.cs_ref, f32[576,128]{1,0:T(8,128)S(1)} %get-tuple-element.42.g1_ref, ...), custom_call_target="tpu_custom_call" | custom-call | tf_op jit(solution)/shard_map/keep/pallas_call | solution.py:397
  12.1 0.2 collective-permute-done.1
  12.3 0.1 collective-permute-start.2
  12.4 3.6 %collective-permute-done.2 = f32[32,864]{1,0:T(8,128)S(1)} collective-permute-done((f32[32,864]{1,0:T(8,128)S(1)}, f32[32,864]{1,0:T(8,128)S(1)}, u32[]{:S(2)}, u32[]{:S(2)}) %collective-permute-start.2) | collective-permute-done | bytes 110624 | tf_op jit(solution)/shard_map/ppermute | solution.py:452
  16.0 0.1 collective-permute-start.3
  16.1 1.3 %input_grad.1 = (f32[8,32,512]{2,1,0:T(8,128)}, f32[2,32,512]{2,1,0:T(8,128)S(1)}) custom-call(bf16[1728,512]{1,0:T(8,128)(2,1)S(1)} %get-tuple-element.58.inner_ref, bf16[576,512]{1,0:T(8,128)(2,1)S(1)} %get-tuple-element.59.edge_ref, bf16[8,32,512]{2,1,0:T(8,128)(2,1)S(1)} %get-tuple-element.39.g_ref, bf16[288,288]{1,0:T(8,128)(2,1)S(1)} %get-tuple-element.45.ws_ref), custom_call_target="tpu_custom_call" | custom-call | tf_op jit(solution)/shard_map/input_grad/pallas_call | solution.py:397
  17.5 2.4 %collective-permute-done.3 = f32[32,864]{1,0:T(8,128)S(1)} collective-permute-done((f32[32,864]{1,0:T(8,128)S(1)}, f32[32,864]{1,0:T(8,128)S(1)}, u32[]{:S(2)}, u32[]{:S(2)}) %collective-permute-start.3) | collective-permute-done | bytes 110624 | tf_op jit(solution)/shard_map/ppermute | solution.py:452
  19.9 0.9 %collective-permute-start.4 = (f32[32,864]{1,0:T(8,128)S(1)}, f32[32,864]{1,0:T(8,128)S(1)}, u32[]{:S(2)}, u32[]{:S(2)}) collective-permute-start(f32[32,864]{1,0:T(8,128)S(1)} %add.14), channel_id=1, source_target_pairs={{0,4},{1,9},{2,6},{3,11},{4,0},{5,13},{6,2},{7,15},{8,12},{9,1},{1... | collective-permute-start | bytes 331784 | tf_op jit(solution)/shard_map/ppermute | solution.py:452
  20.8 3.6 %collective-permute-start.5 = (bf16[2,32,512]{2,1,0:T(8,128)(2,1)S(1)}, bf16[2,32,512]{2,1,0:T(8,128)(2,1)S(1)}, u32[]{:S(2)}, u32[]{:S(2)}) collective-permute-start(bf16[2,32,512]{2,1,0:T(8,128)(2,1)S(1)} %get-tuple-element.63.pg_ref), channel_id=1, source_target_pairs={{0,15},{1,0},{2,1},{3,2},{4,3},{5,4},{6,5},{7,6},{8,7},{9,8},{10,9... | collective-permute-start | bytes 196616 | tf_op jit(solution)/shard_map/ppermute | solution.py:443
  24.4 1.2 %collective-permute-done.4 = f32[32,864]{1,0:T(8,128)S(1)} collective-permute-done((f32[32,864]{1,0:T(8,128)S(1)}, f32[32,864]{1,0:T(8,128)S(1)}, u32[]{:S(2)}, u32[]{:S(2)}) %collective-permute-start.4) | collective-permute-done | bytes 110624 | tf_op jit(solution)/shard_map/ppermute | solution.py:452
  25.6 0.8 %collective-permute-done.5.down_ref = bf16[2,32,512]{2,1,0:T(8,128)(2,1)S(1)} collective-permute-done((bf16[2,32,512]{2,1,0:T(8,128)(2,1)S(1)}, bf16[2,32,512]{2,1,0:T(8,128)(2,1)S(1)}, u32[]{:S(2)}, u32[]{:S(2)}) %collective-permute-start.5) | collective-permute-done | bytes 65568 | tf_op jit(solution)/shard_map/ppermute | solution.py:443
  26.4 2.8 %collective-permute-start.6 = (f32[32,864]{1,0:T(8,128)S(1)}, f32[32,864]{1,0:T(8,128)S(1)}, u32[]{:S(2)}, u32[]{:S(2)}) collective-permute-start(f32[32,864]{1,0:T(8,128)S(1)} %add.15.mine_ref), channel_id=1, source_target_pairs={{0,1},{1,0},{2,3},{3,2},{4,5},{5,4},{6,7},{7,6},{8,9},{9,8},{10,11... | collective-permute-start | bytes 331784 | tf_op jit(solution)/shard_map/ppermute | solution.py:440
  29.2 1.4 %upper_planes.1 = (f32[8,32,512]{2,1,0:T(8,128)}, f32[32,864]{1,0:T(8,128)}, f32[32,864]{1,0:T(8,128)}) custom-call(bf16[2,32,512]{2,1,0:T(8,128)(2,1)S(1)} %collective-permute-done.5.down_ref, s32[2,8,128]{2,1,0:T(8,128)S(1)} %get-tuple-element.40.codes_ref, bf16[288,288]{1,0:T(8,128)(2,1)S(1)} %get-tuple-element.45.ws_ref, ...), custom_call_target="tpu_custom_call", output_to_operand_aliasing={{0}: (5, {})} | custom-call | tf_op jit(solution)/shard_map/upper_planes/pallas_call | solution.py:397
  30.6 0.0 collective-permute-done.6.other_ref
  30.6 0.9 %normalize.1 = (f32[32,864]{1,0:T(8,128)}, f32[32,864]{1,0:T(8,128)}) custom-call(f32[32,864]{1,0:T(8,128)S(1)} %collective-permute-done.6.other_ref, f32[32,864]{1,0:T(8,128)} %get-tuple-element.69._, f32[32,864]{1,0:T(8,128)} %get-tuple-element.70.__), custom_call_target="tpu_custom_call", output_to_operand_aliasing={{0}: (1, {}), {1}: (2, {})} | custom-call | tf_op jit(solution)/shard_map/normalize/pallas_call | solution.py:397
  (4 shorter events, 0.1 us)
Async XLA Ops:
  1.7 6.2 %collective-permute-start = (bf16[4,32,512]{2,1,0:T(8,128)(2,1)S(1)}, bf16[4,32,512]{2,1,0:T(8,128)(2,1)S(1)}, u32[]{:S(2)}, u32[]{:S(2)}) collective-permute-start(bf16[4,32,512]{2,1,0:T(8,128)(2,1)S(1)} %get-tuple-element.44), channel_id=1, source_target_pairs={{0,1},{1,2},{2,3},{3,4},{4,5},{5,6},{6,7},{7,8},{8,9},{9,10},{10,1... | collective-permute-start | bytes 393224 | tf_op jit(solution)/shard_map/ppermute | solution.py:419
  9.3 3.0 %collective-permute-start.1 = (f32[32,864]{1,0:T(8,128)S(1)}, f32[32,864]{1,0:T(8,128)S(1)}, u32[]{:S(2)}, u32[]{:S(2)}) collective-permute-start(f32[32,864]{1,0:T(8,128)S(1)} %get-tuple-element.56), channel_id=1, source_target_pairs={{0,1},{1,0},{2,3},{3,2},{4,5},{5,4},{6,7},{7,6},{8,9},{9,8},{10,11... | collective-permute-start | bytes 331784 | tf_op jit(solution)/shard_map/ppermute | solution.py:440
  12.3 3.7 %collective-permute-start.2 = (f32[32,864]{1,0:T(8,128)S(1)}, f32[32,864]{1,0:T(8,128)S(1)}, u32[]{:S(2)}, u32[]{:S(2)}) collective-permute-start(f32[32,864]{1,0:T(8,128)S(1)} %add.12), channel_id=1, source_target_pairs={{0,8},{1,3},{2,10},{3,1},{4,12},{5,7},{6,14},{7,5},{8,0},{9,11},{1... | collective-permute-start | bytes 331784 | tf_op jit(solution)/shard_map/ppermute | solution.py:452
  16.0 3.8 %collective-permute-start.3 = (f32[32,864]{1,0:T(8,128)S(1)}, f32[32,864]{1,0:T(8,128)S(1)}, u32[]{:S(2)}, u32[]{:S(2)}) collective-permute-start(f32[32,864]{1,0:T(8,128)S(1)} %add.13), channel_id=1, source_target_pairs={{0,2},{1,5},{2,0},{3,7},{4,6},{5,1},{6,4},{7,3},{8,10},{9,13},{10,... | collective-permute-start | bytes 331784 | tf_op jit(solution)/shard_map/ppermute | solution.py:452
  19.9 5.7 %collective-permute-start.4 = (f32[32,864]{1,0:T(8,128)S(1)}, f32[32,864]{1,0:T(8,128)S(1)}, u32[]{:S(2)}, u32[]{:S(2)}) collective-permute-start(f32[32,864]{1,0:T(8,128)S(1)} %add.14), channel_id=1, source_target_pairs={{0,4},{1,9},{2,6},{3,11},{4,0},{5,13},{6,2},{7,15},{8,12},{9,1},{1... | collective-permute-start | bytes 331784 | tf_op jit(solution)/shard_map/ppermute | solution.py:452
  20.8 5.6 %collective-permute-start.5 = (bf16[2,32,512]{2,1,0:T(8,128)(2,1)S(1)}, bf16[2,32,512]{2,1,0:T(8,128)(2,1)S(1)}, u32[]{:S(2)}, u32[]{:S(2)}) collective-permute-start(bf16[2,32,512]{2,1,0:T(8,128)(2,1)S(1)} %get-tuple-element.63.pg_ref), channel_id=1, source_target_pairs={{0,15},{1,0},{2,1},{3,2},{4,3},{5,4},{6,5},{7,6},{8,7},{9,8},{10,9... | collective-permute-start | bytes 196616 | tf_op jit(solution)/shard_map/ppermute | solution.py:443
  26.4 4.2 %collective-permute-start.6 = (f32[32,864]{1,0:T(8,128)S(1)}, f32[32,864]{1,0:T(8,128)S(1)}, u32[]{:S(2)}, u32[]{:S(2)}) collective-permute-start(f32[32,864]{1,0:T(8,128)S(1)} %add.15.mine_ref), channel_id=1, source_target_pairs={{0,1},{1,0},{2,3},{3,2},{4,5},{5,4},{6,7},{7,6},{8,9},{9,8},{10,11... | collective-permute-start | bytes 331784 | tf_op jit(solution)/shard_map/ppermute | solution.py:440

commit v9 on v6

--- a/solution.py
+++ b/solution.py
@@ -439,7 +439,7 @@
         [pltpu.VMEM((count - 2, channels, cells), F32),
          pltpu.SemaphoreType.DMA((count - 2,))], out_specs=(HB, VM))
     bits = [1 << power for power in range(1, size.bit_length() - 1)]
-    rounds = list(zip(bits[-1:] + bits[:-1], bits))
+    rounds = list(zip(bits, bits[1:2] + bits[:1] + bits[2:]))
     for index, choice in enumerate(rounds):
         total = total + lax.ppermute(total, AXIS, [(b, b ^ choice[b % 2]) for b in range(size)])
         if index == len(rounds) - 2:

time: 31.7 us -> 31.7 us (level)
  starting transfers between devices: 11.8 us -> 10.7 us
  waiting for transfers between devices: 8.31 us -> 9.41 us
    ppermute x1, starting transfers between devices: 3.57 us -> 2.64 us  [body(): lax.ppermute(pg_sent, AXIS, [(b, (b - 1) % size) for b in range(size)])]
    ppermute x3, waiting for transfers between devices: 7.22 us -> 8.07 us  [body(): lax.ppermute(total, AXIS, [(b, b ^ choice[b % 2]) for b in range(size)])]
where the time goes in v9:
time: 31.7 us; the launch traced here: 31.5 us
  starting transfers between devices  10.7 us (34%)
  Pallas kernels  10.6 us (33%)
  waiting for transfers between devices  9.41 us (30%)
  between operations  0.72 us (2%)
    pallas_call x7, Pallas kernels, call(): pl.pallas_call(kernel, out_shape=outs, in_specs=specs or [VM] * len(opera...  10.6 us
    ppermute x3, waiting for transfers between devices, body(): lax.ppermute(total, AXIS, [(b, b ^ choice[b % 2]) for b in range(size)])  8.07 us
    ppermute x2, starting transfers between devices, swap(): return lax.ppermute(value, AXIS, [(b, b ^ bit) for b in range(size)])  4.25 us
    ppermute x1, starting transfers between devices, body(): up = lax.ppermute(up, AXIS, [(b, (b + 1) % size) for b in range(size)])  2.65 us
    ppermute x1, starting transfers between devices, body(): lax.ppermute(pg_sent, AXIS, [(b, (b - 1) % size) for b in range(size)])  2.64 us
    ppermute x3, starting transfers between devices, body(): lax.ppermute(total, AXIS, [(b, b ^ choice[b % 2]) for b in range(size)])  1.18 us
    ppermute x1, waiting for transfers between devices, body(): lax.ppermute(pg_sent, AXIS, [(b, (b - 1) % size) for b in range(size)])  1.18 us
  transfers between devices with their start and end apart: 7, of which 5 were waited for; matrix products, arithmetic and copies ran while one was open for 0% of the time, Pallas kernels for 23%

profile of v9, /device:TPU:1, one launch (start us, length us, event | category | flops | bytes accessed | tf_op | source)
XLA Modules:
  0.0 31.5 jit_solution(6717347837411237770)
XLA Ops:
  0.6 1.1 %pack.1 = (bf16[4,32,512]{2,1,0:T(8,128)(2,1)S(1)}, s32[2,8,128]{2,1,0:T(8,128)S(1)}, bf16[8,32,512]{2,1,0:T(8,128)(2,1)S(1)}, bf16[8,32,512]{2,1,0:T(8,128)(2,1...) custom-call(s32[1,2]{1,0:T(1,128)} %codes_ref.1, bf16[8,32,512]{2,1,0:T(8,128)(2,1)} %bitcast.4, ...), custom_call_target="tpu_custom_call" | custom-call | tf_op jit(solution)/shard_map/pack/pallas_call | solution.py:392
  1.7 2.7 %collective-permute-start = (bf16[4,32,512]{2,1,0:T(8,128)(2,1)S(1)}, bf16[4,32,512]{2,1,0:T(8,128)(2,1)S(1)}, u32[]{:S(2)}, u32[]{:S(2)}) collective-permute-start(bf16[4,32,512]{2,1,0:T(8,128)(2,1)S(1)} %get-tuple-element.48), channel_id=1, source_target_pairs={{0,1},{1,2},{2,3},{3,4},{4,5},{5,6},{6,7},{7,8},{8,9},{9,10},{10,1... | collective-permute-start | bytes 393224 | tf_op jit(solution)/shard_map/ppermute | solution.py:414
  4.4 3.7 %interior.1 = (bf16[288,288]{1,0:T(8,128)(2,1)S(1)}, bf16[320,256]{1,0:T(8,128)(2,1)S(1)}, bf16[320,256]{1,0:T(8,128)(2,1)S(1)}, f32[2,32,512]{2,1,0:T(8,128)S(1...) custom-call(bf16[8,32,512]{2,1,0:T(8,128)(2,1)S(1)} %get-tuple-eleme, ...), custom_call_target="tpu_custom_call" | custom-call | tf_op jit(solution)/shard_map/interior/pallas_call | solution.py:392
  8.1 0.0 collective-permute-done.up_ref
  8.1 1.4 %edge.1 = (f32[32,864]{1,0:T(8,128)S(1)}, bf16[2,32,512]{2,1,0:T(8,128)(2,1)S(1)}, bf16[64,512]{1,0:T(8,128)(2,1)S(1)}, bf16[64,512]{1,0:T(8,128)(2,1)S(1)}, bf16[576,512]{1,0:T(8,128)(2,1)S(1)}) custom-call(bf16[4,32,512]{2,1,0:T(8,128)(2,1)S(1)} %collective-permute-done.up_ref, bf16[8,32,512]{2,1,0:T(8,128)(2,1)S(1)} %get-tuple-element.40.x_ref, ...), custom_call_target="tpu_custom_call" | custom-call | tf_op jit(solution)/shard_map/edge/pallas_call | solution.py:392
  9.5 1.9 %collective-permute-start.1 = (f32[32,864]{1,0:T(8,128)S(1)}, f32[32,864]{1,0:T(8,128)S(1)}, u32[]{:S(2)}, u32[]{:S(2)}) collective-permute-start(f32[32,864]{1,0:T(8,128)S(1)} %get-tuple-element.60), channel_id=1, source_target_pairs={{0,1},{1,0},{2,3},{3,2},{4,5},{5,4},{6,7},{7,6},{8,9},{9,8},{10,11... | collective-permute-start | bytes 331784 | tf_op jit(solution)/shard_map/ppermute | solution.py:432
  11.4 0.8 %keep.1 = (f32[32,864]{1,0:T(8,128)S(1)}, bf16[576,512]{1,0:T(8,128)(2,1)S(1)}) custom-call(bf16[8,32,512]{2,1,0:T(8,128)(2,1)S(1)} %get-tuple-element.40.x_ref, s32[2,8,128]{2,1,0:T(8,128)S(1)} %get-tuple-element.41.codes_ref, bf16[2304,512]{1,0:T(8,128)(2,1)S(1)} %get-tuple-element.45.cs_ref, f32[576,128]{1,0:T(8,128)S(1)} %get-tuple-element.46.g1_ref, ...), custom_call_target="tpu_custom_call" | custom-call | tf_op jit(solution)/shard_map/keep/pallas_call | solution.py:392
  12.2 0.2 collective-permute-done.1
  12.3 0.1 collective-permute-start.2
  12.4 3.9 %collective-permute-done.2 = f32[32,864]{1,0:T(8,128)S(1)} collective-permute-done((f32[32,864]{1,0:T(8,128)S(1)}, f32[32,864]{1,0:T(8,128)S(1)}, u32[]{:S(2)}, u32[]{:S(2)}) %collective-permute-start.2) | collective-permute-done | bytes 110624 | tf_op jit(solution)/shard_map/ppermute | solution.py:444
  16.4 0.1 collective-permute-start.3
  16.4 1.3 %input_grad.1 = (f32[8,32,512]{2,1,0:T(8,128)}, f32[2,32,512]{2,1,0:T(8,128)S(1)}) custom-call(bf16[1728,512]{1,0:T(8,128)(2,1)S(1)} %get-tuple-element.62.inner_ref, bf16[576,512]{1,0:T(8,128)(2,1)S(1)} %get-tuple-element.63.edge_ref, bf16[8,32,512]{2,1,0:T(8,128)(2,1)S(1)} %get-tuple-element.42.g_ref, bf16[288,288]{1,0:T(8,128)(2,1)S(1)} %get-tuple-element.49.ws_ref), custom_call_target="tpu_custom_call" | custom-call | tf_op jit(solution)/shard_map/input_grad/pallas_call | solution.py:392
  17.8 2.3 %collective-permute-done.3 = f32[32,864]{1,0:T(8,128)S(1)} collective-permute-done((f32[32,864]{1,0:T(8,128)S(1)}, f32[32,864]{1,0:T(8,128)S(1)}, u32[]{:S(2)}, u32[]{:S(2)}) %collective-permute-start.3) | collective-permute-done | bytes 110624 | tf_op jit(solution)/shard_map/ppermute | solution.py:444
  20.1 1.0 %collective-permute-start.4 = (f32[32,864]{1,0:T(8,128)S(1)}, f32[32,864]{1,0:T(8,128)S(1)}, u32[]{:S(2)}, u32[]{:S(2)}) collective-permute-start(f32[32,864]{1,0:T(8,128)S(1)} %add.14), channel_id=1, source_target_pairs={{0,8},{1,9},{2,10},{3,11},{4,12},{5,13},{6,14},{7,15},{8,0},{9,1},... | collective-permute-start | bytes 331784 | tf_op jit(solution)/shard_map/ppermute | solution.py:444
  21.1 2.6 %collective-permute-start.5 = (bf16[2,32,512]{2,1,0:T(8,128)(2,1)S(1)}, bf16[2,32,512]{2,1,0:T(8,128)(2,1)S(1)}, u32[]{:S(2)}, u32[]{:S(2)}) collective-permute-start(bf16[2,32,512]{2,1,0:T(8,128)(2,1)S(1)} %get-tuple-element.67.pg_ref), channel_id=1, source_target_pairs={{0,15},{1,0},{2,1},{3,2},{4,3},{5,4},{6,5},{7,6},{8,7},{9,8},{10,9... | collective-permute-start | bytes 196616 | tf_op jit(solution)/shard_map/ppermute | solution.py:435
  23.8 1.9 %collective-permute-done.4 = f32[32,864]{1,0:T(8,128)S(1)} collective-permute-done((f32[32,864]{1,0:T(8,128)S(1)}, f32[32,864]{1,0:T(8,128)S(1)}, u32[]{:S(2)}, u32[]{:S(2)}) %collective-permute-start.4) | collective-permute-done | bytes 110624 | tf_op jit(solution)/shard_map/ppermute | solution.py:444
  25.7 1.2 %collective-permute-done.5.down_ref = bf16[2,32,512]{2,1,0:T(8,128)(2,1)S(1)} collective-permute-done((bf16[2,32,512]{2,1,0:T(8,128)(2,1)S(1)}, bf16[2,32,512]{2,1,0:T(8,128)(2,1)S(1)}, u32[]{:S(2)}, u32[]{:S(2)}) %collective-permute-start.5) | collective-permute-done | bytes 65568 | tf_op jit(solution)/shard_map/ppermute | solution.py:435
  26.8 2.4 %collective-permute-start.6 = (f32[32,864]{1,0:T(8,128)S(1)}, f32[32,864]{1,0:T(8,128)S(1)}, u32[]{:S(2)}, u32[]{:S(2)}) collective-permute-start(f32[32,864]{1,0:T(8,128)S(1)} %add.15.mine_ref), channel_id=1, source_target_pairs={{0,1},{1,0},{2,3},{3,2},{4,5},{5,4},{6,7},{7,6},{8,9},{9,8},{10,11... | collective-permute-start | bytes 331784 | tf_op jit(solution)/shard_map/ppermute | solution.py:432
  29.2 1.4 %upper_planes.1 = (f32[8,32,512]{2,1,0:T(8,128)}, f32[32,864]{1,0:T(8,128)}, f32[32,864]{1,0:T(8,128)}) custom-call(bf16[2,32,512]{2,1,0:T(8,128)(2,1)S(1)} %collective-permute-done.5.down_ref, s32[2,8,128]{2,1,0:T(8,128)S(1)} %get-tuple-element.41.codes_ref, bf16[288,288]{1,0:T(8,128)(2,1)S(1)} %get-tuple-element.49.ws_ref, ...), custom_call_target="tpu_custom_call", output_to_operand_aliasing={{0}: (5, {})} | custom-call | tf_op jit(solution)/shard_map/upper_planes/pallas_call | solution.py:392
  30.6 0.0 collective-permute-done.6.other_ref
  30.6 0.9 %normalize.1 = (f32[32,864]{1,0:T(8,128)}, f32[32,864]{1,0:T(8,128)}) custom-call(f32[32,864]{1,0:T(8,128)S(1)} %collective-permute-done.6.other_ref, f32[32,864]{1,0:T(8,128)} %get-tuple-element.73._, f32[32,864]{1,0:T(8,128)} %get-tuple-element.74.__), custom_call_target="tpu_custom_call", output_to_operand_aliasing={{0}: (1, {}), {1}: (2, {})} | custom-call | tf_op jit(solution)/shard_map/normalize/pallas_call | solution.py:392
  (4 shorter events, 0.1 us)
Async XLA Ops:
  1.7 6.4 %collective-permute-start = (bf16[4,32,512]{2,1,0:T(8,128)(2,1)S(1)}, bf16[4,32,512]{2,1,0:T(8,128)(2,1)S(1)}, u32[]{:S(2)}, u32[]{:S(2)}) collective-permute-start(bf16[4,32,512]{2,1,0:T(8,128)(2,1)S(1)} %get-tuple-element.48), channel_id=1, source_target_pairs={{0,1},{1,2},{2,3},{3,4},{4,5},{5,6},{6,7},{7,8},{8,9},{9,10},{10,1... | collective-permute-start | bytes 393224 | tf_op jit(solution)/shard_map/ppermute | solution.py:414
  9.5 2.8 %collective-permute-start.1 = (f32[32,864]{1,0:T(8,128)S(1)}, f32[32,864]{1,0:T(8,128)S(1)}, u32[]{:S(2)}, u32[]{:S(2)}) collective-permute-start(f32[32,864]{1,0:T(8,128)S(1)} %get-tuple-element.60), channel_id=1, source_target_pairs={{0,1},{1,0},{2,3},{3,2},{4,5},{5,4},{6,7},{7,6},{8,9},{9,8},{10,11... | collective-permute-start | bytes 331784 | tf_op jit(solution)/shard_map/ppermute | solution.py:432
  12.3 4.0 %collective-permute-start.2 = (f32[32,864]{1,0:T(8,128)S(1)}, f32[32,864]{1,0:T(8,128)S(1)}, u32[]{:S(2)}, u32[]{:S(2)}) collective-permute-start(f32[32,864]{1,0:T(8,128)S(1)} %add.12), channel_id=1, source_target_pairs={{0,2},{1,5},{2,0},{3,7},{4,6},{5,1},{6,4},{7,3},{8,10},{9,13},{10,... | collective-permute-start | bytes 331784 | tf_op jit(solution)/shard_map/ppermute | solution.py:444
  16.4 3.7 %collective-permute-start.3 = (f32[32,864]{1,0:T(8,128)S(1)}, f32[32,864]{1,0:T(8,128)S(1)}, u32[]{:S(2)}, u32[]{:S(2)}) collective-permute-start(f32[32,864]{1,0:T(8,128)S(1)} %add.13), channel_id=1, source_target_pairs={{0,4},{1,3},{2,6},{3,1},{4,0},{5,7},{6,2},{7,5},{8,12},{9,11},{10,... | collective-permute-start | bytes 331784 | tf_op jit(solution)/shard_map/ppermute | solution.py:444
  20.1 5.6 %collective-permute-start.4 = (f32[32,864]{1,0:T(8,128)S(1)}, f32[32,864]{1,0:T(8,128)S(1)}, u32[]{:S(2)}, u32[]{:S(2)}) collective-permute-start(f32[32,864]{1,0:T(8,128)S(1)} %add.14), channel_id=1, source_target_pairs={{0,8},{1,9},{2,10},{3,11},{4,12},{5,13},{6,14},{7,15},{8,0},{9,1},... | collective-permute-start | bytes 331784 | tf_op jit(solution)/shard_map/ppermute | solution.py:444
  21.1 5.7 %collective-permute-start.5 = (bf16[2,32,512]{2,1,0:T(8,128)(2,1)S(1)}, bf16[2,32,512]{2,1,0:T(8,128)(2,1)S(1)}, u32[]{:S(2)}, u32[]{:S(2)}) collective-permute-start(bf16[2,32,512]{2,1,0:T(8,128)(2,1)S(1)} %get-tuple-element.67.pg_ref), channel_id=1, source_target_pairs={{0,15},{1,0},{2,1},{3,2},{4,3},{5,4},{6,5},{7,6},{8,7},{9,8},{10,9... | collective-permute-start | bytes 196616 | tf_op jit(solution)/shard_map/ppermute | solution.py:435
  26.8 3.8 %collective-permute-start.6 = (f32[32,864]{1,0:T(8,128)S(1)}, f32[32,864]{1,0:T(8,128)S(1)}, u32[]{:S(2)}, u32[]{:S(2)}) collective-permute-start(f32[32,864]{1,0:T(8,128)S(1)} %add.15.mine_ref), channel_id=1, source_target_pairs={{0,1},{1,0},{2,3},{3,2},{4,5},{5,4},{6,7},{7,6},{8,9},{9,8},{10,11... | collective-permute-start | bytes 331784 | tf_op jit(solution)/shard_map/ppermute | solution.py:432

commit v10 on v9

--- a/solution.py
+++ b/solution.py
@@ -439,7 +439,7 @@
         [pltpu.VMEM((count - 2, channels, cells), F32),
          pltpu.SemaphoreType.DMA((count - 2,))], out_specs=(HB, VM))
     bits = [1 << power for power in range(1, size.bit_length() - 1)]
-    rounds = list(zip(bits, bits[1:2] + bits[:1] + bits[2:]))
+    rounds = list(zip(bits[:1] + bits[-1:] + bits[1:-1], bits[-1:] + bits[:1] + bits[1:-1]))
     for index, choice in enumerate(rounds):
         total = total + lax.ppermute(total, AXIS, [(b, b ^ choice[b % 2]) for b in range(size)])
         if index == len(rounds) - 2:

time: 31.7 us -> 31.7 us (level)
  no operation moved by 1% of the time
where the time goes in v10:
time: 31.7 us; the launch traced here: 31.5 us
  starting transfers between devices  10.9 us (34%)
  Pallas kernels  10.6 us (33%)
  waiting for transfers between devices  9.21 us (29%)
  between operations  0.72 us (2%)
    pallas_call x7, Pallas kernels, call(): pl.pallas_call(kernel, out_shape=outs, in_specs=specs or [VM] * len(opera...  10.6 us
    ppermute x3, waiting for transfers between devices, body(): lax.ppermute(total, AXIS, [(b, b ^ choice[b % 2]) for b in range(size)])  8.13 us
    ppermute x2, starting transfers between devices, swap(): return lax.ppermute(value, AXIS, [(b, b ^ bit) for b in range(size)])  4.55 us
    ppermute x1, starting transfers between devices, body(): up = lax.ppermute(up, AXIS, [(b, (b + 1) % size) for b in range(size)])  2.65 us
    ppermute x1, starting transfers between devices, body(): lax.ppermute(pg_sent, AXIS, [(b, (b - 1) % size) for b in range(size)])  2.42 us
    ppermute x3, starting transfers between devices, body(): lax.ppermute(total, AXIS, [(b, b ^ choice[b % 2]) for b in range(size)])  1.31 us
    ppermute x1, waiting for transfers between devices, body(): lax.ppermute(pg_sent, AXIS, [(b, (b - 1) % size) for b in range(size)])  0.92 us
  transfers between devices with their start and end apart: 7, of which 5 were waited for; matrix products, arithmetic and copies ran while one was open for 0% of the time, Pallas kernels for 23%

profile of v10, /device:TPU:1, one launch (start us, length us, event | category | flops | bytes accessed | tf_op | source)
XLA Modules:
  0.0 31.5 jit_solution(16965157461384689875)
XLA Ops:
  0.6 1.1 %pack.1 = (bf16[4,32,512]{2,1,0:T(8,128)(2,1)S(1)}, s32[2,8,128]{2,1,0:T(8,128)S(1)}, bf16[8,32,512]{2,1,0:T(8,128)(2,1)S(1)}, bf16[8,32,512]{2,1,0:T(8,128)(2,1...) custom-call(s32[1,2]{1,0:T(1,128)} %codes_ref.1, bf16[8,32,512]{2,1,0:T(8,128)(2,1)} %bitcast.4, ...), custom_call_target="tpu_custom_call" | custom-call | tf_op jit(solution)/shard_map/pack/pallas_call | solution.py:392
  1.7 2.7 %collective-permute-start = (bf16[4,32,512]{2,1,0:T(8,128)(2,1)S(1)}, bf16[4,32,512]{2,1,0:T(8,128)(2,1)S(1)}, u32[]{:S(2)}, u32[]{:S(2)}) collective-permute-start(bf16[4,32,512]{2,1,0:T(8,128)(2,1)S(1)} %get-tuple-element.48), channel_id=1, source_target_pairs={{0,1},{1,2},{2,3},{3,4},{4,5},{5,6},{6,7},{7,8},{8,9},{9,10},{10,1... | collective-permute-start | bytes 393224 | tf_op jit(solution)/shard_map/ppermute | solution.py:414
  4.4 3.7 %interior.1 = (bf16[288,288]{1,0:T(8,128)(2,1)S(1)}, bf16[320,256]{1,0:T(8,128)(2,1)S(1)}, bf16[320,256]{1,0:T(8,128)(2,1)S(1)}, f32[2,32,512]{2,1,0:T(8,128)S(1...) custom-call(bf16[8,32,512]{2,1,0:T(8,128)(2,1)S(1)} %get-tuple-eleme, ...), custom_call_target="tpu_custom_call" | custom-call | tf_op jit(solution)/shard_map/interior/pallas_call | solution.py:392
  8.1 0.0 collective-permute-done.up_ref
  8.1 1.4 %edge.1 = (f32[32,864]{1,0:T(8,128)S(1)}, bf16[2,32,512]{2,1,0:T(8,128)(2,1)S(1)}, bf16[64,512]{1,0:T(8,128)(2,1)S(1)}, bf16[64,512]{1,0:T(8,128)(2,1)S(1)}, bf16[576,512]{1,0:T(8,128)(2,1)S(1)}) custom-call(bf16[4,32,512]{2,1,0:T(8,128)(2,1)S(1)} %collective-permute-done.up_ref, bf16[8,32,512]{2,1,0:T(8,128)(2,1)S(1)} %get-tuple-element.40.x_ref, ...), custom_call_target="tpu_custom_call" | custom-call | tf_op jit(solution)/shard_map/edge/pallas_call | solution.py:392
  9.5 1.9 %collective-permute-start.1 = (f32[32,864]{1,0:T(8,128)S(1)}, f32[32,864]{1,0:T(8,128)S(1)}, u32[]{:S(2)}, u32[]{:S(2)}) collective-permute-start(f32[32,864]{1,0:T(8,128)S(1)} %get-tuple-element.60), channel_id=1, source_target_pairs={{0,1},{1,0},{2,3},{3,2},{4,5},{5,4},{6,7},{7,6},{8,9},{9,8},{10,11... | collective-permute-start | bytes 331784 | tf_op jit(solution)/shard_map/ppermute | solution.py:432
  11.4 0.8 %keep.1 = (f32[32,864]{1,0:T(8,128)S(1)}, bf16[576,512]{1,0:T(8,128)(2,1)S(1)}) custom-call(bf16[8,32,512]{2,1,0:T(8,128)(2,1)S(1)} %get-tuple-element.40.x_ref, s32[2,8,128]{2,1,0:T(8,128)S(1)} %get-tuple-element.41.codes_ref, bf16[2304,512]{1,0:T(8,128)(2,1)S(1)} %get-tuple-element.45.cs_ref, f32[576,128]{1,0:T(8,128)S(1)} %get-tuple-element.46.g1_ref, ...), custom_call_target="tpu_custom_call" | custom-call | tf_op jit(solution)/shard_map/keep/pallas_call | solution.py:392
  12.2 0.2 collective-permute-done.1
  12.3 1.0 %collective-permute-start.2 = (f32[32,864]{1,0:T(8,128)S(1)}, f32[32,864]{1,0:T(8,128)S(1)}, u32[]{:S(2)}, u32[]{:S(2)}) collective-permute-start(f32[32,864]{1,0:T(8,128)S(1)} %add.12), channel_id=1, source_target_pairs={{0,2},{1,9},{2,0},{3,11},{4,6},{5,13},{6,4},{7,15},{8,10},{9,1},{1... | collective-permute-start | bytes 331784 | tf_op jit(solution)/shard_map/ppermute | solution.py:444
  13.4 4.5 %collective-permute-done.2 = f32[32,864]{1,0:T(8,128)S(1)} collective-permute-done((f32[32,864]{1,0:T(8,128)S(1)}, f32[32,864]{1,0:T(8,128)S(1)}, u32[]{:S(2)}, u32[]{:S(2)}) %collective-permute-start.2) | collective-permute-done | bytes 110624 | tf_op jit(solution)/shard_map/ppermute | solution.py:444
  17.9 0.2 collective-permute-start.3
  18.1 1.4 %input_grad.1 = (f32[8,32,512]{2,1,0:T(8,128)}, f32[2,32,512]{2,1,0:T(8,128)S(1)}) custom-call(bf16[1728,512]{1,0:T(8,128)(2,1)S(1)} %get-tuple-element.62.inner_ref, bf16[576,512]{1,0:T(8,128)(2,1)S(1)} %get-tuple-element.63.edge_ref, bf16[8,32,512]{2,1,0:T(8,128)(2,1)S(1)} %get-tuple-element.42.g_ref, bf16[288,288]{1,0:T(8,128)(2,1)S(1)} %get-tuple-element.49.ws_ref), custom_call_target="tpu_custom_call" | custom-call | tf_op jit(solution)/shard_map/input_grad/pallas_call | solution.py:392
  19.4 2.4 %collective-permute-done.3 = f32[32,864]{1,0:T(8,128)S(1)} collective-permute-done((f32[32,864]{1,0:T(8,128)S(1)}, f32[32,864]{1,0:T(8,128)S(1)}, u32[]{:S(2)}, u32[]{:S(2)}) %collective-permute-start.3) | collective-permute-done | bytes 110624 | tf_op jit(solution)/shard_map/ppermute | solution.py:444
  21.9 0.1 collective-permute-start.4
  22.0 2.4 %collective-permute-start.5 = (bf16[2,32,512]{2,1,0:T(8,128)(2,1)S(1)}, bf16[2,32,512]{2,1,0:T(8,128)(2,1)S(1)}, u32[]{:S(2)}, u32[]{:S(2)}) collective-permute-start(bf16[2,32,512]{2,1,0:T(8,128)(2,1)S(1)} %get-tuple-element.67.pg_ref), channel_id=1, source_target_pairs={{0,15},{1,0},{2,1},{3,2},{4,3},{5,4},{6,5},{7,6},{8,7},{9,8},{10,9... | collective-permute-start | bytes 196616 | tf_op jit(solution)/shard_map/ppermute | solution.py:435
  24.4 1.2 %collective-permute-done.4 = f32[32,864]{1,0:T(8,128)S(1)} collective-permute-done((f32[32,864]{1,0:T(8,128)S(1)}, f32[32,864]{1,0:T(8,128)S(1)}, u32[]{:S(2)}, u32[]{:S(2)}) %collective-permute-start.4) | collective-permute-done | bytes 110624 | tf_op jit(solution)/shard_map/ppermute | solution.py:444
  25.6 0.9 %collective-permute-done.5.down_ref = bf16[2,32,512]{2,1,0:T(8,128)(2,1)S(1)} collective-permute-done((bf16[2,32,512]{2,1,0:T(8,128)(2,1)S(1)}, bf16[2,32,512]{2,1,0:T(8,128)(2,1)S(1)}, u32[]{:S(2)}, u32[]{:S(2)}) %collective-permute-start.5) | collective-permute-done | bytes 65568 | tf_op jit(solution)/shard_map/ppermute | solution.py:435
  26.5 2.7 %collective-permute-start.6 = (f32[32,864]{1,0:T(8,128)S(1)}, f32[32,864]{1,0:T(8,128)S(1)}, u32[]{:S(2)}, u32[]{:S(2)}) collective-permute-start(f32[32,864]{1,0:T(8,128)S(1)} %add.15.mine_ref), channel_id=1, source_target_pairs={{0,1},{1,0},{2,3},{3,2},{4,5},{5,4},{6,7},{7,6},{8,9},{9,8},{10,11... | collective-permute-start | bytes 331784 | tf_op jit(solution)/shard_map/ppermute | solution.py:432
  29.2 1.4 %upper_planes.1 = (f32[8,32,512]{2,1,0:T(8,128)}, f32[32,864]{1,0:T(8,128)}, f32[32,864]{1,0:T(8,128)}) custom-call(bf16[2,32,512]{2,1,0:T(8,128)(2,1)S(1)} %collective-permute-done.5.down_ref, s32[2,8,128]{2,1,0:T(8,128)S(1)} %get-tuple-element.41.codes_ref, bf16[288,288]{1,0:T(8,128)(2,1)S(1)} %get-tuple-element.49.ws_ref, ...), custom_call_target="tpu_custom_call", output_to_operand_aliasing={{0}: (5, {})} | custom-call | tf_op jit(solution)/shard_map/upper_planes/pallas_call | solution.py:392
  30.6 0.0 collective-permute-done.6.other_ref
  30.6 0.9 %normalize.1 = (f32[32,864]{1,0:T(8,128)}, f32[32,864]{1,0:T(8,128)}) custom-call(f32[32,864]{1,0:T(8,128)S(1)} %collective-permute-done.6.other_ref, f32[32,864]{1,0:T(8,128)} %get-tuple-element.73._, f32[32,864]{1,0:T(8,128)} %get-tuple-element.74.__), custom_call_target="tpu_custom_call", output_to_operand_aliasing={{0}: (1, {}), {1}: (2, {})} | custom-call | tf_op jit(solution)/shard_map/normalize/pallas_call | solution.py:392
  (4 shorter events, 0.1 us)
Async XLA Ops:
  1.7 6.4 %collective-permute-start = (bf16[4,32,512]{2,1,0:T(8,128)(2,1)S(1)}, bf16[4,32,512]{2,1,0:T(8,128)(2,1)S(1)}, u32[]{:S(2)}, u32[]{:S(2)}) collective-permute-start(bf16[4,32,512]{2,1,0:T(8,128)(2,1)S(1)} %get-tuple-element.48), channel_id=1, source_target_pairs={{0,1},{1,2},{2,3},{3,4},{4,5},{5,6},{6,7},{7,8},{8,9},{9,10},{10,1... | collective-permute-start | bytes 393224 | tf_op jit(solution)/shard_map/ppermute | solution.py:414
  9.5 2.8 %collective-permute-start.1 = (f32[32,864]{1,0:T(8,128)S(1)}, f32[32,864]{1,0:T(8,128)S(1)}, u32[]{:S(2)}, u32[]{:S(2)}) collective-permute-start(f32[32,864]{1,0:T(8,128)S(1)} %get-tuple-element.60), channel_id=1, source_target_pairs={{0,1},{1,0},{2,3},{3,2},{4,5},{5,4},{6,7},{7,6},{8,9},{9,8},{10,11... | collective-permute-start | bytes 331784 | tf_op jit(solution)/shard_map/ppermute | solution.py:432
  12.3 5.5 %collective-permute-start.2 = (f32[32,864]{1,0:T(8,128)S(1)}, f32[32,864]{1,0:T(8,128)S(1)}, u32[]{:S(2)}, u32[]{:S(2)}) collective-permute-start(f32[32,864]{1,0:T(8,128)S(1)} %add.12), channel_id=1, source_target_pairs={{0,2},{1,9},{2,0},{3,11},{4,6},{5,13},{6,4},{7,15},{8,10},{9,1},{1... | collective-permute-start | bytes 331784 | tf_op jit(solution)/shard_map/ppermute | solution.py:444
  17.9 4.0 %collective-permute-start.3 = (f32[32,864]{1,0:T(8,128)S(1)}, f32[32,864]{1,0:T(8,128)S(1)}, u32[]{:S(2)}, u32[]{:S(2)}) collective-permute-start(f32[32,864]{1,0:T(8,128)S(1)} %add.13), channel_id=1, source_target_pairs={{0,8},{1,3},{2,10},{3,1},{4,12},{5,7},{6,14},{7,5},{8,0},{9,11},{1... | collective-permute-start | bytes 331784 | tf_op jit(solution)/shard_map/ppermute | solution.py:444
  21.9 3.7 %collective-permute-start.4 = (f32[32,864]{1,0:T(8,128)S(1)}, f32[32,864]{1,0:T(8,128)S(1)}, u32[]{:S(2)}, u32[]{:S(2)}) collective-permute-start(f32[32,864]{1,0:T(8,128)S(1)} %add.14), channel_id=1, source_target_pairs={{0,4},{1,5},{2,6},{3,7},{4,0},{5,1},{6,2},{7,3},{8,12},{9,13},{10,... | collective-permute-start | bytes 331784 | tf_op jit(solution)/shard_map/ppermute | solution.py:444
  22.0 4.6 %collective-permute-start.5 = (bf16[2,32,512]{2,1,0:T(8,128)(2,1)S(1)}, bf16[2,32,512]{2,1,0:T(8,128)(2,1)S(1)}, u32[]{:S(2)}, u32[]{:S(2)}) collective-permute-start(bf16[2,32,512]{2,1,0:T(8,128)(2,1)S(1)} %get-tuple-element.67.pg_ref), channel_id=1, source_target_pairs={{0,15},{1,0},{2,1},{3,2},{4,3},{5,4},{6,5},{7,6},{8,7},{9,8},{10,9... | collective-permute-start | bytes 196616 | tf_op jit(solution)/shard_map/ppermute | solution.py:435
  26.5 4.1 %collective-permute-start.6 = (f32[32,864]{1,0:T(8,128)S(1)}, f32[32,864]{1,0:T(8,128)S(1)}, u32[]{:S(2)}, u32[]{:S(2)}) collective-permute-start(f32[32,864]{1,0:T(8,128)S(1)} %add.15.mine_ref), channel_id=1, source_target_pairs={{0,1},{1,0},{2,3},{3,2},{4,5},{5,4},{6,7},{7,6},{8,9},{9,8},{10,11... | collective-permute-start | bytes 331784 | tf_op jit(solution)/shard_map/ppermute | solution.py:432
